TPU v7x, 32 devices: a whole 2x2x4 slice. The times are simulated.
32 devices in a mesh: seq: 8 (over z, x), head: 4 (over y, core).
Axes of the slice: x: 2, y: 2, z: 4, core: 2. Of those that a mesh axis runs over, the one named last changes fastest.
Arguments:
- block_input: bfloat16 [4096, 2048], P(('seq', 'head')), may hold values from -6 to 6
- norm1_gain: float32 [2048], replicated, may hold values from 0.5 to 1.5
- query_weight: bfloat16 [2048, 2048], P(None, 'head'), may hold values from -0.125 to 0.125
- key_weight: bfloat16 [2048, 2048], P(None, 'head'), may hold values from -0.125 to 0.125
- value_weight: bfloat16 [2048, 2048], P(None, 'head'), may hold values from -0.125 to 0.125
- gate_weight: bfloat16 [2048, 2048], P(None, 'head'), may hold values from -0.125 to 0.125
- rate_weight: bfloat16 [2048, 32], P(None, 'head'), may hold values from -0.125 to 0.125
- rate_bias: float32 [32], P('head'), may hold values from -3 to 3
- rate_scale: float32 [32], P('head'), may hold values from 7.324219e-05 to 0.008
- init_state: float32 [32, 64, 64], P('head'), may hold values from -0.75 to 0.75
- init_bias: float32 [32, 64], P('head'), may hold values from -5 to 5
- post_gain: float32 [2048], P('head'), may hold values from 0.5 to 1.5
- post_bias: float32 [2048], P('head'), may hold values from -3 to 3
- out_weight: bfloat16 [2048, 2048], P('head'), may hold values from -0.25 to 0.25
- norm2_gain: float32 [2048], replicated, may hold values from 0.5 to 1.5
- mlp_gate: bfloat16 [2048, 5504], P(None, 'head'), may hold values from -0.125 to 0.125
- mlp_up: bfloat16 [2048, 5504], P(None, 'head'), may hold values from -0.125 to 0.125
- mlp_down: bfloat16 [5504, 2048], P('head'), may hold values from -0.15625 to 0.15625
- out_cotangent: bfloat16 [4096, 2048], P(('seq', 'head')), may hold values from -6 to 6
Outputs:
- block_out: bfloat16 [4096, 2048], P(('seq', 'head'))
- input_grad: float32 [4096, 2048], P(('seq', 'head'))
- norm1_gain_grad: float32 [2048], replicated
- query_weight_grad: float32 [2048, 2048], P(None, 'head')
- key_weight_grad: float32 [2048, 2048], P(None, 'head')
- value_weight_grad: float32 [2048, 2048], P(None, 'head')
- gate_weight_grad: float32 [2048, 2048], P(None, 'head')
- rate_weight_grad: float32 [2048, 32], P(None, 'head')
- rate_bias_grad: float32 [32], P('head')
- rate_scale_grad: float32 [32], P('head')
- init_state_grad: float32 [32, 64, 64], P('head')
- init_bias_grad: float32 [32, 64], P('head')
- post_gain_grad: float32 [2048], P('head')
- post_bias_grad: float32 [2048], P('head')
- out_weight_grad: float32 [2048, 2048], P('head')
- norm2_gain_grad: float32 [2048], replicated
- mlp_gate_grad: float32 [2048, 5504], P(None, 'head')
- mlp_up_grad: float32 [2048, 5504], P(None, 'head')
- mlp_down_grad: float32 [5504, 2048], P('head')
All inputs are finite; a program needn't handle non-finite values.
Results may differ from a plain program's by a relative error of at most 0.025.
Values may be sent and summed in bfloat16 or wider, within the bound.
No kernel may reach another device: no remote copies, remote signals or barrier semaphores. Data moves between devices by JAX's collectives and lax.ppermute only.
A program may use at most 256 MiB of HBM per device.

v0:
```python
import jax
import jax.numpy as jnp
from jax import lax
from jax.sharding import PartitionSpec as P

MB = 16


HIGHEST = lax.Precision.HIGHEST
EPSILON = 1e-06


def passed_along(shard, axis, by):
    size = lax.axis_size(axis)
    pairs = [(i, i + by) for i in range(size) if 0 <= i + by < size]
    return lax.ppermute(shard, axis, pairs)


def augment(values):
    ones_col = jnp.ones(values.shape[:-1] + (1,), jnp.float32)
    return jnp.concatenate([values, ones_col], axis=-1)


def compose(earlier, later):
    matrix = jnp.einsum("...ij,...jk->...ik", later[0], earlier[0], precision=HIGHEST)
    offset = jnp.einsum("...ij,...jk->...ik", later[0], earlier[1], precision=HIGHEST) + later[1]
    return (matrix, offset)


def apply_map(matrix, offset, inner_state):
    return jnp.einsum("...ij,...jk->...ik", matrix, inner_state, precision=HIGHEST) + offset


def step_matrix_of(key_block, rate_block):
    key_aug = augment(key_block)
    weighted_keys = key_aug * rate_block[..., None]
    identity = jnp.eye(key_aug.shape[-1], dtype=jnp.float32)
    return (
        identity - jnp.einsum("hni,hnj->hij", weighted_keys, key_aug, precision=HIGHEST),
        weighted_keys,
    )


def segment_map(identity, zero_state, key_blocks, value_blocks, rate_blocks):

    def turn(carry, inputs):
        key_block, value_block, rate_block = inputs
        step_matrix, weighted_keys = step_matrix_of(key_block, rate_block)
        step_offset = jnp.einsum(
            "hni,hno->hio", weighted_keys, value_block - key_block, precision=HIGHEST
        )
        return (compose(carry, (step_matrix, step_offset)), None)

    result, unused = lax.scan(turn, (identity, zero_state), (key_blocks, value_blocks, rate_blocks))
    return result


def causal_weights(query_block, key_block, rate_block):
    query_aug = augment(query_block)
    key_aug = augment(key_block)
    scores = jnp.einsum("hmi,hni->hmn", query_aug, key_aug, precision=HIGHEST)
    causal_mask = jnp.tril(jnp.ones((scores.shape[1], scores.shape[2]), jnp.float32))
    return (query_aug, key_aug, scores * causal_mask * rate_block[:, None, :])


def inner_block(inner_state, inputs):
    query_block, key_block, value_block, rate_block = inputs
    query_aug, key_aug, weighted = causal_weights(query_block, key_block, rate_block)
    errors = jnp.einsum("hmi,hio->hmo", key_aug, inner_state, precision=HIGHEST) - (
        value_block - key_block
    )
    outputs = (
        query_block
        + jnp.einsum("hmi,hio->hmo", query_aug, inner_state, precision=HIGHEST)
        - jnp.einsum("hmn,hno->hmo", weighted, errors, precision=HIGHEST)
    )
    new_state = inner_state - jnp.einsum(
        "hni,hno->hio", key_aug * rate_block[:, :, None], errors, precision=HIGHEST
    )
    return (new_state, outputs)


def segment_run(state_in, query_blocks, key_blocks, value_blocks, rate_blocks):
    last_state, outputs = lax.scan(
        jax.checkpoint(inner_block), state_in, (query_blocks, key_blocks, value_blocks, rate_blocks)
    )
    return (outputs, last_state)


def local_state_grad(zero_state, query_blocks, key_blocks, rate_blocks, d_z_blocks):

    def turn(pending, inputs):
        query_block, key_block, rate_block, d_z_block = inputs
        query_aug, key_aug, weighted = causal_weights(query_block, key_block, rate_block)
        back_errors = jnp.einsum("hmn,hmo->hno", weighted, d_z_block, precision=HIGHEST)
        direct = jnp.einsum("hmi,hmo->hio", query_aug, d_z_block, precision=HIGHEST) - jnp.einsum(
            "hni,hno->hio", key_aug, back_errors, precision=HIGHEST
        )
        step_matrix, unused = step_matrix_of(key_block, rate_block)
        return (jnp.einsum("hji,hjo->hio", step_matrix, pending, precision=HIGHEST) + direct, None)

    result, unused = lax.scan(
        turn, zero_state, (query_blocks, key_blocks, rate_blocks, d_z_blocks), reverse=True
    )
    return result


def to_heads(values, local_heads, head_width):
    return values.reshape(-1, MB, local_heads, head_width).transpose(0, 2, 1, 3)


def from_heads(values):
    block_count, head_count, block_size, head_width = values.shape
    return values.transpose(0, 2, 1, 3).reshape(block_count * block_size, head_count * head_width)


def gelu_tanh(values):
    return jax.nn.gelu(values, approximate=True)


def relay_state(values, offset):
    return passed_along(values, "seq", offset)


def body(
    block_input,
    norm1_gain,
    query_weight,
    key_weight,
    value_weight,
    gate_weight,
    rate_weight,
    rate_bias,
    rate_scale,
    init_state,
    init_bias,
    post_gain,
    post_bias,
    out_weight,
    norm2_gain,
    mlp_gate,
    mlp_up,
    mlp_down,
    out_cotangent,
):
    local_heads = init_state.shape[0]
    head_width = init_state.shape[1]
    model_width = block_input.shape[1]
    seq_index = lax.axis_index("seq")
    seq_count = lax.axis_size("seq")
    input_f32 = block_input.astype(jnp.float32)
    scale_in = lax.rsqrt(jnp.mean(input_f32 * input_f32, axis=-1, keepdims=True) + EPSILON)
    unit_in = input_f32 * scale_in
    normed = (unit_in * norm1_gain).astype(jnp.bfloat16)
    group_in, group_cot = (
        lax.all_gather(normed, "head", axis=0, tiled=True),
        lax.all_gather(out_cotangent, "head", axis=0, tiled=True),
    )
    query_rows = jnp.dot(group_in, query_weight, preferred_element_type=jnp.float32)
    key_rows = jnp.dot(group_in, key_weight, preferred_element_type=jnp.float32)
    value_rows = jnp.dot(group_in, value_weight, preferred_element_type=jnp.float32)
    gate_pre = jnp.dot(group_in, gate_weight, preferred_element_type=jnp.float32)
    rate_pre = jnp.dot(group_in, rate_weight, preferred_element_type=jnp.float32) + rate_bias
    rate_sig = jax.nn.sigmoid(rate_pre)
    rate_rows = rate_sig * rate_scale
    query_blocks = to_heads(query_rows, local_heads, head_width)
    key_blocks = to_heads(key_rows, local_heads, head_width)
    value_blocks = to_heads(value_rows, local_heads, head_width)
    rate_blocks = rate_rows.reshape(-1, MB, local_heads).transpose(0, 2, 1)
    aug_width = head_width + 1
    identity = jnp.broadcast_to(
        jnp.eye(aug_width, dtype=jnp.float32), (local_heads, aug_width, aug_width)
    )
    start_state = jnp.concatenate([init_state, init_bias[:, None, :]], axis=1)
    zero_state = jnp.zeros_like(start_state)
    segment_matrix, segment_offset = segment_map(
        identity, zero_state, key_blocks, value_blocks, rate_blocks
    )

    def forward_turn(turn, incoming):
        received = relay_state(apply_map(segment_matrix, segment_offset, incoming), 1)
        return jnp.where(seq_index == 0, start_state, received)

    state_in = lax.fori_loop(0, seq_count - 1, forward_turn, start_state)
    (z_blocks, last_state), inner_pullback = jax.vjp(
        segment_run, state_in, query_blocks, key_blocks, value_blocks, rate_blocks
    )
    z_rows = from_heads(z_blocks)
    stat_sums = lax.psum((jnp.sum(z_rows, axis=-1), jnp.sum(z_rows * z_rows, axis=-1)), "head")
    row_mean = stat_sums[0] / model_width
    row_var = stat_sums[1] / model_width - row_mean * row_mean
    inv_scale = lax.rsqrt(row_var + EPSILON)[:, None]
    z_hat = (z_rows - row_mean[:, None]) * inv_scale
    post_out = z_hat * post_gain + post_bias
    gate_act, gelu_back = jax.vjp(gelu_tanh, gate_pre)
    gated_out = (gate_act * post_out).astype(jnp.bfloat16)
    picked = gated_out
    attn_out = lax.psum_scatter(
        jnp.dot(picked, out_weight, preferred_element_type=jnp.float32).astype(jnp.bfloat16),
        "head",
        scatter_dimension=0,
        tiled=True,
    ).astype(jnp.float32)
    middle = input_f32 + attn_out
    scale_mid = lax.rsqrt(jnp.mean(middle * middle, axis=-1, keepdims=True) + EPSILON)
    unit_mid = middle * scale_mid
    mlp_input = (unit_mid * norm2_gain).astype(jnp.bfloat16)
    mlp_group = lax.all_gather(mlp_input, "head", axis=0, tiled=True)
    gate_mlp = jnp.dot(mlp_group, mlp_gate, preferred_element_type=jnp.float32)
    up_mlp = jnp.dot(mlp_group, mlp_up, preferred_element_type=jnp.float32)
    silu_gate, silu_back = jax.vjp(jax.nn.silu, gate_mlp)
    hidden = (silu_gate * up_mlp).astype(jnp.bfloat16)
    picked = hidden
    mlp_out = lax.psum_scatter(
        jnp.dot(picked, mlp_down, preferred_element_type=jnp.float32).astype(jnp.bfloat16),
        "head",
        scatter_dimension=0,
        tiled=True,
    ).astype(jnp.float32)
    block_out = (middle + mlp_out).astype(jnp.bfloat16)
    cot_f32 = out_cotangent.astype(jnp.float32)
    d_hidden = jnp.dot(group_cot, mlp_down.T, preferred_element_type=jnp.float32)
    mlp_down_grad = jnp.dot(hidden.T, group_cot, preferred_element_type=jnp.float32)
    d_gate_mlp = silu_back(d_hidden * up_mlp)[0].astype(jnp.bfloat16)
    d_up_mlp = (d_hidden * silu_gate).astype(jnp.bfloat16)
    mlp_gate_grad = jnp.dot(mlp_group.T, d_gate_mlp, preferred_element_type=jnp.float32)
    mlp_up_grad = jnp.dot(mlp_group.T, d_up_mlp, preferred_element_type=jnp.float32)
    d_mlp_input = lax.psum_scatter(
        jnp.dot(d_gate_mlp, mlp_gate.T, preferred_element_type=jnp.float32)
        + jnp.dot(d_up_mlp, mlp_up.T, preferred_element_type=jnp.float32),
        "head",
        scatter_dimension=0,
        tiled=True,
    )
    scaled_mid = d_mlp_input * norm2_gain
    norm2_part = jnp.sum(d_mlp_input * unit_mid, axis=0)
    d_middle = cot_f32 + scale_mid * (
        scaled_mid - unit_mid * jnp.mean(scaled_mid * unit_mid, axis=-1, keepdims=True)
    )
    d_attn = d_middle.astype(jnp.bfloat16)
    d_attn_group = lax.all_gather(d_attn, "head", axis=0, tiled=True)
    d_gated = jnp.dot(d_attn_group, out_weight.T, preferred_element_type=jnp.float32)
    out_weight_grad = jnp.dot(gated_out.T, d_attn_group, preferred_element_type=jnp.float32)
    d_post = d_gated * gate_act
    d_gate_pre = gelu_back(d_gated * post_out)[0].astype(jnp.bfloat16)
    post_gain_part = jnp.sum(d_post * z_hat, axis=0)
    post_bias_part = jnp.sum(d_post, axis=0)
    d_zhat = d_post * post_gain
    back_sums = lax.psum((jnp.sum(d_zhat, axis=-1), jnp.sum(d_zhat * z_hat, axis=-1)), "head")
    d_z = inv_scale * (
        d_zhat - back_sums[0][:, None] / model_width - z_hat * (back_sums[1][:, None] / model_width)
    )
    d_z_blocks = to_heads(d_z, local_heads, head_width)
    local_state = local_state_grad(zero_state, query_blocks, key_blocks, rate_blocks, d_z_blocks)
    back_matrix = jnp.swapaxes(segment_matrix, 1, 2)

    def backward_turn(turn, pending):
        return relay_state(apply_map(back_matrix, local_state, pending), -1)

    grad_out = lax.fori_loop(0, seq_count - 1, backward_turn, zero_state)
    all_terms = inner_pullback((d_z_blocks, grad_out))
    init_part = jnp.where(seq_index == 0, all_terms[0], 0.0)
    d_query = from_heads(all_terms[1]).astype(jnp.bfloat16)
    d_key = from_heads(all_terms[2]).astype(jnp.bfloat16)
    d_value = from_heads(all_terms[3]).astype(jnp.bfloat16)
    d_rate = all_terms[4].transpose(0, 2, 1).reshape(-1, local_heads)
    d_rate_pre = (d_rate * rate_scale * rate_sig * (1.0 - rate_sig)).astype(jnp.bfloat16)
    scale_part = jnp.sum(d_rate * rate_sig, axis=0)
    rate_bias_part = jnp.sum(d_rate_pre.astype(jnp.float32), axis=0)
    query_grad = jnp.dot(group_in.T, d_query, preferred_element_type=jnp.float32)
    key_grad = jnp.dot(group_in.T, d_key, preferred_element_type=jnp.float32)
    value_grad = jnp.dot(group_in.T, d_value, preferred_element_type=jnp.float32)
    gate_grad = jnp.dot(group_in.T, d_gate_pre, preferred_element_type=jnp.float32)
    rate_weight_part = jnp.dot(group_in.T, d_rate_pre, preferred_element_type=jnp.float32)

    def picked(values):
        return values

    total = jnp.dot(picked(d_query), query_weight.T, preferred_element_type=jnp.float32)
    total = total + jnp.dot(picked(d_key), key_weight.T, preferred_element_type=jnp.float32)
    total = total + jnp.dot(picked(d_value), value_weight.T, preferred_element_type=jnp.float32)
    total = total + jnp.dot(picked(d_gate_pre), gate_weight.T, preferred_element_type=jnp.float32)
    d_normed = lax.psum_scatter(
        (
            total + jnp.dot(picked(d_rate_pre), rate_weight.T, preferred_element_type=jnp.float32)
        ).astype(jnp.bfloat16),
        "head",
        scatter_dimension=0,
        tiled=True,
    ).astype(jnp.float32)
    scaled_in = d_normed * norm1_gain
    norm1_part = jnp.sum(d_normed * unit_in, axis=0)
    input_grad = d_middle + scale_in * (
        scaled_in - unit_in * jnp.mean(scaled_in * unit_in, axis=-1, keepdims=True)
    )
    summed = (
        lax.psum(query_grad.astype(jnp.bfloat16), "seq").astype(jnp.float32),
        lax.psum(key_grad.astype(jnp.bfloat16), "seq").astype(jnp.float32),
        lax.psum(value_grad.astype(jnp.bfloat16), "seq").astype(jnp.float32),
        lax.psum(gate_grad.astype(jnp.bfloat16), "seq").astype(jnp.float32),
        lax.psum(rate_weight_part.astype(jnp.bfloat16), "seq").astype(jnp.float32),
        lax.psum(rate_bias_part.astype(jnp.bfloat16), "seq").astype(jnp.float32),
        lax.psum(scale_part.astype(jnp.bfloat16), "seq").astype(jnp.float32),
        lax.psum(init_part.astype(jnp.bfloat16), "seq").astype(jnp.float32),
        lax.psum(post_gain_part.astype(jnp.bfloat16), "seq").astype(jnp.float32),
        lax.psum(post_bias_part.astype(jnp.bfloat16), "seq").astype(jnp.float32),
        lax.psum(out_weight_grad.astype(jnp.bfloat16), "seq").astype(jnp.float32),
        lax.psum(mlp_gate_grad.astype(jnp.bfloat16), "seq").astype(jnp.float32),
        lax.psum(mlp_up_grad.astype(jnp.bfloat16), "seq").astype(jnp.float32),
        lax.psum(mlp_down_grad.astype(jnp.bfloat16), "seq").astype(jnp.float32),
    )
    gain_grads = lax.psum((norm1_part, norm2_part), ("seq", "head"))
    init_total = summed[7]
    return (
        block_out,
        input_grad,
        gain_grads[0],
        summed[0],
        summed[1],
        summed[2],
        summed[3],
        summed[4],
        summed[5],
        summed[6],
        init_total[:, :head_width, :],
        init_total[:, head_width, :],
        summed[8],
        summed[9],
        summed[10],
        gain_grads[1],
        summed[11],
        summed[12],
        summed[13],
    )


def solution(mesh):
    in_specs = (
        P(("seq", "head"), None),
        P(),
        P(None, "head"),
        P(None, "head"),
        P(None, "head"),
        P(None, "head"),
        P(None, "head"),
        P("head"),
        P("head"),
        P("head", None, None),
        P("head", None),
        P("head"),
        P("head"),
        P("head", None),
        P(),
        P(None, "head"),
        P(None, "head"),
        P("head", None),
        P(("seq", "head"), None),
    )
    out_specs = (
        P(("seq", "head"), None),
        P(("seq", "head"), None),
        P(),
        P(None, "head"),
        P(None, "head"),
        P(None, "head"),
        P(None, "head"),
        P(None, "head"),
        P("head"),
        P("head"),
        P("head", None, None),
        P("head", None),
        P("head"),
        P("head"),
        P("head", None),
        P(),
        P(None, "head"),
        P(None, "head"),
        P("head", None),
    )
    return jax.shard_map(body, mesh=mesh, in_specs=in_specs, out_specs=out_specs, check_vma=False)
```

profile of v0, /device:TPU:0, one launch (start us, length us, event | category | flops | bytes accessed | tf_op | source)
XLA Modules:
  0.0 2290.9 jit_solution(17241817064741074859)
XLA Ops:
  11.3 24.8 %all-gather.5.cloned.1.call-done = bf16[512,2048]{1,0:T(8,128)(2,1)} async-done(((bf16[128,2048]{1,0:T(8,128)(2,1)}), bf16[512,2048]{1,0:T(8,128)(2,1)}) %all-gather.5.cloned.1.call-update) | async-done | bytes 2097168 | tf_op jit(solution)/shard_map/all_gather | solution.py:156
  39.3 4.4 fusion.137
  46.5 3.4 copy.93
  54.8 4.4 fusion.135
  62.0 5.2 copy_bitcast_fusion.2
  67.1 164.2 %while.97 = (s32[]{:T(128)}, f32[8,65,65]{2,1,0:T(8,128)S(1)}, f32[8,65,64]{1,2,0:T(8,128)S(1)}, f32[32,8,16,64]{3,2,1,0:T(8,128)}, f32[32,8,16]{2,1,0:T(8,128)}, /*index=5*/f32[32,8,16,64]{3,2,1,0:T(8,128)}) while((s32[]{:T(128)}, f32[8,65,65]{2,1,0:T(8,128)S(1)}, f32[8,65,64]{1,2,0:T(8,128)S(1)}, ...), condition=%wide.region_2.3_spmd.clone.clone, body=%wide.region_1.2_spmd.clone.sunk.clone | while | flops 65335404 | bytes 1942347 | solution.py:54
  231.3 75.0 %while.93 = (s32[]{:T(128)}, f32[8,65,64]{1,2,0:T(8,128)S(1)}, pred[]{:T(512)}, f32[8,65,65]{2,1,0:T(8,128)S(1)}, f32[8,65,64]{1,2,0:T(8,128)S(1)}, /*index=5*/f32[8,65,64]{1,2,0:T(8,128)S(1)}) while((s32[]{:T(128)}, f32[8,65,64]{1,2,0:T(8,128)S(1)}, pred[]{:T(512)}, f32[8,65,65]{2,1,0:T(8,128)S(1)}, f32[8,65,64]{1,2,0:T(8,128)S(1)}, ...), condition=%wide.region_4.5_spmd.clone, body=%wide.region_3.4_spmd.sunk.clone | while | flops 26024960 | bytes 1466510 | solution.py:184
  232.7 3.4 collective-permute-start
  236.0 6.3 collective-permute-done
  243.6 4.3 collective-permute-start
  247.9 5.4 collective-permute-done
  254.7 4.3 collective-permute-start
  259.0 4.5 collective-permute-done
  264.9 5.2 collective-permute-start
  270.0 4.2 collective-permute-done
  275.6 5.2 collective-permute-start
  280.8 4.2 collective-permute-done
  286.3 5.2 collective-permute-start
  291.5 4.2 collective-permute-done
  297.0 5.2 collective-permute-start
  302.2 4.2 collective-permute-done
  306.4 189.6 %while.96 = (s32[]{:T(128)}, f32[8,65,64]{1,2,0:T(8,128)S(1)}, f32[32,8,16,64]{3,2,1,0:T(8,128)}, f32[32,8,65,64]{2,3,1,0:T(8,128)}, f32[32,8,16,64]{3,2,1,0:T(8...) while((s32[]{:T(128)}, f32[8,65,64]{1,2,0:T(8,128)S(1)}, ...), condition=%wide.region_6.7_spmd.clone.clone, body=%wide.region_5.6_spmd.clone.sunk.clone | while | flops 22418560 | bytes 1732721 | solution.py:84
  498.2 3.8 copy.61
  504.7 6.1 all-reduce.9
  510.8 5.0 multiply_convert_fusion.3
  518.4 34.2 %reduce-scatter.5.cloned.1.call-done = bf16[128,2048]{1,0:T(8,128)(2,1)} async-done(((bf16[512,2048]{1,0:T(8,128)(2,1)}), bf16[128,2048]{1,0:T(8,128)(2,1)}) %reduce-scatter.5.cloned.1.call-update) | async-done | bytes 524304 | tf_op jit(solution)/shard_map/reduce_scatter | solution.py:198
  556.6 22.1 all-gather.7.cloned.1.call-done
  578.8 8.1 fusion.139
  586.8 7.7 fusion.138
  594.5 8.4 all-gather.9.cloned.1.call-done
  602.9 10.3 multiply_convert_fusion
  613.1 6.4 fusion.140
  619.6 7.6 convolution_add_fusion.7
  627.3 44.6 %reduce-scatter.9.cloned.1.call-done = f32[128,2048]{1,0:T(8,128)} async-done(((f32[512,2048]{1,0:T(8,128)}), f32[128,2048]{1,0:T(8,128)}) %reduce-scatter.9.cloned.1.call-update) | async-done | bytes 1048592 | tf_op jit(solution)/shard_map/reduce_scatter | solution.py:228
  677.7 20.0 all-gather.11.cloned.1.call-done
  697.7 6.2 multiply_reduce_fusion.4
  703.9 6.0 all-reduce.8
  709.9 2.9 subtract_multiply_fusion.1
  716.1 201.9 %while.98 = (s32[]{:T(128)}, f32[8,65,64]{1,2,0:T(8,128)S(1)}, f32[32,8,16,64]{3,2,1,0:T(8,128)}, f32[32,8,16]{2,1,0:T(8,128)}, f32[32,8,16,64]{3,2,1,0:T(8,128)}, /*index=5*/f32[32,8,16,64]{3,2,1,0:T(8,128)}) while((s32[]{:T(128)}, f32[8,65,64]{1,2,0:T(8,128)S(1)}, f32[32,8,16,64]{3,2,1,0:T(8,128)}, ...), condition=%wide.region_21.22_spmd.clone.clone, body=%wide.region_20.21_spmd.clone.sunk.clone | while | flops 48552844 | bytes 1615035 | solution.py:102
  918.0 69.7 %while.94 = (s32[]{:T(128)}, f32[8,65,64]{1,2,0:T(8,128)S(1)}, f32[8,65,65]{2,1,0:T(8,128)S(1)}, f32[8,65,64]{1,2,0:T(8,128)S(1)}) while((s32[]{:T(128)}, f32[8,65,64]{1,2,0:T(8,128)S(1)}, f32[8,65,65]{2,1,0:T(8,128)S(1)}, f32[8,65,64]{1,2,0:T(8,128)S(1)}) %tuple.220), condition=%wide.region_23.24_spmd.clone, body=%wide.region_22.23_spmd.sunk.clone | while | flops 25991680 | bytes 1067133 | solution.py:260
  920.0 8.4 collective-permute-done.1
  930.3 8.0 collective-permute-done.1
  940.2 7.6 collective-permute-done.1
  949.7 7.9 collective-permute-done.1
  959.4 7.9 collective-permute-done.1
  969.2 8.5 collective-permute-done.1
  979.6 8.1 collective-permute-done.1
  987.8 335.0 %while.95 = (s32[]{:T(128)}, f32[8,65,64]{1,2,0:T(8,128)S(1)}, bf16[32,8,16,64]{3,2,1,0:T(8,128)(2,1)S(1)}, bf16[32,8,16,64]{3,2,1,0:T(8,128)(2,1)}, bf16[32,8,1...) while((s32[]{:T(128)}, f32[8,65,64]{1,2,0:T(8,128)S(1)}, ...), condition=%wide.region_27.28_spmd.clone, body=%wide.region_24.27_spmd.sunk.clone | while | flops 52939520 | bytes 3343009 | solution.py:84
  1333.9 3.3 fusion.144
  1345.7 7.2 convolution_convert_fusion.9
  1353.0 8.2 convolution_convert_fusion.2
  1361.2 5.1 convolution_convert_fusion
  1366.4 4.8 convolution_convert_fusion.1
  1372.1 4.5 convolution_convert_fusion.3
  1389.6 36.2 %all-reduce.10 = (bf16[2048,8]{0,1:T(8,128)(2,1)S(1)}, bf16[8]{0:T(256)(128)(2,1)S(1)}, bf16[8]{0:T(256)(128)(2,1)S(1)}, bf16[512]{0:T(512)(128)(2,1)S(1)}, bf16[512]{0:T(512)(128)(2,1)S(1)}) all-reduce(bf16[2048,8]{0,1:T(8,128)(2,1)S(1)} %convolution_convert_fusion.10, ...), channel_id=1, replica_groups=mesh['seq'=8,'head'=4] {'seq'}, use_global_device_ids=true, to_apply=%region_36.37 | all-reduce | flops 17424 | bytes 69696 | tf_op jit(solution)/shard_map/psum | solution.py:301
  1430.1 42.8 %all-reduce.7 = (f32[2048]{0:T(1024)}, f32[2048]{0:T(1024)}) all-reduce(f32[2048]{0:T(1024)S(1)} %get-tuple-element.720, f32[2048]{0:T(1024)S(1)} %get-tuple-element.715), channel_id=1, replica_groups=mesh['seq'=8,'head'=4] {'seq','head'}, use_global_device_ids=true, to_apply=%region_31.32 | all-reduce | flops 4096 | bytes 32768 | tf_op jit(solution)/shard_map/psum | solution.py:312
  1472.9 3.1 fusion.113
  1476.0 770.8 %all-reduce.14.cloned.1.call-done = (bf16[2048,512]{1,0:T(8,128)(2,1)}, bf16[2048,512]{1,0:T(8,128)(2,1)}, bf16[2048,512]{1,0:T(8,128)(2,1)}, bf16[2048,512]{1,0...) async-done(((bf16[2048,512]{1,0:T(8,128)(2,1)}, ...) | async-done | bytes 27460624 | tf_op jit(solution)/shard_map/psum | solution.py:297
  2250.0 4.3 convert_element_type.216
  2257.0 2.7 convert_element_type.220
  2259.7 2.7 convert_element_type.222
  2266.1 5.9 convert_element_type.237
  2272.0 5.9 convert_element_type.239
  2278.0 5.9 convert_element_type.241
  (1775 shorter events, 990.9 us)
Async XLA Ops:
  7.2 508.6 %copy-start = (bf16[512,2048]{1,0:T(8,128)(2,1)S(1)}, bf16[512,2048]{1,0:T(8,128)(2,1)}, u32[]{:S(2)}) copy-start(bf16[512,2048]{1,0:T(8,128)(2,1)} %param.44) | copy-start | bytes 6291460
  7.2 3.6 copy-start.29
  7.2 3.8 copy-start.35
  7.2 29.0 %copy-start.30 = (bf16[2048,8]{0,1:T(8,128)(2,1)S(1)}, bf16[2048,8]{0,1:T(8,128)(2,1)}, u32[]{:S(2)}) copy-start(bf16[2048,8]{0,1:T(8,128)(2,1)} %param.37) | copy-start | bytes 98308
  7.2 29.0 %copy-start.38 = (f32[8]{0:T(128)S(1)}, f32[8]{0:T(128)}, u32[]{:S(2)}) copy-start(f32[8]{0:T(128)} %param.39) | copy-start | bytes 100
  7.2 28.9 %copy-start.42 = (f32[8]{0:T(128)S(1)}, f32[8]{0:T(128)}, u32[]{:S(2)}) copy-start(f32[8]{0:T(128)} %param.38) | copy-start | bytes 100
  7.3 28.9 %all-gather.5.cloned.1.call-start = ((), (), s32[]{:S(2)}) async-start(), calls=%async_computation.4 | async-start | bytes 2621440 | tf_op jit(solution)/shard_map/all_gather | solution.py:156
  10.7 541.9 %reduce-scatter.5.cloned.1.call-start = ((), (), s32[]{:S(2)}) async-start(), calls=%async_computation.5 | async-start | bytes 2621440 | tf_op jit(solution)/shard_map/reduce_scatter | solution.py:198
  46.4 3.5 copy-start.9
  46.4 3.5 copy-start.24
  232.7 9.6 collective-permute-start
  243.6 9.7 collective-permute-start
  254.7 8.8 collective-permute-start
  264.9 9.3 collective-permute-start
  275.6 9.4 collective-permute-start
  286.3 9.4 collective-permute-start
  297.0 9.4 collective-permute-start
  502.0 8.9 copy-start.36
  502.0 8.9 copy-start.45
  518.4 34.2 %copy-start.2 = (bf16[128,2048]{1,0:T(8,128)(2,1)S(1)}, bf16[128,2048]{1,0:T(8,128)(2,1)}, u32[]{:S(2)}) copy-start(bf16[128,2048]{1,0:T(8,128)(2,1)} %param.31) | copy-start | bytes 1572868
  518.4 35.5 %copy-start.31 = (f32[2048]{0:T(1024)S(1)}, f32[2048]{0:T(1024)}, u32[]{:S(2)}) copy-start(f32[2048]{0:T(1024)} %param.45) | copy-start | bytes 24580
  518.4 60.4 %all-gather.7.cloned.1.call-start = ((), (), s32[]{:S(2)}) async-start(), calls=%async_computation.6 | async-start | bytes 2621440 | tf_op jit(solution)/shard_map/all_gather | solution.py:208
  556.0 46.9 %all-gather.9.cloned.1.call-start = ((), (), s32[]{:S(2)}) async-start(), calls=%async_computation.8 | async-start | bytes 2621440 | tf_op jit(solution)/shard_map/all_gather | solution.py:157
  556.6 115.3 %reduce-scatter.9.cloned.1.call-start = ((), (), s32[]{:S(2)}) async-start(), calls=%async_computation.9 | async-start | bytes 5242880 | tf_op jit(solution)/shard_map/reduce_scatter | solution.py:228
  578.8 8.1 copy-start.43
  613.1 6.4 copy-start.46
  613.1 6.5 copy-start.26
  627.2 44.7 %copy-start.5 = (bf16[128,2048]{1,0:T(8,128)(2,1)S(1)}, bf16[128,2048]{1,0:T(8,128)(2,1)}, u32[]{:S(2)}) copy-start(bf16[128,2048]{1,0:T(8,128)(2,1)} %reduce-scatter.5.cloned.1.call-done) | copy-start | bytes 1572868
  627.2 70.5 %all-gather.11.cloned.1.call-start = ((), (), s32[]{:S(2)}) async-start(), calls=%async_computation.10 | async-start | bytes 2621440 | tf_op jit(solution)/shard_map/all_gather | solution.py:241
  674.9 753.7 %reduce-scatter.11.cloned.1.call-start = ((), (), s32[]{:S(2)}) async-start(), calls=%async_computation.11 | async-start | bytes 2621440 | tf_op jit(solution)/shard_map/reduce_scatter | solution.py:283
  697.7 12.3 copy-start.37
  918.0 69.7 %copy-start.4 = (bf16[32,8,16,64]{3,2,1,0:T(8,128)(2,1)S(1)}, bf16[32,8,16,64]{3,2,1,0:T(8,128)(2,1)}, u32[]{:S(2)}) copy-start(bf16[32,8,16,64]{3,2,1,0:T(8,128)(2,1)} %copy-done.3) | copy-start | bytes 1572868
  918.7 9.7 collective-permute-start.1
  929.0 9.3 collective-permute-start.1
  938.9 8.9 collective-permute-start.1
  948.4 9.2 collective-permute-start.1
  958.1 9.2 collective-permute-start.1
  967.9 9.8 collective-permute-start.1
  978.3 9.4 collective-permute-start.1
  1326.1 4.5 copy-start.13
  1330.5 8.0 copy-start.14
  1333.9 6.2 copy-start.16
  1333.9 3.3 copy-start.22
  1344.4 128.5 %reduce-scatter.7.cloned.1.call-start = ((), (), s32[]{:S(2)}) async-start(), calls=%async_computation.7 | async-start | bytes 2621440 | tf_op jit(solution)/shard_map/reduce_scatter | solution.py:214
  1352.9 8.3 copy-start.27
  1352.9 893.9 %all-reduce.14.cloned.1.call-start = ((), (), s32[]{:S(2)}) async-start(), calls=%async_computation.12 | async-start | bytes 55054336 | tf_op jit(solution)/shard_map/psum | solution.py:297
  1353.0 8.3 copy-start.44
  1361.2 5.1 copy-start.47
  1372.1 4.5 copy-start.10
  1372.1 4.5 copy-start.17
  1387.2 41.5 %copy-start.32 = (f32[2048]{0:T(1024)S(1)}, f32[2048]{0:T(1024)}, u32[]{:S(2)}) copy-start(f32[2048]{0:T(1024)} %param.32) | copy-start | bytes 24580
  1387.2 41.5 %copy-start.34 = (f32[128]{0:T(128)S(1)}, f32[128]{0:T(128)}, u32[]{:S(2)}) copy-start(f32[128]{0:T(128)} %copy-done.33) | copy-start | bytes 1540
  1387.2 85.7 %copy-start.6 = (bf16[128,2048]{1,0:T(8,128)(2,1)S(1)}, bf16[128,2048]{1,0:T(8,128)(2,1)}, u32[]{:S(2)}) copy-start(bf16[128,2048]{1,0:T(8,128)(2,1)} %reduce-scatter.5.cloned.1.call-done) | copy-start | bytes 1572868
  1387.2 85.7 %copy-start.8 = (f32[128,2048]{1,0:T(8,128)S(1)}, f32[128,2048]{1,0:T(8,128)}, u32[]{:S(2)}) copy-start(f32[128,2048]{1,0:T(8,128)} %reduce-scatter.9.cloned.1.call-done) | copy-start | bytes 3145732
  1387.2 85.7 %copy-start.12 = (bf16[128,2048]{1,0:T(8,128)(2,1)S(1)}, bf16[128,2048]{1,0:T(8,128)(2,1)}, u32[]{:S(2)}) copy-start(bf16[128,2048]{1,0:T(8,128)(2,1)} %param.49) | copy-start | bytes 1572868
  2250.0 4.4 copy-start.21
  2257.0 9.1 slice-start.4
  2259.7 3.7 copy-start.18
  2259.7 6.4 slice-start.5
  2263.4 8.6 slice-start.2
  2266.1 5.9 slice-start.3
  2266.1 11.8 slice-start
  2272.0 5.9 slice-start.1
  2277.9 5.9 copy-start.1
  (15 other events, 30.9 us)
Sparse Core Ops, SparseCore 0:
  10.9 25.2 all-gather.4
  518.5 34.0 reduce-scatter.4
  556.1 22.5 all-gather.6
  580.2 22.5 all-gather.8
  627.3 44.4 reduce-scatter.8
  675.0 22.5 all-gather.10
  1344.5 33.6 reduce-scatter.10
  1381.4 31.4 reduce-scatter.6
  1421.0 825.7 all-reduce.13
where the time goes:
time: 2320 us; the launch traced here: 2290 us
  waiting for transfers between devices  1010 us (44%)
  matrix products  658 us (28%)
  local copies, waits for them, and re-layouts  380 us (16%)
  blocking collectives  91.2 us (4%)
  other arithmetic  81.4 us (4%)
  starting transfers between devices  42.1 us (2%)
    psum x1, waiting for transfers between devices, body(): lax.psum(query_grad.astype(jnp.bfloat16), 'seq').astype(jnp.float32)  771 us
    squeeze x256, local copies, waits for them, and re-layouts, segment_map(): lax.scan(turn, (identity, zero_state), (key_blocks, value_blocks, rate_bl...  213 us
    dot_general x128, matrix products, inner_block(): jnp.einsum('hmi,hio->hmo', key_aug, inner_state, precision=HIGHEST)  90.1 us
    ppermute x14, waiting for transfers between devices, passed_along(): return lax.ppermute(shard, axis, pairs)  89.2 us
    dot_general x64, matrix products, step_matrix_of(): jnp.einsum('hni,hnj->hij', weighted_keys, key_aug, precision=HIGHEST)  53.1 us
    dot_general x96, matrix products, inner_block(): jnp.einsum('hni,hno->hio', key_aug * rate_block[:, :, None], errors, prec...  52.9 us
    dot_general x32, matrix products, turn(): jnp.einsum('hni,hno->hio', weighted_keys, value_block - key_block, precis...  47.8 us
  transfers between devices with their start and end apart: 23, of which 21 were waited for; matrix products, arithmetic and copies ran while one was open for 3% of the time, Pallas kernels for 0%

commit v1 on v0

v1 whole, which is shorter than its diff:
```python
import functools
import jax, jax.numpy as jnp
from jax import lax
from jax.experimental import pallas as pl
from jax.experimental.pallas import tpu as pltpu
from jax.sharding import PartitionSpec as P

CHUNK=128
MB=16
F32=jnp.float32; BF=jnp.bfloat16
LN=128
HW=64
VL=48*1024*1024

def mm(a,b,ca,cb):
    return lax.dot_general(a.astype(BF),b.astype(BF),(((ca,),(cb,)),((),())),preferred_element_type=F32)
def nn(a,b): return mm(a,b,1,0)
def nt(a,b): return mm(a,b,1,1)
def tn(a,b): return mm(a,b,0,0)
def split(a):
    hi=a.astype(BF)
    return hi,(a-hi.astype(F32)).astype(BF)
def nn3(a,b):
    ah,al=a; bh,bl=b
    return nn(ah,bh)+(nn(ah,bl)+nn(al,bh))

def lanes(shape): return lax.broadcasted_iota(jnp.int32,shape,1)
def rows(shape): return lax.broadcasted_iota(jnp.int32,shape,0)
def head_of(x,odd):
    y=pltpu.roll(x,HW,1) if odd else x
    return jnp.where(lanes(x.shape)<HW,y,0.0)
def aug(x): return jnp.where(lanes(x.shape)==HW,1.0,x)
def pair(a,b):
    return jnp.where(lanes(a.shape)<HW,a,pltpu.roll(b,HW,1))
def column(block,h):
    return jnp.sum(jnp.where(lanes(block.shape)==h,block,0.0),axis=1,keepdims=True)
def causal(C): return rows((C,C))>=lanes((C,C))
def earlier(C): return (rows((C,C))//MB)>(lanes((C,C))//MB)
def level(C,size):
    i=rows((C,C)); j=lanes((C,C))
    return (i//(2*size)==j//(2*size))&((i//size)%2==1)&((j//size)%2==0)

def block_inverse(low,C):
    eye=jnp.where(rows((C,C))==lanes((C,C)),1.0,0.0)
    size=MB
    t=eye-jnp.where(level(C,size),low,0.0)
    size*=2
    while size<C:
        part=split(jnp.where(level(C,size),low,0.0))
        ts=split(t)
        t=t-nn3(split(nn3(ts,part)),ts)
        size*=2
    return t

def map_kernel(C,k_ref,v_ref,r_ref,t_ref,uw_ref,x_ref,y_ref):
    p=pl.program_id(0)
    N=k_ref.shape[0]
    last=y_ref.shape[0]-1
    @pl.when(p==0)
    def _(): y_ref[last]=jnp.zeros((80,LN),BF)
    for odd in range(2):
        h=2*p+odd
        total=None
        for c in range(N//C):
            sl=pl.ds(c*C,C)
            k=head_of(k_ref[sl,:],odd)
            w=head_of(v_ref[sl,:],odd)-k
            ka=aug(k)
            r=column(r_ref[sl,:],h)
            kr=ka*r
            t=block_inverse(jnp.where(earlier(C),nt(ka,kr),0.0),C)
            t_ref[odd,c]=t.astype(BF)
            uw=nn(t,jnp.concatenate([ka,w],axis=1))
            uw_ref[odd,sl,:]=uw.astype(BF)
            xc=tn(kr,jnp.where(lanes(uw.shape)<LN,-uw,uw))
            x_ref[odd,c]=xc.astype(BF)
            total=xc if total is None else total+xc+nn(xc[:,:LN],total)
        a=total[:,:LN]; o=total[:,LN:]
        y_ref[h]=pair(a,o)[:80].astype(BF)
        col=jnp.sum(jnp.where(lanes(a.shape)==HW,a,0.0),axis=1,keepdims=True)[:80]
        y_ref[last]=jnp.where(lanes((80,LN))==h,col,y_ref[last].astype(F32)).astype(BF)

def local_kernel(C,q_ref,k_ref,r_ref,t_ref,uw_ref,qe_ref,zo_ref,pt_ref,vv_ref):
    p=pl.program_id(0)
    N=q_ref.shape[0]
    for c in range(N//C):
        sl=pl.ds(c*C,C)
        offs=[]
        for odd in range(2):
            h=2*p+odd
            q=head_of(q_ref[sl,:],odd); qa=aug(q)
            ka=aug(head_of(k_ref[sl,:],odd))
            kr=ka*column(r_ref[sl,:],h)
            pm=jnp.where(causal(C),nt(qa,kr),0.0)
            t=t_ref[odd,c]
            puw=nn(pm,uw_ref[odd,sl,:])
            qe_ref[odd,sl,:]=(qa-puw[:,:LN]).astype(BF)
            offs.append(q+puw[:,LN:])
            pt_ref[odd,c]=nn(pm,t).astype(BF)
            vv_ref[odd,sl,:]=tn(t,kr).astype(BF)
        zo_ref[sl,:]=pair(offs[0],offs[1])

def unpack(y,yb,h):
    y=y.astype(F32)
    col=column(yb.astype(F32),h)
    ln=lanes(y.shape)
    a=jnp.where(ln<HW,y,jnp.where(ln==HW,col,0.0))
    o=jnp.where(ln<HW,pltpu.roll(y,HW,1),0.0)
    pad=jnp.zeros((LN-80,LN),F32)
    return jnp.concatenate([a,pad],0),jnp.concatenate([o,pad],0)

def start_of(is_ref,ib_ref,odd):
    s=jnp.concatenate([is_ref[odd],ib_ref[odd],jnp.zeros((LN-HW-1,HW),F32)],axis=0)
    return jnp.concatenate([s,jnp.zeros_like(s)],axis=1)

def forward_kernel(C,seg_ref,y_ref,yb_ref,is_ref,ib_ref,x_ref,uw_ref,qe_ref,zo_ref,z_ref,e_ref,s_ref):
    p=pl.program_id(0)
    N=zo_ref.shape[0]
    segs=y_ref.shape[0]
    seg=seg_ref[0]
    add=[[None]*(N//C) for _ in range(2)]
    for odd in range(2):
        h=2*p+odd
        s=start_of(is_ref,ib_ref,odd)
        for j in range(segs-1):
            a,o=unpack(y_ref[j,odd],yb_ref[j,0],h)
            s=s+jnp.where(j<seg,1.0,0.0)*(nn(a,s)+o)
        for c in range(N//C):
            sl=pl.ds(c*C,C)
            sb=s.astype(BF)
            s_ref[odd,c]=sb
            uw=uw_ref[odd,sl,:]
            e_ref[odd,sl,:]=(nn(uw[:,:LN],sb)-uw[:,LN:].astype(F32)).astype(BF)
            add[odd][c]=nn(qe_ref[odd,sl,:],sb)
            x=x_ref[odd,c]
            s=s+nn(x[:,:LN],sb)+x[:,LN:].astype(F32)
    for c in range(N//C):
        sl=pl.ds(c*C,C)
        z_ref[sl,:]=zo_ref[sl,:]+pair(add[0][c],add[1][c])

def state_grad_kernel(C,dz_ref,qe_ref,x_ref,d_ref,dseg_ref):
    N=dz_ref.shape[0]
    outs=[]
    for odd in range(2):
        g=jnp.zeros((LN,LN),F32)
        for c in reversed(range(N//C)):
            sl=pl.ds(c*C,C)
            dz=head_of(dz_ref[sl,:],odd)
            d=tn(qe_ref[odd,sl,:],dz)
            d_ref[odd,c]=d
            g=g+tn(x_ref[odd,c][:,:LN],g)+d
        outs.append(g)
    dseg_ref[0]=pair(outs[0],outs[1])[:72]

def query_grad_kernel(C,q_ref,k_ref,r_ref,dz_ref,e_ref,s_ref,pt_ref,dq_ref,b_ref,l_ref):
    p=pl.program_id(0)
    N=q_ref.shape[0]
    for c in range(N//C):
        sl=pl.ds(c*C,C)
        outs=[]
        for odd in range(2):
            h=2*p+odd
            dz=head_of(dz_ref[sl,:],odd); dzb=dz.astype(BF)
            qa=aug(head_of(q_ref[sl,:],odd))
            ka=aug(head_of(k_ref[sl,:],odd))
            kr=ka*column(r_ref[sl,:],h)
            fu=jnp.where(causal(C),-nt(dzb,e_ref[odd,sl,:]),0.0).astype(BF)
            outs.append(dz+nt(dzb,s_ref[odd,c])+nn(fu,kr))
            b_ref[odd,sl,:]=tn(fu,qa).astype(BF)
            l_ref[odd,sl,:]=-tn(pt_ref[odd,c],dzb)
        dq_ref[sl,:]=pair(outs[0],outs[1]).astype(BF)

def key_grad_kernel(C,seg_ref,y_ref,yb_ref,da_ref,k_ref,r_ref,e_ref,s_ref,vv_ref,b_ref,l_ref,x_ref,d_ref,dk_ref,dv_ref,dr_ref,gi_ref):
    p=pl.program_id(0)
    N=k_ref.shape[0]
    segs=y_ref.shape[0]
    seg=seg_ref[0]
    @pl.when(p==0)
    def _(): dr_ref[...]=jnp.zeros_like(dr_ref)
    pad=jnp.zeros((LN-72,LN),F32)
    dks=[[None]*(N//C) for _ in range(2)]
    lams=[[None]*(N//C) for _ in range(2)]
    for odd in range(2):
        h=2*p+odd
        full=jnp.zeros((LN,LN),F32)
        g=jnp.zeros((LN,LN),F32)
        for j in reversed(range(segs)):
            a,_=unpack(y_ref[j,odd],yb_ref[j,0],h)
            d=jnp.concatenate([head_of(da_ref[j,0],odd),pad],0)
            full=full+tn(a,full)+d
            g=jnp.where(j==seg+1,full,g)
        gi_ref[odd]=full[:72]
        for c in reversed(range(N//C)):
            sl=pl.ds(c*C,C)
            gb=g.astype(BF)
            ka=aug(head_of(k_ref[sl,:],odd))
            r=column(r_ref[sl,:],h)
            kr=ka*r
            e=e_ref[odd,sl,:]
            lam=l_ref[odd,sl,:]-nn(vv_ref[odd,sl,:],gb)
            lb=lam.astype(BF)
            hu=jnp.where(earlier(C),-nt(lb,e),0.0).astype(BF)
            b=b_ref[odd,sl,:].astype(F32)+tn(hu,ka)-nt(e,gb)
            dks[odd][c]=r*b+nt(lb,s_ref[odd,c])+nn(hu,kr)+lam
            lams[odd][c]=lam
            dr=jnp.sum(ka*b,axis=1,keepdims=True)
            dr_ref[sl,:]=jnp.where(lanes((C,dr_ref.shape[1]))==h,dr,dr_ref[sl,:])
            g=g+tn(x_ref[odd,c][:,:LN],gb)+d_ref[odd,c]
    for c in range(N//C):
        sl=pl.ds(c*C,C)
        dk_ref[sl,:]=pair(dks[0][c],dks[1][c]).astype(BF)
        dv_ref[sl,:]=-pair(lams[0][c],lams[1][c]).astype(BF)

def params(): return pltpu.CompilerParams(dimension_semantics=("arbitrary",),vmem_limit_bytes=VL)
def S(shape,dt): return jax.ShapeDtypeStruct(shape,dt)

def specs(N,hl,C):
    nc=N//C
    d={}
    d["row"]=pl.BlockSpec((N,LN),lambda p,*_:(0,p))
    d["rate"]=pl.BlockSpec((N,hl),lambda p,*_:(0,0))
    d["cc"]=pl.BlockSpec((2,nc,C,C),lambda p,*_:(p,0,0,0))
    d["n256"]=pl.BlockSpec((2,N,2*LN),lambda p,*_:(p,0,0))
    d["n128"]=pl.BlockSpec((2,N,LN),lambda p,*_:(p,0,0))
    d["x"]=pl.BlockSpec((2,nc,LN,2*LN),lambda p,*_:(p,0,0,0))
    d["s"]=pl.BlockSpec((2,nc,LN,LN),lambda p,*_:(p,0,0,0))
    d["y"]=pl.BlockSpec((hl+1,80,LN),lambda p,*_:(0,0,0))
    return d

def build(N,hl,segs,C=128):
    nc=N//C; sp=specs(N,hl,C); G=(hl//2,)
    w=hl*HW
    K={}
    K["map"]=pl.pallas_call(functools.partial(map_kernel,C),grid=G,in_specs=[sp["row"],sp["row"],sp["rate"]],
        out_specs=[sp["cc"],sp["n256"],sp["x"],sp["y"]],
        out_shape=[S((hl,nc,C,C),BF),S((hl,N,2*LN),BF),S((hl,nc,LN,2*LN),BF),S((hl+1,80,LN),BF)],compiler_params=params(),name="segment_maps")
    K["local"]=pl.pallas_call(functools.partial(local_kernel,C),grid=G,in_specs=[sp["row"],sp["row"],sp["rate"],sp["cc"],sp["n256"]],
        out_specs=[sp["n128"],sp["row"],sp["cc"],sp["n128"]],
        out_shape=[S((hl,N,LN),BF),S((N,w),F32),S((hl,nc,C,C),BF),S((hl,N,LN),BF)],compiler_params=params(),name="local_parts")
    yall=pl.BlockSpec((segs,2,80,LN),lambda p,*_:(0,p,0,0)); yball=pl.BlockSpec((segs,1,80,LN),lambda p,*_:(0,hl,0,0))
    dall=pl.BlockSpec((segs,1,72,LN),lambda p,*_:(0,p,0,0))
    ist=pl.BlockSpec((2,HW,HW),lambda p,*_:(p,0,0)); ibs=pl.BlockSpec((2,1,HW),lambda p,*_:(p,0,0))
    def gs(i,o): return pltpu.PrefetchScalarGridSpec(num_scalar_prefetch=1,grid=G,in_specs=i,out_specs=o)
    K["forward"]=pl.pallas_call(functools.partial(forward_kernel,C),grid_spec=gs([yall,yball,ist,ibs,sp["x"],sp["n256"],sp["n128"],sp["row"]],[sp["row"],sp["n128"],sp["s"]]),
        out_shape=[S((N,w),F32),S((hl,N,LN),BF),S((hl,nc,LN,LN),BF)],compiler_params=params(),name="forward_states")
    K["sgrad"]=pl.pallas_call(functools.partial(state_grad_kernel,C),grid=G,in_specs=[sp["row"],sp["n128"],sp["x"]],
        out_specs=[sp["s"],pl.BlockSpec((1,72,LN),lambda p:(p,0,0))],out_shape=[S((hl,nc,LN,LN),F32),S((hl//2,72,LN),F32)],compiler_params=params(),name="state_grads")
    K["qgrad"]=pl.pallas_call(functools.partial(query_grad_kernel,C),grid=G,in_specs=[sp["row"],sp["row"],sp["rate"],sp["row"],sp["n128"],sp["s"],sp["cc"]],
        out_specs=[sp["row"],sp["n128"],sp["n128"]],out_shape=[S((N,w),BF),S((hl,N,LN),BF),S((hl,N,LN),F32)],compiler_params=params(),name="query_grads")
    K["kgrad"]=pl.pallas_call(functools.partial(key_grad_kernel,C),grid_spec=gs([yall,yball,dall,sp["row"],sp["rate"],sp["n128"],sp["s"],sp["n128"],sp["n128"],sp["n128"],sp["x"],sp["s"]],
        [sp["row"],sp["row"],sp["rate"],pl.BlockSpec((2,72,LN),lambda p,*_:(p,0,0))]),
        out_shape=[S((N,w),BF),S((N,w),BF),S((N,hl),F32),S((hl,72,LN),F32)],compiler_params=params(),name="key_grads")
    return K


EPSILON = 1e-06


def gelu_tanh(values):
    return jax.nn.gelu(values, approximate=True)


def dot(a, b):
    return jnp.dot(a, b, preferred_element_type=F32)


def body(
    block_input,
    norm1_gain,
    query_weight,
    key_weight,
    value_weight,
    gate_weight,
    rate_weight,
    rate_bias,
    rate_scale,
    init_state,
    init_bias,
    post_gain,
    post_bias,
    out_weight,
    norm2_gain,
    mlp_gate,
    mlp_up,
    mlp_down,
    out_cotangent,
):
    local_heads = init_state.shape[0]
    head_width = init_state.shape[1]
    model_width = block_input.shape[1]
    seq_index = lax.axis_index("seq")
    segs = lax.axis_size("seq")
    tokens = block_input.shape[0] * lax.axis_size("head")
    K = build(tokens, local_heads, segs, CHUNK)
    seg = seq_index.astype(jnp.int32).reshape(1)

    input_f32 = block_input.astype(F32)
    scale_in = lax.rsqrt(jnp.mean(input_f32 * input_f32, axis=-1, keepdims=True) + EPSILON)
    unit_in = input_f32 * scale_in
    normed = (unit_in * norm1_gain).astype(BF)
    group_in = lax.all_gather(normed, "head", axis=0, tiled=True)
    group_cot = lax.all_gather(out_cotangent, "head", axis=0, tiled=True)
    query_rows = dot(group_in, query_weight)
    key_rows = dot(group_in, key_weight)
    value_rows = dot(group_in, value_weight)
    gate_pre = dot(group_in, gate_weight)
    rate_pre = dot(group_in, rate_weight) + rate_bias
    rate_sig = jax.nn.sigmoid(rate_pre)
    rate_rows = rate_sig * rate_scale

    inv, uw, step_maps, seg_map = K["map"](key_rows, value_rows, rate_rows)
    all_maps = lax.all_gather(seg_map, "seq", axis=0, tiled=False)
    q_eff, z_off, pt, vv = K["local"](query_rows, key_rows, rate_rows, inv, uw)
    z_rows, errors, states = K["forward"](
        seg, all_maps, all_maps, init_state, init_bias[:, None, :], step_maps, uw, q_eff, z_off
    )
    stat_sums = lax.psum((jnp.sum(z_rows, axis=-1), jnp.sum(z_rows * z_rows, axis=-1)), "head")
    row_mean = stat_sums[0] / model_width
    row_var = stat_sums[1] / model_width - row_mean * row_mean
    inv_scale = lax.rsqrt(row_var + EPSILON)[:, None]
    z_hat = (z_rows - row_mean[:, None]) * inv_scale
    post_out = z_hat * post_gain + post_bias
    gate_act, gelu_back = jax.vjp(gelu_tanh, gate_pre)
    gated_out = (gate_act * post_out).astype(BF)
    attn_out = lax.psum_scatter(
        dot(gated_out, out_weight).astype(BF), "head", scatter_dimension=0, tiled=True
    ).astype(F32)
    middle = input_f32 + attn_out
    scale_mid = lax.rsqrt(jnp.mean(middle * middle, axis=-1, keepdims=True) + EPSILON)
    unit_mid = middle * scale_mid
    mlp_input = (unit_mid * norm2_gain).astype(BF)
    mlp_group = lax.all_gather(mlp_input, "head", axis=0, tiled=True)
    gate_mlp = dot(mlp_group, mlp_gate)
    up_mlp = dot(mlp_group, mlp_up)
    silu_gate, silu_back = jax.vjp(jax.nn.silu, gate_mlp)
    hidden = (silu_gate * up_mlp).astype(BF)
    mlp_out = lax.psum_scatter(
        dot(hidden, mlp_down).astype(BF), "head", scatter_dimension=0, tiled=True
    ).astype(F32)
    block_out = (middle + mlp_out).astype(BF)
    cot_f32 = out_cotangent.astype(F32)
    d_hidden = dot(group_cot, mlp_down.T)
    mlp_down_grad = dot(hidden.T, group_cot)
    d_gate_mlp = silu_back(d_hidden * up_mlp)[0].astype(BF)
    d_up_mlp = (d_hidden * silu_gate).astype(BF)
    mlp_gate_grad = dot(mlp_group.T, d_gate_mlp)
    mlp_up_grad = dot(mlp_group.T, d_up_mlp)
    mlp_sums = lax.psum(
        (mlp_down_grad.astype(BF), mlp_gate_grad.astype(BF), mlp_up_grad.astype(BF)), "seq"
    )
    d_mlp_input = lax.psum_scatter(
        (dot(d_gate_mlp, mlp_gate.T) + dot(d_up_mlp, mlp_up.T)).astype(BF),
        "head",
        scatter_dimension=0,
        tiled=True,
    ).astype(F32)
    scaled_mid = d_mlp_input * norm2_gain
    norm2_part = jnp.sum(d_mlp_input * unit_mid, axis=0)
    d_middle = cot_f32 + scale_mid * (
        scaled_mid - unit_mid * jnp.mean(scaled_mid * unit_mid, axis=-1, keepdims=True)
    )
    d_attn = d_middle.astype(BF)
    d_attn_group = lax.all_gather(d_attn, "head", axis=0, tiled=True)
    d_gated = dot(d_attn_group, out_weight.T)
    out_weight_grad = dot(gated_out.T, d_attn_group)
    d_post = d_gated * gate_act
    d_gate_pre = gelu_back(d_gated * post_out)[0].astype(BF)
    post_gain_part = jnp.sum(d_post * z_hat, axis=0)
    post_bias_part = jnp.sum(d_post, axis=0)
    d_zhat = d_post * post_gain
    back_sums = lax.psum((jnp.sum(d_zhat, axis=-1), jnp.sum(d_zhat * z_hat, axis=-1)), "head")
    d_z = inv_scale * (
        d_zhat - back_sums[0][:, None] / model_width - z_hat * (back_sums[1][:, None] / model_width)
    )
    step_grads, seg_grad = K["sgrad"](d_z, q_eff, step_maps)
    all_grads = lax.all_gather(seg_grad, "seq", axis=0, tiled=False)
    d_query, b_part, lam_part = K["qgrad"](query_rows, key_rows, rate_rows, d_z, errors, states, pt)
    d_key, d_value, d_rate, init_grad = K["kgrad"](
        seg, all_maps, all_maps, all_grads, key_rows, rate_rows, errors, states, vv,
        b_part, lam_part, step_maps, step_grads,
    )
    d_rate_pre = (d_rate * rate_scale * rate_sig * (1.0 - rate_sig)).astype(BF)
    scale_part = jnp.sum(d_rate * rate_sig, axis=0)
    rate_bias_part = jnp.sum(d_rate_pre.astype(F32), axis=0)
    gate_grad = dot(group_in.T, d_gate_pre)
    query_grad = dot(group_in.T, d_query)
    key_grad = dot(group_in.T, d_key)
    value_grad = dot(group_in.T, d_value)
    rate_weight_part = dot(group_in.T, d_rate_pre)
    total = dot(d_query, query_weight.T)
    total = total + dot(d_key, key_weight.T)
    total = total + dot(d_value, value_weight.T)
    total = total + dot(d_gate_pre, gate_weight.T)
    d_normed = lax.psum_scatter(
        (total + dot(d_rate_pre, rate_weight.T)).astype(BF), "head", scatter_dimension=0, tiled=True
    ).astype(F32)
    scaled_in = d_normed * norm1_gain
    norm1_part = jnp.sum(d_normed * unit_in, axis=0)
    input_grad = d_middle + scale_in * (
        scaled_in - unit_in * jnp.mean(scaled_in * unit_in, axis=-1, keepdims=True)
    )
    mid_in = (out_weight_grad.astype(BF), gate_grad.astype(BF), d_query)
    mid_in, mlp_sums = lax.optimization_barrier((mid_in, mlp_sums))
    mid_sums = lax.psum(mid_in[:2], "seq")
    late_in = (query_grad.astype(BF), key_grad.astype(BF), value_grad.astype(BF))
    late_in, mid_sums = lax.optimization_barrier((late_in, mid_sums))
    late_sums = lax.psum(late_in, "seq")
    small = lax.psum(
        (rate_weight_part, rate_bias_part, scale_part, post_gain_part, post_bias_part), "seq"
    )
    gain_grads = lax.psum((norm1_part, norm2_part), ("seq", "head"))
    up = lambda x: x.astype(F32)
    return (
        block_out,
        input_grad,
        gain_grads[0],
        up(late_sums[0]),
        up(late_sums[1]),
        up(late_sums[2]),
        up(mid_sums[1]),
        small[0],
        small[1],
        small[2],
        init_grad[:, :head_width, :head_width],
        init_grad[:, head_width, :head_width],
        small[3],
        small[4],
        up(mid_sums[0]),
        gain_grads[1],
        up(mlp_sums[1]),
        up(mlp_sums[2]),
        up(mlp_sums[0]),
    )


def solution(mesh):
    in_specs = (
        P(("seq", "head"), None),
        P(),
        P(None, "head"),
        P(None, "head"),
        P(None, "head"),
        P(None, "head"),
        P(None, "head"),
        P("head"),
        P("head"),
        P("head", None, None),
        P("head", None),
        P("head"),
        P("head"),
        P("head", None),
        P(),
        P(None, "head"),
        P(None, "head"),
        P("head", None),
        P(("seq", "head"), None),
    )
    out_specs = (
        P(("seq", "head"), None),
        P(("seq", "head"), None),
        P(),
        P(None, "head"),
        P(None, "head"),
        P(None, "head"),
        P(None, "head"),
        P(None, "head"),
        P("head"),
        P("head"),
        P("head", None, None),
        P("head", None),
        P("head"),
        P("head"),
        P("head", None),
        P(),
        P(None, "head"),
        P(None, "head"),
        P("head", None),
    )
    return jax.shard_map(body, mesh=mesh, in_specs=in_specs, out_specs=out_specs, check_vma=False)
```

time: 2320 us -> 1420 us (0.61)
  matrix products: 658 us -> 118 us
  local copies, waits for them, and re-layouts: 380 us -> 26.3 us
  Pallas kernels: 0 us -> 97.1 us
  starting transfers between devices: 42.1 us -> 0.75 us
  other arithmetic: 81.4 us -> 56.9 us
    dot_general x905 -> x27, matrix products: 658 us -> 118 us  [dot(): return jnp.dot(a, b, preferred_element_type=F32)]
    squeeze x289 -> x0, local copies, waits for them, and re-layouts: 245 us -> none  [the longest x256 213 us: segment_map(): lax.scan(turn, (identity, zero_state), (key_blocks, value_blocks, rate_bl...]
    pallas_call x0 -> x6, Pallas kernels: none -> 97.1 us  [the longest x1 32.3 us: body(): inv, uw, step_maps, seg_map = K['map'](key_rows, value_rows, rate_rows)]
    ppermute x14 -> x0, waiting for transfers between devices: 89.2 us -> none  [passed_along(): return lax.ppermute(shard, axis, pairs)]
    mul x96 -> x0, local copies, waits for them, and re-layouts: 65.6 us -> none  [the longest x64 43.8 us: step_matrix_of(): weighted_keys = key_aug * rate_block[..., None]]
    all_gather x2 -> x4, waiting for transfers between devices: 33.2 us -> 95.8 us  [the longest x1 34 us: body(): all_grads = lax.all_gather(seg_grad, 'seq', axis=0, tiled=False)]
    ppermute x14 -> x0, starting transfers between devices: 41.7 us -> none  [passed_along(): return lax.ppermute(shard, axis, pairs)]
    reduce_scatter x4, waiting for transfers between devices: 78.8 us -> 103 us  [the longest x1 33 us: body(): lax.psum_scatter(dot(hidden, mlp_down).astype(BF), 'head', scatter_dimens...]
  transfers between devices with their start and end apart: 23 -> 14, of which waited for: 21 -> 14; matrix products, arithmetic and copies ran while one was open for 3% -> 9% of each run, Pallas kernels for 0% -> 4%
where the time goes in v1:
time: 1420 us; the launch traced here: 1410 us
  waiting for transfers between devices  1020 us (72%)
  matrix products  118 us (8%)
  Pallas kernels  97.1 us (7%)
  blocking collectives  75.2 us (5%)
  other arithmetic  56.9 us (4%)
  local copies, waits for them, and re-layouts  26.3 us (2%)
  between operations  14.7 us (1%)
    psum x1, waiting for transfers between devices, body(): lax.psum((mlp_down_grad.astype(BF), mlp_gate_grad.astype(BF), mlp_up_grad...  482 us
    psum x1, waiting for transfers between devices, body(): late_sums = lax.psum(late_in, 'seq')  145 us
    dot_general x27, matrix products, dot(): return jnp.dot(a, b, preferred_element_type=F32)  118 us
    psum x1, waiting for transfers between devices, body(): mid_sums = lax.psum(mid_in[:2], 'seq')  104 us
    psum x1, waiting for transfers between devices, body(): lax.psum((rate_weight_part, rate_bias_part, scale_part, post_gain_part, p...  61.8 us
    psum x1, blocking collectives, body(): gain_grads = lax.psum((norm1_part, norm2_part), ('seq', 'head'))  42.9 us
    convert_element_type x8, other arithmetic, body(): up = lambda x: x.astype(F32)  38.2 us
    all_gather x1, waiting for transfers between devices, body(): all_grads = lax.all_gather(seg_grad, 'seq', axis=0, tiled=False)  34 us
  transfers between devices with their start and end apart: 14, of which 14 were waited for; matrix products, arithmetic and copies ran while one was open for 9% of the time, Pallas kernels for 4%

profile of v1, /device:TPU:0, one launch (start us, length us, event | category | flops | bytes accessed | tf_op | source)
XLA Modules:
  0.0 1409.2 jit_solution(8993058126788149740)
XLA Ops:
  8.6 2.0 fusion.28
  10.7 25.4 %all-gather.9.cloned.1.call-done = bf16[512,2048]{1,0:T(8,128)(2,1)} async-done(((bf16[128,2048]{1,0:T(8,128)(2,1)}), bf16[512,2048]{1,0:T(8,128)(2,1)}) %all-gather.9.cloned.1.call-update) | async-done | bytes 2097168 | tf_op jit(solution)/shard_map/all_gather | solution.py:301
  36.1 3.6 fusion.37.k_ref
  42.5 32.3 %segment_maps.1 = (bf16[8,4,128,128]{3,2,1,0:T(8,128)(2,1)S(1)}, bf16[8,512,256]{2,1,0:T(8,128)(2,1)S(1)}, bf16[8,4,128,256]{3,2,1,0:T(8,128)(2,1)}, bf16[9,80,128]{2,1,0:T(8,128)(2,1)}) custom-call(f32[512,512]{1,0:T(8,128)S(1)} %fusion.37.k_ref, f32[512,512]{1,0:T(8,128)S(1)} %fusion.38.v_ref, f32[512,8]{1,0:T(8,128)S(1)} %get-tuple-element.119.r_ref), custom_call_target="tpu_custom_call" | custom-call | tf_op jit(solution)/shard_map/segment_maps/pallas_call | solution.py:311
  77.1 3.5 fusion.39.q_ref
  80.6 8.2 local_parts.1
  92.7 28.1 %all-gather.17.cloned.1.call-done = bf16[72,80,128]{2,1,0:T(8,128)(2,1)} async-done(((bf16[9,80,128]{2,1,0:T(8,128)(2,1)}), bf16[72,80,128]{2,1,0:T(8,128)(2,1)}) %all-gather.17.cloned.1.call-update) | async-done | bytes 1474576 | tf_op jit(solution)/shard_map/all_gather | solution.py:312
  124.2 14.3 %forward_states.1 = (f32[512,512]{1,0:T(8,128)S(1)}, bf16[8,512,128]{2,1,0:T(8,128)(2,1)S(1)}, bf16[8,4,128,128]{3,2,1,0:T(8,128)(2,1)S(1)}) custom-call(s32[1]{0:T(128)} %bitcast.seg_ref, bf16[8,9,80,128]{3,2,1,0:T(8,128)(2,1)} %bitcast.60, bf16[8,9,80,128]{3,2,1,0:T(8,128)(2,1)} %bitcast.61, f32[8,64,64]{2,1,0:T(8,128)S(1)} %copy-done.28, ...), custom_call_target="tpu_custom_call" | custom-call | tf_op jit(solution)/shard_map/forward_states/pallas_call | solution.py:314
  140.7 5.9 all-reduce.3
  146.7 5.0 multiply_convert_fusion.3
  152.5 2.6 convolution_convert_fusion.8
  155.4 29.7 %reduce-scatter.5.cloned.1.call-done = bf16[128,2048]{1,0:T(8,128)(2,1)} async-done(((bf16[512,2048]{1,0:T(8,128)(2,1)}), bf16[128,2048]{1,0:T(8,128)(2,1)}) %reduce-scatter.5.cloned.1.call-update) | async-done | bytes 524304 | tf_op jit(solution)/shard_map/reduce_scatter | solution.py:325
  185.0 1.5 multiply_reduce_fusion.2
  186.5 2.2 multiply_convert_fusion.2
  189.4 22.1 %all-gather.11.cloned.1.call-done = bf16[512,2048]{1,0:T(8,128)(2,1)} async-done(((bf16[128,2048]{1,0:T(8,128)(2,1)}), bf16[512,2048]{1,0:T(8,128)(2,1)}) %all-gather.11.cloned.1.call-update) | async-done | bytes 2097168 | tf_op jit(solution)/shard_map/all_gather | solution.py:332
  211.5 8.1 fusion.41
  219.5 7.7 fusion.40
  227.2 8.3 all-gather.13.cloned.1.call-done
  235.6 10.3 multiply_convert_fusion
  245.9 6.6 fusion.42
  252.5 7.3 add_convert_fusion.1
  259.8 31.5 %reduce-scatter.9.cloned.1.call-done = bf16[128,2048]{1,0:T(8,128)(2,1)} async-done(((bf16[512,2048]{1,0:T(8,128)(2,1)}), bf16[128,2048]{1,0:T(8,128)(2,1)}) %reduce-scatter.9.cloned.1.call-update) | async-done | bytes 524304 | tf_op jit(solution)/shard_map/reduce_scatter | solution.py:351
  291.3 1.9 fusion.20
  293.2 2.8 fusion.34
  296.0 7.7 convolution_convert_fusion
  303.8 4.9 convolution_convert_fusion.1
  308.7 4.8 convolution_convert_fusion.2
  313.6 5.1 all-gather.15.cloned.1.call-done
  318.7 5.6 multiply_reduce_fusion
  324.3 6.3 all-reduce.2
  330.6 1.9 subtract_multiply_fusion.1.dz_ref
  333.8 6.3 state_grads.1
  342.7 9.1 query_grads.1
  351.9 2.7 convolution_convert_fusion.4
  354.6 2.6 convolution_convert_fusion.3
  357.2 482.3 %all-reduce.18.cloned.1.call-done = (bf16[1376,2048]{1,0:T(8,128)(2,1)}, bf16[2048,1376]{0,1:T(8,128)(2,1)}, bf16[2048,1376]{0,1:T(8,128)(2,1)}) async-done(((bf16[1376,2048]{1,0:T(8,128)(2,1)}, bf16[2048,1376]{0,1:T(8,128)(2,1)}, bf16[2048,1376]{0,1:T(8,128)(2,1)}), (bf16[1376,2048]{1,0:T(8,128)(2,1)}, bf16[2048,1376]{0,1:T(8,128)(2,1)}, bf16[2048,1376]{0,1:T(8,128)(2,1)})) %all-reduce.18.cloned.1.call-update) | async-done | bytes 16908304 | tf_op jit(solution)/shard_map/psum | solution.py:348
  839.5 5.0 fusion.46
  844.6 3.3 fusion.43
  847.9 34.0 %all-gather.19.cloned.1.call-done = f32[32,72,128]{2,1,0:T(8,128)} async-done(((f32[4,72,128]{2,1,0:T(8,128)}), f32[32,72,128]{2,1,0:T(8,128)}) %all-gather.19.cloned.1.call-update) | async-done | bytes 1179664 | tf_op jit(solution)/shard_map/all_gather | solution.py:376
  883.1 26.9 %key_grads.1 = (bf16[512,512]{1,0:T(8,128)(2,1)S(1)}, bf16[512,512]{1,0:T(8,128)(2,1)S(1)}, f32[512,8]{1,0:T(8,128)S(1)}, f32[8,72,128]{2,1,0:T(8,128)S(1)}) custom-call(s32[1]{0:T(128)} %bitcast.seg_ref, bf16[8,9,80,128]{3,2,1,0:T(8,128)(2,1)} %bitcast.62, bf16[8,9,80,128]{3,2,1,0:T(8,128)(2,1)} %bitcast.63, f32[8,4,72,128]{3,2,1,0:T(8,128)} %bitcast.66, ...), custom_call_target="tpu_custom_call" | custom-call | tf_op jit(solution)/shard_map/key_grads/pallas_call | solution.py:378
  915.7 2.4 add_convert_fusion
  919.5 7.3 convolution_convert_fusion.9
  927.9 4.4 convolution_convert_fusion.7
  932.2 2.6 convolution_convert_fusion.6
  934.9 2.6 convolution_convert_fusion.5
  937.5 104.0 %all-reduce.16.cloned.1.call-done = (bf16[512,2048]{1,0:T(8,128)(2,1)}, bf16[2048,512]{1,0:T(8,128)(2,1)}) async-done(((bf16[512,2048]{1,0:T(8,128)(2,1)}, bf16[2048,512]{1,0:T(8,128)(2,1)}), (bf16[512,2048]{1,0:T(8,128)(2,1)}, bf16[2048,512]{1,0:T(8,128)(2,1)})) %all-reduce.16.cloned.1.call-update) | async-done | bytes 4194320 | tf_op jit(solution)/shard_map/psum | solution.py:404
  1043.8 2.6 fusion.47
  1046.5 20.1 %all-reduce.1 = (f32[8]{0:T(128)}, f32[8]{0:T(128)}, f32[512]{0:T(512)}, f32[512]{0:T(512)}) all-reduce(f32[8]{0:T(128)S(1)} %get-tuple-element.107, f32[8]{0:T(128)S(1)} %get-tuple-element.116, f32[512]{0:T(512)S(1)} %get-tuple-element.79, f32[512]{0:T(512)S(1)} %get-tuple-element.86), channel_id=1, replica_groups=mesh['seq'=8,'head'=4] {'seq'}, use_global_device_ids=true, to_apply=%region_28.29 | all-reduce | flops 1040 | bytes 8320 | tf_op jit(solution)/shard_map/psum | solution.py:408
  1066.6 8.6 reduce-scatter.11.cloned.1.call-done
  1075.3 1.5 fusion.30
  1076.7 33.0 %reduce-scatter.7.cloned.1.call-done = bf16[128,2048]{1,0:T(8,128)(2,1)} async-done(((bf16[512,2048]{1,0:T(8,128)(2,1)}), bf16[128,2048]{1,0:T(8,128)(2,1)}) %reduce-scatter.7.cloned.1.call-update) | async-done | bytes 524304 | tf_op jit(solution)/shard_map/reduce_scatter | solution.py:337
  1109.7 3.2 fusion.16
  1112.9 42.9 %all-reduce = (f32[2048]{0:T(1024)}, f32[2048]{0:T(1024)}) all-reduce(f32[2048]{0:T(1024)S(1)} %get-tuple-element.84, f32[2048]{0:T(1024)S(1)} %get-tuple-element.81), channel_id=1, replica_groups=mesh['seq'=8,'head'=4] {'seq','head'}, use_global_device_ids=true, to_apply=%region_17.18 | all-reduce | flops 4096 | bytes 32768 | tf_op jit(solution)/shard_map/psum | solution.py:411
  1155.7 8.9 convert_element_type.145
  1164.6 8.7 convert_element_type.146
  1173.3 5.9 convert_element_type.147
  1179.3 2.6 convert_element_type.142
  1181.9 2.5 convert_element_type.144
  1184.4 145.2 %all-reduce.14.cloned.1.call-done = (bf16[2048,512]{1,0:T(8,128)(2,1)}, bf16[2048,512]{1,0:T(8,128)(2,1)}, bf16[2048,512]{1,0:T(8,128)(2,1)}) async-done(((bf16[2048,512]{1,0:T(8,128)(2,1)}, bf16[2048,512]{1,0:T(8,128)(2,1)}, bf16[2048,512]{1,0:T(8,128)(2,1)}), (bf16[2048,512]{1,0:T(8,128)(2,1)}, bf16[2048,512]{1,0:T(8,128)(2,1)}, bf16[2048,512]{1,0:T(8,128)(2,1)})) %all-reduce.14.cloned.1.call-update) | async-done | bytes 6291472 | tf_op jit(solution)/shard_map/psum | solution.py:407
  1329.6 4.3 convert_element_type.139
  1333.9 2.6 convert_element_type.140
  1336.6 2.6 convert_element_type.141
  1339.2 61.8 %all-reduce.12.cloned.1.call-done = f32[2048,8]{0,1:T(8,128)} async-done(((f32[2048,8]{0,1:T(8,128)}), f32[2048,8]{0,1:T(8,128)}) %all-reduce.12.cloned.1.call-update) | async-done | bytes 65552 | tf_op jit(solution)/shard_map/psum | solution.py:408
  1400.9 1.5 copy.50
  (186 shorter events, 33.4 us)
Async XLA Ops:
  7.2 145.3 %copy-start = (bf16[512,2048]{1,0:T(8,128)(2,1)S(1)}, bf16[512,2048]{1,0:T(8,128)(2,1)}, u32[]{:S(2)}) copy-start(bf16[512,2048]{1,0:T(8,128)(2,1)} %param.32) | copy-start | bytes 6291460
  7.2 28.9 %all-gather.9.cloned.1.call-start = ((), (), s32[]{:S(2)}) async-start(), calls=%async_computation.4 | async-start | bytes 2621440 | tf_op jit(solution)/shard_map/all_gather | solution.py:301
  10.7 110.1 %all-gather.17.cloned.1.call-start = ((), (), s32[]{:S(2)}) async-start(), calls=%async_computation.13 | async-start | bytes 1658880 | tf_op jit(solution)/shard_map/all_gather | solution.py:312
  36.1 3.6 copy-start.43
  36.1 3.6 copy-start.47
  39.8 2.7 copy-start.2
  77.1 107.9 %reduce-scatter.5.cloned.1.call-start = ((), (), s32[]{:S(2)}) async-start(), calls=%async_computation.5 | async-start | bytes 2621440 | tf_op jit(solution)/shard_map/reduce_scatter | solution.py:325
  80.6 8.2 copy-start.7
  80.6 40.2 %copy-start.31 = (f32[8,64]{1,0:T(8,128)S(1)}, f32[8,64]{1,0:T(8,128)}, u32[]{:S(2)}) copy-start(f32[8,64]{1,0:T(8,128)} %param.29) | copy-start | bytes 6148
  124.2 22.5 %copy-start.55 = (f32[512]{0:T(512)S(1)}, f32[512]{0:T(512)}, u32[]{:S(2)}) copy-start(f32[512]{0:T(512)} %param.30) | copy-start | bytes 6148
  124.2 22.5 %copy-start.61 = (f32[512]{0:T(512)S(1)}, f32[512]{0:T(512)}, u32[]{:S(2)}) copy-start(f32[512]{0:T(512)} %param.31) | copy-start | bytes 6148
  155.1 31.4 %copy-start.52 = (f32[2048]{0:T(1024)S(1)}, f32[2048]{0:T(1024)}, u32[]{:S(2)}) copy-start(f32[2048]{0:T(1024)} %param.33) | copy-start | bytes 24580
  155.1 56.3 %all-gather.11.cloned.1.call-start = ((), (), s32[]{:S(2)}) async-start(), calls=%async_computation.6 | async-start | bytes 2621440 | tf_op jit(solution)/shard_map/all_gather | solution.py:332
  188.7 46.9 %all-gather.13.cloned.1.call-start = ((), (), s32[]{:S(2)}) async-start(), calls=%async_computation.8 | async-start | bytes 2621440 | tf_op jit(solution)/shard_map/all_gather | solution.py:302
  189.3 102.0 %reduce-scatter.9.cloned.1.call-start = ((), (), s32[]{:S(2)}) async-start(), calls=%async_computation.9 | async-start | bytes 2621440 | tf_op jit(solution)/shard_map/reduce_scatter | solution.py:351
  211.5 8.1 copy-start.58
  245.8 6.6 copy-start.63
  245.9 6.6 copy-start.38
  259.7 59.0 %all-gather.15.cloned.1.call-start = ((), (), s32[]{:S(2)}) async-start(), calls=%async_computation.10 | async-start | bytes 2621440 | tf_op jit(solution)/shard_map/all_gather | solution.py:363
  296.0 543.5 %all-reduce.18.cloned.1.call-start = ((), (), s32[]{:S(2)}) async-start(), calls=%async_computation.17 | async-start | bytes 33816576 | tf_op jit(solution)/shard_map/psum | solution.py:348
  296.0 7.8 copy-start.59
  296.0 7.8 copy-start.64
  303.8 4.9 copy-start.60
  303.8 4.9 copy-start.67
  313.5 568.3 %all-gather.19.cloned.1.call-start = ((), (), s32[]{:S(2)}) async-start(), calls=%async_computation.14 | async-start | bytes 1327104 | tf_op jit(solution)/shard_map/all_gather | solution.py:376
  333.8 7.7 copy-start.3
  341.4 700.1 %all-reduce.16.cloned.1.call-start = ((), (), s32[]{:S(2)}) async-start(), calls=%async_computation.16 | async-start | bytes 8388608 | tf_op jit(solution)/shard_map/psum | solution.py:404
  342.7 9.2 copy-start.57
  342.7 9.2 copy-start.66
  351.8 2.7 copy-start.14
  351.9 2.7 copy-start.24
  351.9 2.7 copy-start.44
  351.9 2.7 copy-start.50
  839.5 235.8 %reduce-scatter.11.cloned.1.call-start = ((), (), s32[]{:S(2)}) async-start(), calls=%async_computation.11 | async-start | bytes 2621440 | tf_op jit(solution)/shard_map/reduce_scatter | solution.py:394
  839.5 5.1 copy-start.15
  839.5 5.1 copy-start.46
  844.6 37.3 %copy-start.6 = (bf16[8,4,128,128]{3,2,1,0:T(8,128)(2,1)S(1)}, bf16[8,4,128,128]{3,2,1,0:T(8,128)(2,1)}, u32[]{:S(2)}) copy-start(bf16[8,4,128,128]{3,2,1,0:T(8,128)(2,1)} %copy-done.5) | copy-start | bytes 3145732
  883.1 27.0 %copy-start.51 = (f32[512,8]{1,0:T(8,128)S(1)}, f32[512,8]{1,0:T(8,128)}, u32[]{:S(2)}) copy-start(f32[512,8]{1,0:T(8,128)} %get-tuple-element.120) | copy-start | bytes 49156
  883.1 27.1 %copy-start.48 = (bf16[2048,512]{1,0:T(8,128)(2,1)S(1)}, bf16[2048,512]{1,0:T(8,128)(2,1)}, u32[]{:S(2)}) copy-start(bf16[2048,512]{1,0:T(8,128)(2,1)} %param.23) | copy-start | bytes 6291460
  910.0 1.5 copy-start.17
  910.0 1.5 copy-start.29
  910.1 1.5 copy-start.19
  910.2 1.9 copy-start.49
  912.1 2.3 copy-start.33
  912.1 3.6 copy-start.34
  918.1 1.4 copy-start.68
  918.2 191.5 %reduce-scatter.7.cloned.1.call-start = ((), (), s32[]{:S(2)}) async-start(), calls=%async_computation.7 | async-start | bytes 2621440 | tf_op jit(solution)/shard_map/reduce_scatter | solution.py:337
  926.8 5.4 copy-start.20
  926.8 402.7 %all-reduce.14.cloned.1.call-start = ((), (), s32[]{:S(2)}) async-start(), calls=%async_computation.15 | async-start | bytes 12582912 | tf_op jit(solution)/shard_map/psum | solution.py:407
  927.8 4.4 copy-start.45
  932.2 2.6 copy-start.18
  1041.5 33.7 %copy-start.32 = (bf16[128,2048]{1,0:T(8,128)(2,1)S(1)}, bf16[128,2048]{1,0:T(8,128)(2,1)}, u32[]{:S(2)}) copy-start(bf16[128,2048]{1,0:T(8,128)(2,1)} %param.19) | copy-start | bytes 1572868
  1041.6 33.7 %copy-start.53 = (f32[2048]{0:T(1024)S(1)}, f32[2048]{0:T(1024)}, u32[]{:S(2)}) copy-start(f32[2048]{0:T(1024)} %param.20) | copy-start | bytes 24580
  1041.6 68.1 %copy-start.35 = (bf16[128,2048]{1,0:T(8,128)(2,1)S(1)}, bf16[128,2048]{1,0:T(8,128)(2,1)}, u32[]{:S(2)}) copy-start(bf16[128,2048]{1,0:T(8,128)(2,1)} %reduce-scatter.5.cloned.1.call-done) | copy-start | bytes 1572868
  1041.6 68.1 %copy-start.36 = (bf16[128,2048]{1,0:T(8,128)(2,1)S(1)}, bf16[128,2048]{1,0:T(8,128)(2,1)}, u32[]{:S(2)}) copy-start(bf16[128,2048]{1,0:T(8,128)(2,1)} %param.37) | copy-start | bytes 1572868
  1041.6 68.1 %copy-start.37 = (bf16[128,2048]{1,0:T(8,128)(2,1)S(1)}, bf16[128,2048]{1,0:T(8,128)(2,1)}, u32[]{:S(2)}) copy-start(bf16[128,2048]{1,0:T(8,128)(2,1)} %reduce-scatter.9.cloned.1.call-done) | copy-start | bytes 1572868
  1041.6 359.3 %all-reduce.12.cloned.1.call-start = ((), (), s32[]{:S(2)}) async-start(), calls=%async_computation.12 | async-start | bytes 131072 | tf_op jit(solution)/shard_map/psum | solution.py:408
  1155.7 17.6 %slice-start = ((s8[5636096]{0:T(1024)(128)(4,1)}), s8[4194304]{0:T(1024)(128)(4,1)S(1)}, s32[]{:S(2)}) async-start(s8[5636096]{0:T(1024)(128)(4,1)} %bitcast.64), calls=%async_computation.18 | async-start | bytes 8388608
  1164.6 8.7 slice-start.1
  1173.3 5.9 copy-start.40
  1179.3 2.6 copy-start.39
  1329.6 4.4 copy-start.42
  1333.9 2.6 copy-start.41
  1336.6 65.9 %copy-start.1 = (bf16[512,2048]{1,0:T(8,128)(2,1)S(1)}, bf16[512,2048]{1,0:T(8,128)(2,1)}, u32[]{:S(2)}) copy-start(bf16[512,2048]{1,0:T(8,128)(2,1)} %param.32) | copy-start | bytes 6291460
  (21 other events, 23.3 us)
Sparse Core Ops, SparseCore 0:
  10.8 25.2 all-gather.8
  77.2 43.5 all-gather.16
  155.3 29.7 reduce-scatter.4
  188.8 22.5 all-gather.10
  213.0 22.5 all-gather.12
  259.9 31.4 reduce-scatter.8
  296.1 22.5 all-gather.14
  324.0 515.4 all-reduce.17
  841.9 39.9 all-gather.18
  885.9 155.5 all-reduce.15
  1044.8 30.4 reduce-scatter.10
  1078.2 31.4 reduce-scatter.6
  1115.1 214.4 all-reduce.13
  1333.4 67.4 all-reduce.11

commit v2 on v1

--- a/solution.py
+++ b/solution.py
@@ -123,7 +123,8 @@
         h=2*p+odd
         s=start_of(is_ref,ib_ref,odd)
         for j in range(segs-1):
-            a,o=unpack(y_ref[j,odd],yb_ref[j,0],h)
+            at=seg_ref[1+j]
+            a,o=unpack(y_ref[at,odd],yb_ref[at,0],h)
             s=s+jnp.where(j<seg,1.0,0.0)*(nn(a,s)+o)
         for c in range(N//C):
             sl=pl.ds(c*C,C)
@@ -150,7 +151,7 @@
             d_ref[odd,c]=d
             g=g+tn(x_ref[odd,c][:,:LN],g)+d
         outs.append(g)
-    dseg_ref[0]=pair(outs[0],outs[1])[:72]
+    dseg_ref[0]=pair(outs[0],outs[1])[:80].astype(BF)
 
 def query_grad_kernel(C,q_ref,k_ref,r_ref,dz_ref,e_ref,s_ref,pt_ref,dq_ref,b_ref,l_ref):
     p=pl.program_id(0)
@@ -170,14 +171,14 @@
             l_ref[odd,sl,:]=-tn(pt_ref[odd,c],dzb)
         dq_ref[sl,:]=pair(outs[0],outs[1]).astype(BF)
 
-def key_grad_kernel(C,seg_ref,y_ref,yb_ref,da_ref,k_ref,r_ref,e_ref,s_ref,vv_ref,b_ref,l_ref,x_ref,d_ref,dk_ref,dv_ref,dr_ref,gi_ref):
+def key_grad_kernel(C,seg_ref,y_ref,yb_ref,da_ref,k_ref,r_ref,e_ref,s_ref,vv_ref,b_ref,l_ref,x_ref,d_ref,dq_ref,dg_ref,dk_ref,dv_ref,dr_ref,gi_ref,pk_ref):
     p=pl.program_id(0)
     N=k_ref.shape[0]
     segs=y_ref.shape[0]
     seg=seg_ref[0]
     @pl.when(p==0)
     def _(): dr_ref[...]=jnp.zeros_like(dr_ref)
-    pad=jnp.zeros((LN-72,LN),F32)
+    pad=jnp.zeros((LN-80,LN),F32)
     dks=[[None]*(N//C) for _ in range(2)]
     lams=[[None]*(N//C) for _ in range(2)]
     for odd in range(2):
@@ -185,8 +186,9 @@
         full=jnp.zeros((LN,LN),F32)
         g=jnp.zeros((LN,LN),F32)
         for j in reversed(range(segs)):
-            a,_=unpack(y_ref[j,odd],yb_ref[j,0],h)
-            d=jnp.concatenate([head_of(da_ref[j,0],odd),pad],0)
+            at=seg_ref[1+j]
+            a,_=unpack(y_ref[at,odd],yb_ref[at,0],h)
+            d=jnp.concatenate([head_of(da_ref[at,0].astype(F32),odd),pad],0)
             full=full+tn(a,full)+d
             g=jnp.where(j==seg+1,full,g)
         gi_ref[odd]=full[:72]
@@ -210,6 +212,10 @@
         sl=pl.ds(c*C,C)
         dk_ref[sl,:]=pair(dks[0][c],dks[1][c]).astype(BF)
         dv_ref[sl,:]=-pair(lams[0][c],lams[1][c]).astype(BF)
+        dq=dq_ref[sl,:].astype(F32); dg=dg_ref[sl,:].astype(F32)
+        for odd in range(2):
+            first=pair(head_of(dq,odd),dks[odd][c]); second=pair(-lams[odd][c],head_of(dg,odd))
+            pk_ref[odd,sl,:]=jnp.concatenate([first,second],axis=1).astype(BF)
 
 def params(): return pltpu.CompilerParams(dimension_semantics=("arbitrary",),vmem_limit_bytes=VL)
 def S(shape,dt): return jax.ShapeDtypeStruct(shape,dt)
@@ -238,30 +244,228 @@
         out_specs=[sp["n128"],sp["row"],sp["cc"],sp["n128"]],
         out_shape=[S((hl,N,LN),BF),S((N,w),F32),S((hl,nc,C,C),BF),S((hl,N,LN),BF)],compiler_params=params(),name="local_parts")
     yall=pl.BlockSpec((segs,2,80,LN),lambda p,*_:(0,p,0,0)); yball=pl.BlockSpec((segs,1,80,LN),lambda p,*_:(0,hl,0,0))
-    dall=pl.BlockSpec((segs,1,72,LN),lambda p,*_:(0,p,0,0))
+    dall=pl.BlockSpec((segs,1,80,LN),lambda p,*_:(0,p,0,0))
     ist=pl.BlockSpec((2,HW,HW),lambda p,*_:(p,0,0)); ibs=pl.BlockSpec((2,1,HW),lambda p,*_:(p,0,0))
     def gs(i,o): return pltpu.PrefetchScalarGridSpec(num_scalar_prefetch=1,grid=G,in_specs=i,out_specs=o)
     K["forward"]=pl.pallas_call(functools.partial(forward_kernel,C),grid_spec=gs([yall,yball,ist,ibs,sp["x"],sp["n256"],sp["n128"],sp["row"]],[sp["row"],sp["n128"],sp["s"]]),
         out_shape=[S((N,w),F32),S((hl,N,LN),BF),S((hl,nc,LN,LN),BF)],compiler_params=params(),name="forward_states")
     K["sgrad"]=pl.pallas_call(functools.partial(state_grad_kernel,C),grid=G,in_specs=[sp["row"],sp["n128"],sp["x"]],
-        out_specs=[sp["s"],pl.BlockSpec((1,72,LN),lambda p:(p,0,0))],out_shape=[S((hl,nc,LN,LN),F32),S((hl//2,72,LN),F32)],compiler_params=params(),name="state_grads")
+        out_specs=[sp["s"],pl.BlockSpec((1,80,LN),lambda p:(p,0,0))],out_shape=[S((hl,nc,LN,LN),F32),S((hl//2,80,LN),BF)],compiler_params=params(),name="state_grads")
     K["qgrad"]=pl.pallas_call(functools.partial(query_grad_kernel,C),grid=G,in_specs=[sp["row"],sp["row"],sp["rate"],sp["row"],sp["n128"],sp["s"],sp["cc"]],
         out_specs=[sp["row"],sp["n128"],sp["n128"]],out_shape=[S((N,w),BF),S((hl,N,LN),BF),S((hl,N,LN),F32)],compiler_params=params(),name="query_grads")
-    K["kgrad"]=pl.pallas_call(functools.partial(key_grad_kernel,C),grid_spec=gs([yall,yball,dall,sp["row"],sp["rate"],sp["n128"],sp["s"],sp["n128"],sp["n128"],sp["n128"],sp["x"],sp["s"]],
-        [sp["row"],sp["row"],sp["rate"],pl.BlockSpec((2,72,LN),lambda p,*_:(p,0,0))]),
-        out_shape=[S((N,w),BF),S((N,w),BF),S((N,hl),F32),S((hl,72,LN),F32)],compiler_params=params(),name="key_grads")
+    K["kgrad"]=pl.pallas_call(functools.partial(key_grad_kernel,C),grid_spec=gs([yall,yball,dall,sp["row"],sp["rate"],sp["n128"],sp["s"],sp["n128"],sp["n128"],sp["n128"],sp["x"],sp["s"],sp["row"],sp["row"]],
+        [sp["row"],sp["row"],sp["rate"],pl.BlockSpec((2,72,LN),lambda p,*_:(p,0,0)),sp["n256"]]),
+        out_shape=[S((N,w),BF),S((N,w),BF),S((N,hl),F32),S((hl,72,LN),F32),S((hl,N,2*LN),BF)],compiler_params=params(),name="key_grads")
     return K
 
 
 EPSILON = 1e-06
+
+
+def grid_of():
+    seq = lax.axis_size("seq")
+    x = max(lax.axis_size("head") // 2, 1)
+    if seq % x:
+        x = 1
+    return seq // x, x
+
+
+def shift(v, dz, dx):
+    Z, X = grid_of()
+    pairs = [(z * X + x, ((z + dz) % Z) * X + (x + dx) % X) for z in range(Z) for x in range(X)]
+    return lax.ppermute(v, "seq", pairs)
+
+
+def seq_gather(v):
+    Z, X = grid_of()
+    i = lax.axis_index("seq")
+    j = jnp.arange(Z * X, dtype=jnp.int32)
+    if (Z, X) != (4, 2):
+        return lax.all_gather(v, "seq", axis=0, tiled=False), j
+    both = jnp.stack([v, shift(v, 0, 1)])
+    left = shift(both, 1, 0)
+    right = shift(both, 3, 0)
+    far0 = shift(left[:1], 1, 0)
+    far1 = shift(right[1:], 3, 0)
+    z, x = i // X, i % X
+    order = ((j // X - z) % Z) * X + (j % X - x) % X
+    return jnp.concatenate([both, right, far0, far1, left]), order
+
+
+def head_shift(v, dy, dc):
+    H = lax.axis_size("head")
+    Y = H // 2
+    pairs = [(y * 2 + c, ((y + dy) % Y) * 2 + (c + dc) % 2) for y in range(Y) for c in range(2)]
+    return lax.ppermute(v, "head", pairs)
+
+
+def head_gather(v):
+    H = lax.axis_size("head")
+    if H != 4:
+        return lax.all_gather(v, "head", axis=0, tiled=True)
+    i = lax.axis_index("head")
+    y, c = i // 2, i % 2
+    mine = jnp.stack([v, head_shift(v, 1, 0)])
+    other = head_shift(mine, 0, 1)
+    a = jnp.where(c == 0, mine, other)
+    b = jnp.where(c == 0, other, mine)
+    rows = [jnp.where(y == 0, a[0], a[1]), jnp.where(y == 0, b[0], b[1])]
+    rows += [jnp.where(y == 0, a[1], a[0]), jnp.where(y == 0, b[1], b[0])]
+    return jnp.concatenate(rows, axis=0)
+
+
+def head_scatter(v):
+    H = lax.axis_size("head")
+    v = v.astype(BF)
+    if H != 4:
+        return lax.psum_scatter(v, "head", scatter_dimension=0, tiled=True).astype(F32)
+    i = lax.axis_index("head")
+    y, c = i // 2, i % 2
+    v = v.reshape(2, 2, v.shape[0] // 4, v.shape[1])
+    got = head_shift(jnp.where(c == 0, v[:, 1], v[:, 0]), 0, 1)
+    half = (jnp.where(c == 0, v[:, 0], v[:, 1]).astype(F32) + got.astype(F32)).astype(BF)
+    back = head_shift(jnp.where(y == 0, half[1], half[0]), 1, 0)
+    return jnp.where(y == 0, half[0], half[1]).astype(F32) + back.astype(F32)
 
 
 def gelu_tanh(values):
     return jax.nn.gelu(values, approximate=True)
 
 
-def dot(a, b):
-    return jnp.dot(a, b, preferred_element_type=F32)
+def dot(a, b, ca=1, cb=0):
+    return lax.dot_general(a, b, (((ca,), (cb,)), ((), ())), preferred_element_type=F32)
+
+
+def at(v, i, axis=0):
+    return lax.dynamic_index_in_dim(v, i, axis, keepdims=False)
+
+
+def plus(a, b):
+    return (a.astype(F32) + b.astype(F32)).astype(BF)
+
+
+def pair_reduce(v):
+    x = lax.axis_index("seq") % 2
+    return plus(at(v, x, 1), shift(at(v, 1 - x, 1), 0, 1))
+
+
+def ring_start(v):
+    z = lax.axis_index("seq") // 2
+    v = v.reshape((4, -1) + v.shape[1:])
+    if v.shape[1] == 1:
+        h = v.shape[2] // 32 * 16
+        top, low = v[:, 0, :h], v[:, 0, h:]
+    else:
+        top, low = v[:, 0], v[:, 1]
+    a = shift(at(top, (z + 2) % 4), 1, 0)
+    b = shift(at(low, (z + 2) % 4), 3, 0)
+    return top, low, a, b
+
+
+def ring_end(state, parts):
+    top, low, a, b = state
+    z = lax.axis_index("seq") // 2
+    join = jnp.stack if parts == 2 else lambda p: jnp.concatenate(p, axis=0)
+    up = join([plus(at(top, (z + 1) % 4), a), at(low, (z + 1) % 4)])
+    down = join([at(top, (z + 3) % 4), plus(at(low, (z + 3) % 4), b)])
+    got = shift(up, 1, 0).astype(F32) + shift(down, 3, 0).astype(F32)
+    return (join([at(top, z), at(low, z)]).astype(F32) + got).astype(BF)
+
+
+def split_columns(D):
+    return D * 7 // 16 // LN * LN
+
+
+def result_gather(vc, vd):
+    Z, X = grid_of()
+    i = lax.axis_index("seq")
+    z, x = i // X, i % X
+    h = vc.shape[0] // 32 * 16
+    left, right = shift(vc, 1, 0), shift(vc, 3, 0)
+    both = jnp.stack([vd, shift(vd, 0, 1)])
+    far = jnp.concatenate([shift(left[:h], 1, 0), shift(right[h:], 3, 0)], axis=0)
+    mine = jnp.stack([vc, right, far, left])
+    dl, dr = shift(both, 1, 0), shift(both, 3, 0)
+    other = shift(mine, 0, 1)
+    f0, f1 = shift(dl[:1], 1, 0), shift(dr[1:], 3, 0)
+    k = jnp.arange(4, dtype=jnp.int32)
+    zs = (z + k) % 4
+    at_c = jnp.concatenate([zs * 2 + x, zs * 2 + 1 - x])
+    at_d = jnp.stack([zs * 2 + x, zs * 2 + 1 - x], axis=1).reshape(8)
+    return [mine, other], [both, dr, f0, f1, dl], jnp.concatenate([at_c, at_d]).astype(jnp.int32)
+
+
+def pieces_of(refs):
+    return [(ref, k) for ref in refs for k in range(ref.shape[0])]
+
+
+def finish_kernel(nc, nd, plan, at_ref, *refs):
+    i = pl.program_id(0)
+    outs, scratch = refs[nc + nd : -1], refs[-1]
+
+    def write(group, base):
+        for out, (first, rows, turned) in zip(outs, plan):
+            for slot, (ref, k) in enumerate(pieces_of(group)):
+                start = pl.multiple_of(at_ref[base + slot] * rows, 16)
+                scratch[pl.ds(start, rows), :] = ref[k, pl.ds(first, rows), :].astype(F32)
+            if turned:
+                out[...] = scratch[pl.ds(0, out.shape[1]), :].T
+            else:
+                out[...] = scratch[pl.ds(0, out.shape[0]), :]
+
+    split = pl.num_programs(0) * 7 // 16
+
+    @pl.when(i < split)
+    def _():
+        write(refs[:nc], 0)
+
+    @pl.when(i >= split)
+    def _():
+        write(refs[nc : nc + nd], 8)
+
+
+def finish(gathered, plan, widths):
+    group_c, group_d, slots = gathered
+    D = group_c[0].shape[2] + group_d[0].shape[2]
+    rc, rd = group_c[0].shape[1], group_d[0].shape[1]
+    split = group_c[0].shape[2] // LN
+    in_specs = [
+        pl.BlockSpec((g.shape[0], rc, LN), lambda i, o: (0, 0, jnp.minimum(i, split - 1)))
+        for g in group_c
+    ] + [
+        pl.BlockSpec((g.shape[0], rd, LN), lambda i, o: (0, 0, jnp.maximum(i - split, 0)))
+        for g in group_d
+    ]
+    out_specs, out_shape = [], []
+    for w, (_, _, turned) in zip(widths, plan):
+        if turned:
+            out_specs.append(pl.BlockSpec((LN, w), lambda i, o: (i, 0)))
+            out_shape.append(jax.ShapeDtypeStruct((D, w), F32))
+        else:
+            out_specs.append(pl.BlockSpec((w, LN), lambda i, o: (0, i)))
+            out_shape.append(jax.ShapeDtypeStruct((w, D), F32))
+    return pl.pallas_call(
+        functools.partial(finish_kernel, len(group_c), len(group_d), plan),
+        grid_spec=pltpu.PrefetchScalarGridSpec(
+            num_scalar_prefetch=1,
+            grid=(D // LN,),
+            in_specs=in_specs,
+            out_specs=out_specs,
+            scratch_shapes=[pltpu.VMEM((8 * max(p[1] for p in plan), LN), F32)],
+        ),
+        out_shape=out_shape,
+        compiler_params=params(),
+        name="finish",
+    )(slots, *group_c, *group_d)
+
+
+def halves(v):
+    hi = v.astype(BF)
+    return jnp.stack([hi, (v - hi.astype(F32)).astype(BF)])
+
+
+def together(*values):
+    return lax.optimization_barrier(values)
 
 
 def body(
@@ -286,33 +490,37 @@
     out_cotangent,
 ):
     local_heads = init_state.shape[0]
-    head_width = init_state.shape[1]
     model_width = block_input.shape[1]
-    seq_index = lax.axis_index("seq")
+    width = mlp_gate.shape[1]
     segs = lax.axis_size("seq")
-    tokens = block_input.shape[0] * lax.axis_size("head")
+    heads = lax.axis_size("head")
+    tokens = block_input.shape[0] * heads
     K = build(tokens, local_heads, segs, CHUNK)
-    seg = seq_index.astype(jnp.int32).reshape(1)
+    seg = lax.axis_index("seq").astype(jnp.int32).reshape(1)
+    wide = local_heads == segs and tokens * segs * model_width <= 1 << 23 and grid_of() == (4, 2)
+    everywhere = ("seq", "head")
 
     input_f32 = block_input.astype(F32)
     scale_in = lax.rsqrt(jnp.mean(input_f32 * input_f32, axis=-1, keepdims=True) + EPSILON)
     unit_in = input_f32 * scale_in
     normed = (unit_in * norm1_gain).astype(BF)
-    group_in = lax.all_gather(normed, "head", axis=0, tiled=True)
-    group_cot = lax.all_gather(out_cotangent, "head", axis=0, tiled=True)
-    query_rows = dot(group_in, query_weight)
+    group_in = head_gather(normed)
+    group_cot = head_gather(out_cotangent)
+    if wide:
+        normed_all = lax.all_gather(normed, everywhere, axis=0, tiled=True)
     key_rows = dot(group_in, key_weight)
     value_rows = dot(group_in, value_weight)
-    gate_pre = dot(group_in, gate_weight)
     rate_pre = dot(group_in, rate_weight) + rate_bias
     rate_sig = jax.nn.sigmoid(rate_pre)
     rate_rows = rate_sig * rate_scale
-
     inv, uw, step_maps, seg_map = K["map"](key_rows, value_rows, rate_rows)
-    all_maps = lax.all_gather(seg_map, "seq", axis=0, tiled=False)
+    all_maps, order = seq_gather(seg_map)
+    place = jnp.concatenate([seg, order])
+    query_rows = dot(group_in, query_weight)
+    gate_pre = dot(group_in, gate_weight)
     q_eff, z_off, pt, vv = K["local"](query_rows, key_rows, rate_rows, inv, uw)
     z_rows, errors, states = K["forward"](
-        seg, all_maps, all_maps, init_state, init_bias[:, None, :], step_maps, uw, q_eff, z_off
+        place, all_maps, all_maps, init_state, init_bias[:, None, :], step_maps, uw, q_eff, z_off
     )
     stat_sums = lax.psum((jnp.sum(z_rows, axis=-1), jnp.sum(z_rows * z_rows, axis=-1)), "head")
     row_mean = stat_sums[0] / model_width
@@ -322,47 +530,45 @@
     post_out = z_hat * post_gain + post_bias
     gate_act, gelu_back = jax.vjp(gelu_tanh, gate_pre)
     gated_out = (gate_act * post_out).astype(BF)
-    attn_out = lax.psum_scatter(
-        dot(gated_out, out_weight).astype(BF), "head", scatter_dimension=0, tiled=True
-    ).astype(F32)
-    middle = input_f32 + attn_out
+    middle = input_f32 + head_scatter(dot(gated_out, out_weight))
     scale_mid = lax.rsqrt(jnp.mean(middle * middle, axis=-1, keepdims=True) + EPSILON)
     unit_mid = middle * scale_mid
     mlp_input = (unit_mid * norm2_gain).astype(BF)
-    mlp_group = lax.all_gather(mlp_input, "head", axis=0, tiled=True)
-    gate_mlp = dot(mlp_group, mlp_gate)
-    up_mlp = dot(mlp_group, mlp_up)
+    mlp_group = head_gather(mlp_input)
+    gate_mlp = dot(mlp_gate, mlp_group, 0, 1)
+    up_mlp = dot(mlp_up, mlp_group, 0, 1)
     silu_gate, silu_back = jax.vjp(jax.nn.silu, gate_mlp)
     hidden = (silu_gate * up_mlp).astype(BF)
-    mlp_out = lax.psum_scatter(
-        dot(hidden, mlp_down).astype(BF), "head", scatter_dimension=0, tiled=True
-    ).astype(F32)
-    block_out = (middle + mlp_out).astype(BF)
-    cot_f32 = out_cotangent.astype(F32)
-    d_hidden = dot(group_cot, mlp_down.T)
-    mlp_down_grad = dot(hidden.T, group_cot)
+    d_hidden = dot(mlp_down, group_cot, 1, 1)
     d_gate_mlp = silu_back(d_hidden * up_mlp)[0].astype(BF)
     d_up_mlp = (d_hidden * silu_gate).astype(BF)
-    mlp_gate_grad = dot(mlp_group.T, d_gate_mlp)
-    mlp_up_grad = dot(mlp_group.T, d_up_mlp)
-    mlp_sums = lax.psum(
-        (mlp_down_grad.astype(BF), mlp_gate_grad.astype(BF), mlp_up_grad.astype(BF)), "seq"
-    )
-    d_mlp_input = lax.psum_scatter(
-        (dot(d_gate_mlp, mlp_gate.T) + dot(d_up_mlp, mlp_up.T)).astype(BF),
-        "head",
-        scatter_dimension=0,
-        tiled=True,
-    ).astype(F32)
+    if wide:
+        rows = -(-width // (16 * segs)) * 16
+        fit = lambda v: jnp.pad(v, ((0, rows * segs - width), (0, 0))).reshape(segs, rows, tokens)
+        by_shard = lambda v: v.reshape(segs, -1, v.shape[1])
+        both = jnp.concatenate([fit(d_gate_mlp), fit(d_up_mlp)], axis=1).reshape(-1, tokens)
+        last = fit(hidden).reshape(-1, tokens)
+        c = split_columns(model_width)
+        parts = [
+            jnp.concatenate(
+                [by_shard(dot(both, mlp_group[:, s]).astype(BF)), by_shard(dot(last, group_cot[:, s]).astype(BF))],
+                axis=1,
+            )
+            for s in (slice(0, c), slice(c, None))
+        ]
+        d_gate_mlp, parts[0] = together(d_gate_mlp, parts[0])
+        cross = pair_reduce(parts[0].reshape(4, 2, -1, c))
+        near = ring_start(parts[1])
+    d_mlp_input = head_scatter(dot(d_gate_mlp, mlp_gate, 0, 1) + dot(d_up_mlp, mlp_up, 0, 1))
     scaled_mid = d_mlp_input * norm2_gain
     norm2_part = jnp.sum(d_mlp_input * unit_mid, axis=0)
-    d_middle = cot_f32 + scale_mid * (
+    d_middle = out_cotangent.astype(F32) + scale_mid * (
         scaled_mid - unit_mid * jnp.mean(scaled_mid * unit_mid, axis=-1, keepdims=True)
     )
     d_attn = d_middle.astype(BF)
-    d_attn_group = lax.all_gather(d_attn, "head", axis=0, tiled=True)
-    d_gated = dot(d_attn_group, out_weight.T)
-    out_weight_grad = dot(gated_out.T, d_attn_group)
+    d_attn_group = head_gather(d_attn)
+    d_gated = dot(d_attn_group, out_weight, 1, 1)
+    out_weight_grad = dot(gated_out, d_attn_group, 0, 0).astype(BF)
     d_post = d_gated * gate_act
     d_gate_pre = gelu_back(d_gated * post_out)[0].astype(BF)
     post_gain_part = jnp.sum(d_post * z_hat, axis=0)
@@ -373,63 +579,117 @@
         d_zhat - back_sums[0][:, None] / model_width - z_hat * (back_sums[1][:, None] / model_width)
     )
     step_grads, seg_grad = K["sgrad"](d_z, q_eff, step_maps)
-    all_grads = lax.all_gather(seg_grad, "seq", axis=0, tiled=False)
+    if wide:
+        seg_grad, cross, near = together(seg_grad, cross, near)
+    all_grads, _ = seq_gather(seg_grad)
+    if wide:
+        all_grads, near, out_late = together(all_grads, near, out_weight_grad)
+        second = ring_end(near, 2)
+        out_slice = lax.psum_scatter(out_late, "seq", scatter_dimension=0, tiled=True)
     d_query, b_part, lam_part = K["qgrad"](query_rows, key_rows, rate_rows, d_z, errors, states, pt)
-    d_key, d_value, d_rate, init_grad = K["kgrad"](
-        seg, all_maps, all_maps, all_grads, key_rows, rate_rows, errors, states, vv,
-        b_part, lam_part, step_maps, step_grads,
+    d_key, d_value, d_rate, init_grad, packed = K["kgrad"](
+        place, all_maps, all_maps, all_grads, key_rows, rate_rows, errors, states, vv,
+        b_part, lam_part, step_maps, step_grads, d_query, d_gate_pre,
     )
+    if wide:
+        d_rate, packed, second = together(d_rate, packed, second)
+        second = pair_reduce(second[None])[0]
+        first = ring_end(ring_start(cross), 1)
     d_rate_pre = (d_rate * rate_scale * rate_sig * (1.0 - rate_sig)).astype(BF)
     scale_part = jnp.sum(d_rate * rate_sig, axis=0)
-    rate_bias_part = jnp.sum(d_rate_pre.astype(F32), axis=0)
-    gate_grad = dot(group_in.T, d_gate_pre)
-    query_grad = dot(group_in.T, d_query)
-    key_grad = dot(group_in.T, d_key)
-    value_grad = dot(group_in.T, d_value)
-    rate_weight_part = dot(group_in.T, d_rate_pre)
-    total = dot(d_query, query_weight.T)
-    total = total + dot(d_key, key_weight.T)
-    total = total + dot(d_value, value_weight.T)
-    total = total + dot(d_gate_pre, gate_weight.T)
-    d_normed = lax.psum_scatter(
-        (total + dot(d_rate_pre, rate_weight.T)).astype(BF), "head", scatter_dimension=0, tiled=True
-    ).astype(F32)
+    total = dot(d_query, query_weight, 1, 1)
+    total = total + dot(d_key, key_weight, 1, 1)
+    total = total + dot(d_value, value_weight, 1, 1)
+    total = total + dot(d_gate_pre, gate_weight, 1, 1)
+    d_normed = head_scatter(total + dot(d_rate_pre, rate_weight, 1, 1))
     scaled_in = d_normed * norm1_gain
     norm1_part = jnp.sum(d_normed * unit_in, axis=0)
     input_grad = d_middle + scale_in * (
         scaled_in - unit_in * jnp.mean(scaled_in * unit_in, axis=-1, keepdims=True)
     )
-    mid_in = (out_weight_grad.astype(BF), gate_grad.astype(BF), d_query)
-    mid_in, mlp_sums = lax.optimization_barrier((mid_in, mlp_sums))
-    mid_sums = lax.psum(mid_in[:2], "seq")
-    late_in = (query_grad.astype(BF), key_grad.astype(BF), value_grad.astype(BF))
-    late_in, mid_sums = lax.optimization_barrier((late_in, mid_sums))
-    late_sums = lax.psum(late_in, "seq")
-    small = lax.psum(
-        (rate_weight_part, rate_bias_part, scale_part, post_gain_part, post_bias_part), "seq"
-    )
-    gain_grads = lax.psum((norm1_part, norm2_part), ("seq", "head"))
-    up = lambda x: x.astype(F32)
+    block_out = (middle + head_scatter(dot(hidden, mlp_down, 0, 0))).astype(BF)
+
+    if wide:
+        packed = lax.all_to_all(packed, "seq", split_axis=0, concat_axis=0, tiled=True)
+        packed = packed.reshape(segs * tokens, packed.shape[2])
+        own = [dot(packed, v, 0, 0).astype(BF) for v in (normed_all[:, :c], normed_all[:, c:])]
+        norm_parts = lax.psum((norm1_part, norm2_part), "head")
+        ends = [0]
+        extra = [d_rate_pre.reshape(-1)]
+        for v in (scale_part, post_gain_part, post_bias_part, *norm_parts):
+            extra.append(halves(v).reshape(-1))
+        for v in extra:
+            ends.append(ends[-1] + v.shape[0])
+        cd = model_width - c
+        extra = jnp.concatenate(extra + [jnp.zeros((16 * cd - ends[-1],), BF)]).reshape(16, cd)
+        gathered = result_gather(
+            jnp.concatenate([first, own[0], out_slice[:, :c]], axis=0),
+            jnp.concatenate([second, own[1], out_slice[:, c:], extra], axis=0),
+        )
+        full = segs * HW
+        first_row = 3 * rows
+        plan = tuple((t * rows, rows, False) for t in range(3))
+        plan += tuple((first_row + t * HW, HW, t < 4) for t in range(5))
+        sums = finish(gathered, plan, (width,) * 3 + (full,) * 5)
+        gate_sum, up_sum, down_sum, query_sum, key_sum, value_sum, pre_sum, out_sum = sums
+        gate_sum, up_sum = gate_sum.T, up_sum.T
+        shared = jnp.concatenate([g[:, -16:] for g in gathered[1]], axis=0).reshape(segs, -1)
+        shared = shared[jnp.argsort(gathered[2][segs:])]
+        from_all = [shared[:, s:e] for s, e in zip(ends[:-1], ends[1:])]
+        d_rate_all = from_all[0].reshape(segs * tokens, local_heads)
+        totals = [jnp.sum(v.astype(F32).reshape(2 * segs, -1), axis=0) for v in from_all[1:]]
+        small = (
+            dot(normed_all, d_rate_all, 0, 0),
+            jnp.sum(d_rate_all.astype(F32), axis=0),
+            *totals[:3],
+        )
+        gain_grads = totals[3:]
+    else:
+        grads = (
+            dot(hidden, group_cot),
+            dot(mlp_group, d_gate_mlp, 0, 1),
+            dot(mlp_group, d_up_mlp, 0, 1),
+            dot(group_in, d_query, 0, 0),
+            dot(group_in, d_key, 0, 0),
+            dot(group_in, d_value, 0, 0),
+            dot(group_in, d_gate_pre, 0, 0),
+            out_weight_grad,
+        )
+        sums = lax.psum(tuple(g.astype(BF) for g in grads), "seq")
+        down_sum, gate_sum, up_sum, query_sum, key_sum, value_sum, pre_sum, out_sum = (
+            s.astype(F32) for s in sums
+        )
+        small = lax.psum(
+            (
+                dot(group_in, d_rate_pre, 0, 0),
+                jnp.sum(d_rate_pre.astype(F32), axis=0),
+                scale_part,
+                post_gain_part,
+                post_bias_part,
+            ),
+            "seq",
+        )
+        gain_grads = lax.psum((norm1_part, norm2_part), everywhere)
     return (
         block_out,
         input_grad,
         gain_grads[0],
-        up(late_sums[0]),
-        up(late_sums[1]),
-        up(late_sums[2]),
-        up(mid_sums[1]),
+        query_sum,
+        key_sum,
+        value_sum,
+        pre_sum,
         small[0],
         small[1],
         small[2],
-        init_grad[:, :head_width, :head_width],
-        init_grad[:, head_width, :head_width],
+        init_grad[:, :HW, :HW],
+        init_grad[:, HW, :HW],
         small[3],
         small[4],
-        up(mid_sums[0]),
+        out_sum,
         gain_grads[1],
-        up(mlp_sums[1]),
-        up(mlp_sums[2]),
-        up(mlp_sums[0]),
+        gate_sum,
+        up_sum,
+        down_sum,
     )
 
 

time: 1420 us -> 1140 us (0.80)
  waiting for transfers between devices: 1020 us -> 659 us
  starting transfers between devices: 0.75 us -> 74.6 us
  blocking collectives: 75.2 us -> 25 us
  Pallas kernels: 97.1 us -> 129 us
  local copies, waits for them, and re-layouts: 26.3 us -> 49 us
  other arithmetic: 56.9 us -> 77.2 us
  matrix products: 118 us -> 100 us
    psum x4 -> x0, waiting for transfers between devices: 793 us -> none  [the longest x1 482 us: body(): lax.psum((mlp_down_grad.astype(BF), mlp_gate_grad.astype(BF), mlp_up_grad...]
    ppermute x0 -> x46, waiting for transfers between devices: none -> 643 us  [the longest x30 576 us: shift(): return lax.ppermute(v, 'seq', pairs)]
    all_gather x6 -> x1, waiting for transfers between devices: 123 us -> 5.14 us  [body(): normed_all = lax.all_gather(normed, everywhere, axis=0, tiled=True)]
    reduce_scatter x4 -> x1, waiting for transfers between devices: 103 us -> 0.02 us  [body(): lax.psum_scatter(out_late, 'seq', scatter_dimension=0, tiled=True)]
    ppermute x0 -> x46, starting transfers between devices: none -> 69.9 us  [the longest x30 54.6 us: shift(): return lax.ppermute(v, 'seq', pairs)]
    psum x2 -> x1, blocking collectives: 63 us -> 11.7 us  [body(): norm_parts = lax.psum((norm1_part, norm2_part), 'head')]
    pallas_call x0 -> x1, Pallas kernels: none -> 30.1 us  [finish(): pl.pallas_call(functools.partial(finish_kernel, len(group_c), len(group_d...]
    convert_element_type x8 -> x17, other arithmetic: 38.2 us -> 14.9 us  [the longest x3 8.71 us: plus(): return (a.astype(F32) + b.astype(F32)).astype(BF)]
  transfers between devices with their start and end apart: 14 -> 49, of which waited for: 14 -> 32; matrix products, arithmetic and copies ran while one was open for 9% -> 13% of each run, Pallas kernels for 4% -> 5%
where the time goes in v2:
time: 1140 us; the launch traced here: 1130 us
  waiting for transfers between devices  659 us (58%)
  Pallas kernels  129 us (11%)
  matrix products  100 us (9%)
  other arithmetic  77.2 us (7%)
  starting transfers between devices  74.6 us (7%)
  local copies, waits for them, and re-layouts  49 us (4%)
  blocking collectives  25 us (2%)
  between operations  17.9 us (2%)
    ppermute x30, waiting for transfers between devices, shift(): return lax.ppermute(v, 'seq', pairs)  576 us
    dot_general x26, matrix products, dot(): lax.dot_general(a, b, (((ca,), (cb,)), ((), ())), preferred_element_type=...  100 us
    ppermute x16, waiting for transfers between devices, head_shift(): return lax.ppermute(v, 'head', pairs)  66.8 us
    ppermute x30, starting transfers between devices, shift(): return lax.ppermute(v, 'seq', pairs)  54.6 us
    pallas_call x1, Pallas kernels, body(): inv, uw, step_maps, seg_map = K['map'](key_rows, value_rows, rate_rows)  32.1 us
    pallas_call x1, Pallas kernels, finish(): pl.pallas_call(functools.partial(finish_kernel, len(group_c), len(group_d...  30.1 us
    pallas_call x1, Pallas kernels, body(): K['kgrad']  28.8 us
    unnamed x292, local copies, waits for them, and re-layouts  23 us
  transfers between devices with their start and end apart: 49, of which 32 were waited for; matrix products, arithmetic and copies ran while one was open for 13% of the time, Pallas kernels for 5%

profile of v2, /device:TPU:0, one launch (start us, length us, event | category | flops | bytes accessed | tf_op | source)
XLA Modules:
  0.0 1131.9 jit_solution(11711010365909780197)
XLA Ops:
  15.0 10.7 collective-permute-done
  38.7 32.1 %segment_maps.1 = (bf16[8,4,128,128]{3,2,1,0:T(8,128)(2,1)S(1)}, bf16[8,512,256]{2,1,0:T(8,128)(2,1)S(1)}, bf16[8,4,128,256]{3,2,1,0:T(8,128)(2,1)}, bf16[9,80,128]{2,1,0:T(8,128)(2,1)S(1)}) custom-call(f32[512,512]{1,0:T(8,128)S(1)} %fusion.125.k_ref, f32[512,512]{1,0:T(8,128)S(1)} %fusion.124.v_ref, f32[512,8]{1,0:T(8,128)S(1)} %get-tuple-element.195.r_ref), custom_call_target="tpu_custom_call" | custom-call | tf_op jit(solution)/shard_map/segment_maps/pallas_call | solution.py:516
  72.7 4.9 collective-permute-done.2
  80.7 8.2 local_parts.1
  91.2 8.9 collective-permute-done.3
  100.1 4.3 collective-permute-start.6
  108.8 14.9 %forward_states.1 = (f32[512,512]{1,0:T(8,128)S(1)}, bf16[8,512,128]{2,1,0:T(8,128)(2,1)S(1)}, bf16[8,4,128,128]{3,2,1,0:T(8,128)(2,1)S(1)}) custom-call(s32[9]{0:T(128)S(1)} %pad_add_fusion.1.seg_ref, bf16[8,9,80,128]{3,2,1,0:T(8,128)(2,1)} %copy-done.36, bf16[8,9,80,128]{3,2,1,0:T(8,128)(2,1)} %copy-done.36, f32[8,64,64]{2,1,0:T(8,128)S(1)} %copy-done.26, ...), custom_call_target="tpu_custom_call" | custom-call | tf_op jit(solution)/shard_map/forward_states/pallas_call | solution.py:522
  125.9 5.9 all-reduce.5
  131.8 5.0 multiply_convert_fusion.3
  144.3 10.5 collective-permute-done.13
  155.0 10.0 collective-permute-done.8
  167.5 11.1 collective-permute-done.9
  185.7 3.2 convolution_bitcast_fusion.2
  188.9 6.0 multiply_convert_fusion
  200.4 4.8 convolution_convert_fusion.2
  205.2 6.9 pad_maximum_fusion
  212.2 6.0 fusion.129
  218.2 6.5 add_convert_fusion.2
  231.8 4.4 dynamic-slice_bitcast_fusion
  239.7 5.2 collective-permute-done.16
  249.8 4.1 convolution_convert_fusion
  254.0 7.8 collective-permute-done.17
  262.9 4.3 fusion.90
  270.0 3.8 collective-permute-start.21
  277.6 4.9 multiply_reduce_fusion.1
  282.5 7.4 all-reduce.4
  291.9 5.8 state_grads.1
  301.7 18.6 %collective-permute-done.19 = bf16[4,528,896]{2,1,0:T(8,128)(2,1)} collective-permute-done((bf16[4,528,896]{2,1,0:T(8,128)(2,1)}, bf16[4,528,896]{2,1,0:T(8,128)(2,1)}, u32[]{:S(2)}, u32[]{:S(2)}) %collective-permute-start.19) | collective-permute-done | bytes 3784736 | tf_op jit(solution)/shard_map/ppermute | solution.py:276
  320.3 6.1 fusion.2
  331.6 3.7 collective-permute-start.23
  335.3 4.3 collective-permute-done.24
  339.8 4.6 collective-permute-start.26
  361.3 9.5 query_grads.1
  370.8 3.3 fusion.130
  374.1 3.3 fusion.132
  380.5 28.8 %key_grads.1 = (bf16[512,512]{1,0:T(8,128)(2,1)S(1)}, bf16[512,512]{1,0:T(8,128)(2,1)S(1)}, f32[512,8]{1,0:T(8,128)S(1)}, f32[8,72,128]{2,1,0:T(8,128)S(1)}, bf16[8,512,256]{2,1,0:T(8,128)(2,1)}) custom-call(s32[9]{0:T(128)S(1)} %pad_add_fusion.1.seg_ref, bf16[8,9,80,128]{3,2,1,0:T(8,128)(2,1)} %copy-done.36, bf16[8,9,80,128]{3,2,1,0:T(8,128)(2,1)} %copy-done.36, ...), custom_call_target="tpu_custom_call" | custom-call | tf_op jit(solution)/shard_map/key_grads/pallas_call | solution.py:590
  409.3 3.3 fusion.131
  412.6 22.2 %collective-permute-done.27 = bf16[2,528,1152]{2,1,0:T(8,128)(2,1)S(1)} collective-permute-done((bf16[2,528,1152]{2,1,0:T(8,128)(2,1)}, bf16[2,528,1152]{2,1,0:T(8,128)(2,1)S(1)}, u32[]{:S(2)}, u32[]{:S(2)}) %collective-permute-start.27) | collective-permute-done | bytes 2433056 | tf_op jit(solution)/shard_map/ppermute | solution.py:276
  434.8 73.8 %collective-permute-done.28 = bf16[2,528,1152]{2,1,0:T(8,128)(2,1)S(1)} collective-permute-done((bf16[2,528,1152]{2,1,0:T(8,128)(2,1)}, bf16[2,528,1152]{2,1,0:T(8,128)(2,1)S(1)}, u32[]{:S(2)}, u32[]{:S(2)}) %collective-permute-start.28) | collective-permute-done | bytes 2433056 | tf_op jit(solution)/shard_map/ppermute | solution.py:276
  510.9 4.6 all-to-all-start
  517.9 5.6 add_convert_fusion.1
  538.1 55.9 %collective-permute-done.31 = bf16[1,528,1152]{2,1,0:T(8,128)(2,1)} collective-permute-done((bf16[1,528,1152]{2,1,0:T(8,128)(2,1)}, bf16[1,528,1152]{2,1,0:T(8,128)(2,1)}, u32[]{:S(2)}, u32[]{:S(2)}) %collective-permute-start.31) | collective-permute-done | bytes 1216544 | tf_op jit(solution)/shard_map/ppermute | solution.py:276
  597.9 11.7 %all-reduce.3 = (f32[2048]{0:T(1024)S(1)}, f32[2048]{0:T(1024)S(1)}) all-reduce(f32[2048]{0:T(1024)S(1)} %get-tuple-element.117, f32[2048]{0:T(1024)S(1)} %get-tuple-element.115), channel_id=1, replica_groups=mesh['seq'=8,'head'=4] {'head'}, use_global_device_ids=true, to_apply=%region_17.18 | all-reduce | flops 4096 | bytes 32768 | tf_op jit(solution)/shard_map/psum | solution.py:616
  610.0 9.9 all-to-all-done
  620.0 5.1 all-gather.2.cloned.1.call-done
  625.1 7.3 fusion.10
  636.9 3.8 collective-permute-start.40
  640.7 20.4 %collective-permute-done.38 = bf16[528,896]{1,0:T(8,128)(2,1)S(1)} collective-permute-done((bf16[528,896]{1,0:T(8,128)(2,1)S(1)}, bf16[528,896]{1,0:T(8,128)(2,1)S(1)}, u32[]{:S(2)}, u32[]{:S(2)}) %collective-permute-start.38) | collective-permute-done | bytes 946208 | tf_op jit(solution)/shard_map/ppermute | solution.py:276
  661.1 19.0 %collective-permute-done.40 = bf16[528,896]{1,0:T(8,128)(2,1)S(1)} collective-permute-done((bf16[528,896]{1,0:T(8,128)(2,1)S(1)}, bf16[528,896]{1,0:T(8,128)(2,1)S(1)}, u32[]{:S(2)}, u32[]{:S(2)}) %collective-permute-start.40) | collective-permute-done | bytes 946208 | tf_op jit(solution)/shard_map/ppermute | solution.py:276
  684.4 6.1 fusion.32
  695.3 3.8 collective-permute-start.33
  699.2 3.8 convolution_convert_fusion.6
  704.0 103.1 %collective-permute-done.41 = bf16[848,896]{1,0:T(8,128)(2,1)S(1)} collective-permute-done((bf16[848,896]{1,0:T(8,128)(2,1)}, bf16[848,896]{1,0:T(8,128)(2,1)S(1)}, u32[]{:S(2)}, u32[]{:S(2)}) %collective-permute-start.41) | collective-permute-done | bytes 1519648 | tf_op jit(solution)/shard_map/ppermute | solution.py:276
  811.1 28.7 %collective-permute-done.42 = bf16[848,896]{1,0:T(8,128)(2,1)} collective-permute-done((bf16[848,896]{1,0:T(8,128)(2,1)}, bf16[848,896]{1,0:T(8,128)(2,1)}, u32[]{:S(2)}, u32[]{:S(2)}) %collective-permute-start.42) | collective-permute-done | bytes 1519648 | tf_op jit(solution)/shard_map/ppermute | solution.py:276
  843.0 113.3 %collective-permute-done.43 = bf16[416,896]{1,0:T(8,128)(2,1)S(1)} collective-permute-done((bf16[416,896]{1,0:T(8,128)(2,1)S(1)}, bf16[416,896]{1,0:T(8,128)(2,1)S(1)}, u32[]{:S(2)}, u32[]{:S(2)}) %collective-permute-start.43) | collective-permute-done | bytes 745504 | tf_op jit(solution)/shard_map/ppermute | solution.py:276
  957.6 4.4 pad_maximum_fusion.1.refs_0_
  968.3 3.9 collective-permute-start.36
  973.5 4.0 collective-permute-done.12
  977.6 3.6 fusion.67
  982.1 30.9 %collective-permute-done.35.refs_4_ = bf16[1,864,1152]{2,1,0:T(8,128)(2,1)S(1)} collective-permute-done((bf16[1,864,1152]{2,1,0:T(8,128)(2,1)S(1)}, bf16[1,864,1152]{2,1,0:T(8,128)(2,1)S(1)}, u32[]{:S(2)}, u32[]{:S(2)}) %collective-permute-start.35) | collective-permute-done | bytes 1990688 | tf_op jit(solution)/shard_map/ppermute | solution.py:276
  1013.0 40.2 %collective-permute-done.36.refs_5_ = bf16[1,864,1152]{2,1,0:T(8,128)(2,1)S(1)} collective-permute-done((bf16[1,864,1152]{2,1,0:T(8,128)(2,1)S(1)}, bf16[1,864,1152]{2,1,0:T(8,128)(2,1)S(1)}, u32[]{:S(2)}, u32[]{:S(2)}) %collective-permute-start.36) | collective-permute-done | bytes 1990688 | tf_op jit(solution)/shard_map/ppermute | solution.py:276
  1061.8 8.9 fusion.134
  1070.6 23.5 %collective-permute-done.45.refs_1_ = bf16[4,848,896]{2,1,0:T(8,128)(2,1)} collective-permute-done((bf16[4,848,896]{2,1,0:T(8,128)(2,1)}, bf16[4,848,896]{2,1,0:T(8,128)(2,1)}, u32[]{:S(2)}, u32[]{:S(2)}) %collective-permute-start.45) | collective-permute-done | bytes 6078496 | tf_op jit(solution)/shard_map/ppermute | solution.py:276
  1094.1 30.1 %finish.1 = (f32[1376,2048]{1,0:T(8,128)}, f32[1376,2048]{1,0:T(8,128)}, f32[1376,2048]{1,0:T(8,128)}, f32[2048,512]{1,0:T(8,128)}, f32[2048,512]{1,0:T(8,128)},...) custom-call(s32[16]{0:T(128)S(1)} %pad_add_fusion.2.at_ref, ...), custom_call_target="tpu_custom_call" | custom-call | tf_op jit(solution)/shard_map/finish/pallas_call | solution.py:447
  (517 shorter events, 173.5 us)
Async XLA Ops:
  8.0 129.6 %copy-start = (bf16[512,2048]{1,0:T(8,128)(2,1)S(1)}, bf16[512,2048]{1,0:T(8,128)(2,1)}, u32[]{:S(2)}) copy-start(bf16[512,2048]{1,0:T(8,128)(2,1)} %param.32) | copy-start | bytes 6291460
  8.0 602.0 %reduce-scatter.2.cloned.1.call-start = ((), (), s32[]{:S(2)}) async-start(), calls=%async_computation.3 | async-start | bytes 2359296 | tf_op jit(solution)/shard_map/reduce_scatter | solution.py:588
  10.7 15.0 %collective-permute-start = (bf16[128,2048]{1,0:T(8,128)(2,1)S(1)}, bf16[128,2048]{1,0:T(8,128)(2,1)S(1)}, u32[]{:S(2)}, u32[]{:S(2)}) collective-permute-start(bf16[128,2048]{1,0:T(8,128)(2,1)S(1)} %fusion.63), channel_id=1, source_target_pairs={{0,2},{1,3},{2,0},{3,1},{4,6},{5,7},{6,4},{7,5},{8,10},{9,11},{10,... | collective-permute-start | bytes 1572872 | tf_op jit(solution)/shard_map/ppermute | solution.py:299
  27.5 3.0 collective-permute-start.1
  32.1 47.3 %copy-start.97 = (bf16[128,2048]{1,0:T(8,128)(2,1)}, bf16[128,2048]{1,0:T(8,128)(2,1)S(1)}, u32[]{:S(2)}) copy-start(bf16[128,2048]{1,0:T(8,128)(2,1)S(1)} %get-tuple-element.182) | copy-start | bytes 1572868
  32.2 47.3 %copy-start.98 = (bf16[128,2048]{1,0:T(8,128)(2,1)}, bf16[128,2048]{1,0:T(8,128)(2,1)S(1)}, u32[]{:S(2)}) copy-start(bf16[128,2048]{1,0:T(8,128)(2,1)S(1)} %get-tuple-element.183) | copy-start | bytes 1572868
  32.3 47.2 %copy-start.99 = (bf16[128,2048]{1,0:T(8,128)(2,1)}, bf16[128,2048]{1,0:T(8,128)(2,1)S(1)}, u32[]{:S(2)}) copy-start(bf16[128,2048]{1,0:T(8,128)(2,1)S(1)} %get-tuple-element.184) | copy-start | bytes 1572868
  32.3 47.2 %copy-start.100 = (bf16[128,2048]{1,0:T(8,128)(2,1)}, bf16[128,2048]{1,0:T(8,128)(2,1)S(1)}, u32[]{:S(2)}) copy-start(bf16[128,2048]{1,0:T(8,128)(2,1)S(1)} %get-tuple-element.185) | copy-start | bytes 1572868
  70.8 6.7 collective-permute-start.2
  77.6 13.5 %collective-permute-start.4 = (bf16[2,9,80,128]{3,2,1,0:T(8,128)(2,1)S(1)}, bf16[2,9,80,128]{3,2,1,0:T(8,128)(2,1)S(1)}, u32[]{:S(2)}, u32[]{:S(2)}) collective-permute-start(bf16[2,9,80,128]{3,2,1,0:T(8,128)(2,1)S(1)} %pad_maximum_fusion.18), channel_id=1, source_target_pairs={{0,8},{4,12},{8,16},{12,20},{16,24},{20,28},{24,0},{28,4},{1,9},{5... | collective-permute-start | bytes 1105928 | tf_op jit(solution)/shard_map/ppermute | solution.py:276
  89.0 11.2 collective-permute-start.3
  91.1 15.5 %collective-permute-start.5 = (bf16[1,9,80,128]{3,2,1,0:T(8,128)(2,1)S(1)}, bf16[1,9,80,128]{3,2,1,0:T(8,128)(2,1)S(1)}, u32[]{:S(2)}, u32[]{:S(2)}) collective-permute-start(bf16[1,9,80,128]{3,2,1,0:T(8,128)(2,1)S(1)} %slice.298), channel_id=1, source_target_pairs={{0,8},{4,12},{8,16},{12,20},{16,24},{20,28},{24,0},{28,4},{1,9},{5... | collective-permute-start | bytes 552968 | tf_op jit(solution)/shard_map/ppermute | solution.py:276
  100.1 7.4 collective-permute-start.6
  139.1 2.7 collective-permute-start.7
  140.0 14.8 %collective-permute-start.13 = (bf16[128,2048]{1,0:T(8,128)(2,1)S(1)}, bf16[128,2048]{1,0:T(8,128)(2,1)S(1)}, u32[]{:S(2)}, u32[]{:S(2)}) collective-permute-start(bf16[128,2048]{1,0:T(8,128)(2,1)S(1)} %copy-done.50), channel_id=1, source_target_pairs={{0,2},{1,3},{2,0},{3,1},{4,6},{5,7},{6,4},{7,5},{8,10},{9,11},{10,... | collective-permute-start | bytes 1572872 | tf_op jit(solution)/shard_map/ppermute | solution.py:299
  142.5 22.5 %collective-permute-start.8 = (bf16[128,2048]{1,0:T(8,128)(2,1)S(1)}, bf16[128,2048]{1,0:T(8,128)(2,1)S(1)}, u32[]{:S(2)}, u32[]{:S(2)}) collective-permute-start(bf16[128,2048]{1,0:T(8,128)(2,1)S(1)} %select_bitcast_fusion.19), channel_id=1, source_target_pairs={{0,2},{1,3},{2,0},{3,1},{4,6},{5,7},{6,4},{7,5},{8,10},{9,11},{10,... | collective-permute-start | bytes 1572872 | tf_op jit(solution)/shard_map/ppermute | solution.py:299
  154.9 23.9 %collective-permute-start.14 = (bf16[2,128,2048]{2,1,0:T(8,128)(2,1)S(1)}, bf16[2,128,2048]{2,1,0:T(8,128)(2,1)S(1)}, u32[]{:S(2)}, u32[]{:S(2)}) collective-permute-start(bf16[2,128,2048]{2,1,0:T(8,128)(2,1)S(1)} %pad_maximum_fusion.14), channel_id=1, source_target_pairs={{0,1},{1,0},{2,3},{3,2},{4,5},{5,4},{6,7},{7,6},{8,9},{9,8},{10,11... | collective-permute-start | bytes 3145736 | tf_op jit(solution)/shard_map/ppermute | solution.py:299
  165.6 13.0 %collective-permute-start.9 = (bf16[128,2048]{1,0:T(8,128)(2,1)S(1)}, bf16[128,2048]{1,0:T(8,128)(2,1)S(1)}, u32[]{:S(2)}, u32[]{:S(2)}) collective-permute-start(bf16[128,2048]{1,0:T(8,128)(2,1)S(1)} %multiply_convert_fusion.2), channel_id=1, source_target_pairs={{0,2},{1,3},{2,0},{3,1},{4,6},{5,7},{6,4},{7,5},{8,10},{9,11},{10,... | collective-permute-start | bytes 1572872 | tf_op jit(solution)/shard_map/ppermute | solution.py:299
  178.7 2.7 collective-permute-start.10
  224.8 3.2 collective-permute-start.15
  230.3 14.5 %collective-permute-start.16 = (bf16[128,2048]{1,0:T(8,128)(2,1)}, bf16[128,2048]{1,0:T(8,128)(2,1)}, u32[]{:S(2)}, u32[]{:S(2)}) collective-permute-start(bf16[128,2048]{1,0:T(8,128)(2,1)} %select_bitcast_fusion.9), channel_id=1, source_target_pairs={{0,2},{1,3},{2,0},{3,1},{4,6},{5,7},{6,4},{7,5},{8,10},{9,11},{10,... | collective-permute-start | bytes 1572872 | tf_op jit(solution)/shard_map/ppermute | solution.py:299
  236.2 84.1 %collective-permute-start.19 = (bf16[4,528,896]{2,1,0:T(8,128)(2,1)}, bf16[4,528,896]{2,1,0:T(8,128)(2,1)}, u32[]{:S(2)}, u32[]{:S(2)}) collective-permute-start(bf16[4,528,896]{2,1,0:T(8,128)(2,1)} %dynamic-slice_bitcast_fusion), channel_id=1, source_target_pairs={{0,4},{4,0},{8,12},{12,8},{16,20},{20,16},{24,28},{28,24},{1,5},{5... | collective-permute-start | bytes 11354120 | tf_op jit(solution)/shard_map/ppermute | solution.py:276
  248.3 13.4 %collective-permute-start.17 = (bf16[128,2048]{1,0:T(8,128)(2,1)S(1)}, bf16[128,2048]{1,0:T(8,128)(2,1)S(1)}, u32[]{:S(2)}, u32[]{:S(2)}) collective-permute-start(bf16[128,2048]{1,0:T(8,128)(2,1)S(1)} %fusion.118), channel_id=1, source_target_pairs={{0,2},{1,3},{2,0},{3,1},{4,6},{5,7},{6,4},{7,5},{8,10},{9,11},{10,... | collective-permute-start | bytes 1572872 | tf_op jit(solution)/shard_map/ppermute | solution.py:299
  262.9 10.9 collective-permute-start.18
  268.4 58.0 %collective-permute-start.20 = (bf16[528,1152]{1,0:T(8,128)(2,1)}, bf16[528,1152]{1,0:T(8,128)(2,1)}, u32[]{:S(2)}, u32[]{:S(2)}) collective-permute-start(bf16[528,1152]{1,0:T(8,128)(2,1)} %dynamic-slice_bitcast_fusion.2), channel_id=1, source_target_pairs={{0,8},{4,12},{8,16},{12,20},{16,24},{20,28},{24,0},{28,4},{1,9},{5... | collective-permute-start | bytes 3649544 | tf_op jit(solution)/shard_map/ppermute | solution.py:276
  270.0 56.4 %collective-permute-start.21 = (bf16[528,1152]{1,0:T(8,128)(2,1)}, bf16[528,1152]{1,0:T(8,128)(2,1)}, u32[]{:S(2)}, u32[]{:S(2)}) collective-permute-start(bf16[528,1152]{1,0:T(8,128)(2,1)} %dynamic-slice_bitcast_fusion.1), channel_id=1, source_target_pairs={{0,24},{4,28},{8,0},{12,4},{16,8},{20,12},{24,16},{28,20},{1,25},{... | collective-permute-start | bytes 3649544 | tf_op jit(solution)/shard_map/ppermute | solution.py:276
  326.4 4.4 collective-permute-start.22
  330.8 8.7 collective-permute-start.24
  331.6 8.3 collective-permute-start.23
  339.5 7.3 collective-permute-start.25
  339.8 7.0 collective-permute-start.26
  346.9 278.2 %all-gather.2.cloned.1.call-start = ((), (), s32[]{:S(2)}) async-start(), calls=%async_computation.2 | async-start | bytes 17301504 | tf_op jit(solution)/shard_map/all_gather | solution.py:510
  353.3 81.5 %collective-permute-start.27 = (bf16[2,528,1152]{2,1,0:T(8,128)(2,1)}, bf16[2,528,1152]{2,1,0:T(8,128)(2,1)S(1)}, u32[]{:S(2)}, u32[]{:S(2)}) collective-permute-start(bf16[2,528,1152]{2,1,0:T(8,128)(2,1)} %pad_maximum_fusion.5), channel_id=1, source_target_pairs={{0,8},{4,12},{8,16},{12,20},{16,24},{20,28},{24,0},{28,4},{1,9},{5... | collective-permute-start | bytes 7299080 | tf_op jit(solution)/shard_map/ppermute | solution.py:276
  358.5 150.0 %collective-permute-start.28 = (bf16[2,528,1152]{2,1,0:T(8,128)(2,1)}, bf16[2,528,1152]{2,1,0:T(8,128)(2,1)S(1)}, u32[]{:S(2)}, u32[]{:S(2)}) collective-permute-start(bf16[2,528,1152]{2,1,0:T(8,128)(2,1)} %pad_maximum_fusion.6), channel_id=1, source_target_pairs={{0,24},{4,28},{8,0},{12,4},{16,8},{20,12},{24,16},{28,20},{1,25},{... | collective-permute-start | bytes 7299080 | tf_op jit(solution)/shard_map/ppermute | solution.py:276
  510.9 109.0 %all-to-all-start = ((bf16[8,512,256]{2,1,0:T(8,128)(2,1)}), bf16[8,512,256]{2,1,0:T(8,128)(2,1)}, u32[]{:S(2)}, u32[]{:S(2)}) async-start(bf16[8,512,256]{2,1,0:T(8,128)(2,1)} %get-tuple-element.100), calls=%async_computation | async-start | bytes 4194304 | tf_op jit(solution)/shard_map/all_to_all | solution.py:613
  524.6 11.5 %collective-permute-start.29 = (bf16[2,128,2048]{2,1,0:T(8,128)(2,1)}, bf16[2,128,2048]{2,1,0:T(8,128)(2,1)S(1)}, u32[]{:S(2)}, u32[]{:S(2)}) collective-permute-start(bf16[2,128,2048]{2,1,0:T(8,128)(2,1)} %select_bitcast_fusion), channel_id=1, source_target_pairs={{0,1},{1,0},{2,3},{3,2},{4,5},{5,4},{6,7},{7,6},{8,9},{9,8},{10,11... | collective-permute-start | bytes 3145736 | tf_op jit(solution)/shard_map/ppermute | solution.py:299
  527.7 106.2 %collective-permute-start.37 = (bf16[256,896]{1,0:T(8,128)(2,1)}, bf16[256,896]{1,0:T(8,128)(2,1)}, u32[]{:S(2)}, u32[]{:S(2)}) collective-permute-start(bf16[256,896]{1,0:T(8,128)(2,1)} %get-tuple-element.165), channel_id=1, source_target_pairs={{0,8},{4,12},{8,16},{12,20},{16,24},{20,28},{24,0},{28,4},{1,9},{5... | collective-permute-start | bytes 1376264 | tf_op jit(solution)/shard_map/ppermute | solution.py:276
  530.9 104.5 %collective-permute-start.39 = (bf16[272,896]{1,0:T(8,128)(2,1)}, bf16[272,896]{1,0:T(8,128)(2,1)}, u32[]{:S(2)}, u32[]{:S(2)}) collective-permute-start(bf16[272,896]{1,0:T(8,128)(2,1)} %get-tuple-element.161), channel_id=1, source_target_pairs={{0,24},{4,28},{8,0},{12,4},{16,8},{20,12},{24,16},{28,20},{1,25},{... | collective-permute-start | bytes 1462280 | tf_op jit(solution)/shard_map/ppermute | solution.py:276
  534.0 60.0 %collective-permute-start.31 = (bf16[1,528,1152]{2,1,0:T(8,128)(2,1)}, bf16[1,528,1152]{2,1,0:T(8,128)(2,1)}, u32[]{:S(2)}, u32[]{:S(2)}) collective-permute-start(bf16[1,528,1152]{2,1,0:T(8,128)(2,1)} %constant_dynamic-slice_fusion), channel_id=1, source_target_pairs={{0,4},{4,0},{8,12},{12,8},{16,20},{20,16},{24,28},{28,24},{1,5},{5... | collective-permute-start | bytes 3649544 | tf_op jit(solution)/shard_map/ppermute | solution.py:276
  536.2 57.8 %copy-start.45 = (bf16[2,528,1152]{2,1,0:T(8,128)(2,1)S(1)}, bf16[2,528,1152]{2,1,0:T(8,128)(2,1)}, u32[]{:S(2)}) copy-start(bf16[2,528,1152]{2,1,0:T(8,128)(2,1)} %add_convert_fusion) | copy-start | bytes 7299076
  536.7 59.9 %copy-start.40 = (bf16[128,2048]{1,0:T(8,128)(2,1)S(1)}, bf16[128,2048]{1,0:T(8,128)(2,1)}, u32[]{:S(2)}) copy-start(bf16[128,2048]{1,0:T(8,128)(2,1)} %param.19) | copy-start | bytes 1572868
  536.7 59.9 %copy-start.111 = (f32[2048]{0:T(1024)S(1)}, f32[2048]{0:T(1024)}, u32[]{:S(2)}) copy-start(f32[2048]{0:T(1024)} %param.20) | copy-start | bytes 24580
  536.8 59.9 %copy-start.115 = (f32[128]{0:T(128)S(1)}, f32[128]{0:T(128)}, u32[]{:S(2)}) copy-start(f32[128]{0:T(128)} %copy-done.114) | copy-start | bytes 1540
  536.8 59.8 %collective-permute-start.30 = (bf16[128,2048]{1,0:T(8,128)(2,1)S(1)}, bf16[128,2048]{1,0:T(8,128)(2,1)S(1)}, u32[]{:S(2)}, u32[]{:S(2)}) collective-permute-start(bf16[128,2048]{1,0:T(8,128)(2,1)S(1)} %select_bitcast_fusion.4), channel_id=1, source_target_pairs={{0,2},{1,3},{2,0},{3,1},{4,6},{5,7},{6,4},{7,5},{8,10},{9,11},{10,... | collective-permute-start | bytes 1572872 | tf_op jit(solution)/shard_map/ppermute | solution.py:299
  632.8 47.7 %copy-start.41 = (bf16[1,864,1152]{2,1,0:T(8,128)(2,1)}, bf16[1,864,1152]{2,1,0:T(8,128)(2,1)S(1)}, u32[]{:S(2)}) copy-start(bf16[1,864,1152]{2,1,0:T(8,128)(2,1)S(1)} %get-tuple-element.159) | copy-start | bytes 5971972
  632.8 47.7 %collective-permute-start.32 = (bf16[864,1152]{1,0:T(8,128)(2,1)S(1)}, bf16[864,1152]{1,0:T(8,128)(2,1)S(1)}, u32[]{:S(2)}, u32[]{:S(2)}) collective-permute-start(bf16[864,1152]{1,0:T(8,128)(2,1)S(1)} %get-tuple-element.158), channel_id=1, source_target_pairs={{0,4},{4,0},{8,12},{12,8},{16,20},{20,16},{24,28},{28,24},{1,5},{5... | collective-permute-start | bytes 5971976 | tf_op jit(solution)/shard_map/ppermute | solution.py:276
  635.2 44.9 %copy-start.77 = (bf16[272,896]{1,0:T(8,128)(2,1)S(1)}, bf16[272,896]{1,0:T(8,128)(2,1)}, u32[]{:S(2)}) copy-start(bf16[272,896]{1,0:T(8,128)(2,1)} %get-tuple-element.160) | copy-start | bytes 1462276
  635.2 44.9 %copy-start.79 = (bf16[256,896]{1,0:T(8,128)(2,1)S(1)}, bf16[256,896]{1,0:T(8,128)(2,1)}, u32[]{:S(2)}) copy-start(bf16[256,896]{1,0:T(8,128)(2,1)} %get-tuple-element.163) | copy-start | bytes 1376260
  635.3 25.8 %collective-permute-start.38 = (bf16[528,896]{1,0:T(8,128)(2,1)S(1)}, bf16[528,896]{1,0:T(8,128)(2,1)S(1)}, u32[]{:S(2)}, u32[]{:S(2)}) collective-permute-start(bf16[528,896]{1,0:T(8,128)(2,1)S(1)} %pad_maximum_fusion.16), channel_id=1, source_target_pairs={{0,8},{4,12},{8,16},{12,20},{16,24},{20,28},{24,0},{28,4},{1,9},{5... | collective-permute-start | bytes 2838536 | tf_op jit(solution)/shard_map/ppermute | solution.py:276
  636.9 43.2 %collective-permute-start.40 = (bf16[528,896]{1,0:T(8,128)(2,1)S(1)}, bf16[528,896]{1,0:T(8,128)(2,1)S(1)}, u32[]{:S(2)}, u32[]{:S(2)}) collective-permute-start(bf16[528,896]{1,0:T(8,128)(2,1)S(1)} %pad_maximum_fusion.17), channel_id=1, source_target_pairs={{0,24},{4,28},{8,0},{12,4},{16,8},{20,12},{24,16},{28,20},{1,25},{... | collective-permute-start | bytes 2838536 | tf_op jit(solution)/shard_map/ppermute | solution.py:276
  683.5 279.6 %collective-permute-start.34 = (bf16[2,864,1152]{2,1,0:T(8,128)(2,1)}, bf16[2,864,1152]{2,1,0:T(8,128)(2,1)}, u32[]{:S(2)}, u32[]{:S(2)}) collective-permute-start(bf16[2,864,1152]{2,1,0:T(8,128)(2,1)} %pad_maximum_fusion.3.refs_2_), channel_id=1, source_target_pairs={{0,8},{4,12},{8,16},{12,20},{16,24},{20,28},{24,0},{28,4},{1,9},{5... | collective-permute-start | bytes 11943944 | tf_op jit(solution)/shard_map/ppermute | solution.py:276
  692.4 114.8 %collective-permute-start.41 = (bf16[848,896]{1,0:T(8,128)(2,1)}, bf16[848,896]{1,0:T(8,128)(2,1)S(1)}, u32[]{:S(2)}, u32[]{:S(2)}) collective-permute-start(bf16[848,896]{1,0:T(8,128)(2,1)} %get-tuple-element.167), channel_id=1, source_target_pairs={{0,24},{4,28},{8,0},{12,4},{16,8},{20,12},{24,16},{28,20},{1,25},{... | collective-permute-start | bytes 4558856 | tf_op jit(solution)/shard_map/ppermute | solution.py:276
  695.3 144.4 %collective-permute-start.42 = (bf16[848,896]{1,0:T(8,128)(2,1)}, bf16[848,896]{1,0:T(8,128)(2,1)}, u32[]{:S(2)}, u32[]{:S(2)}) collective-permute-start(bf16[848,896]{1,0:T(8,128)(2,1)} %get-tuple-element.167), channel_id=1, source_target_pairs={{0,8},{4,12},{8,16},{12,20},{16,24},{20,28},{24,0},{28,4},{1,9},{5... | collective-permute-start | bytes 4558856 | tf_op jit(solution)/shard_map/ppermute | solution.py:276
  695.3 271.2 %collective-permute-start.33 = (bf16[2,864,1152]{2,1,0:T(8,128)(2,1)}, bf16[2,864,1152]{2,1,0:T(8,128)(2,1)}, u32[]{:S(2)}, u32[]{:S(2)}) collective-permute-start(bf16[2,864,1152]{2,1,0:T(8,128)(2,1)} %pad_maximum_fusion.3.refs_2_), channel_id=1, source_target_pairs={{0,24},{4,28},{8,0},{12,4},{16,8},{20,12},{24,16},{28,20},{1,25},{... | collective-permute-start | bytes 11943944 | tf_op jit(solution)/shard_map/ppermute | solution.py:276
  704.0 137.2 %collective-permute-start.11 = (bf16[2,128,2048]{2,1,0:T(8,128)(2,1)}, bf16[2,128,2048]{2,1,0:T(8,128)(2,1)}, u32[]{:S(2)}, u32[]{:S(2)}) collective-permute-start(bf16[2,128,2048]{2,1,0:T(8,128)(2,1)} %select_bitcast_fusion.2), channel_id=1, source_target_pairs={{0,1},{1,0},{2,3},{3,2},{4,5},{5,4},{6,7},{7,6},{8,9},{9,8},{10,11... | collective-permute-start | bytes 3145736 | tf_op jit(solution)/shard_map/ppermute | solution.py:299
  809.2 147.2 %collective-permute-start.44 = (bf16[432,896]{1,0:T(8,128)(2,1)}, bf16[432,896]{1,0:T(8,128)(2,1)}, u32[]{:S(2)}, u32[]{:S(2)}) collective-permute-start(bf16[432,896]{1,0:T(8,128)(2,1)} %slice.348), channel_id=1, source_target_pairs={{0,24},{4,28},{8,0},{12,4},{16,8},{20,12},{24,16},{28,20},{1,25},{... | collective-permute-start | bytes 2322440 | tf_op jit(solution)/shard_map/ppermute | solution.py:276
  841.0 115.4 %collective-permute-start.43 = (bf16[416,896]{1,0:T(8,128)(2,1)S(1)}, bf16[416,896]{1,0:T(8,128)(2,1)S(1)}, u32[]{:S(2)}, u32[]{:S(2)}) collective-permute-start(bf16[416,896]{1,0:T(8,128)(2,1)S(1)} %slice.347), channel_id=1, source_target_pairs={{0,8},{4,12},{8,16},{12,20},{16,24},{20,28},{24,0},{28,4},{1,9},{5... | collective-permute-start | bytes 2236424 | tf_op jit(solution)/shard_map/ppermute | solution.py:276
  843.0 114.6 %copy-start.57 = (bf16[1,848,896]{2,1,0:T(8,128)(2,1)S(1)}, bf16[1,848,896]{2,1,0:T(8,128)(2,1)}, u32[]{:S(2)}) copy-start(bf16[1,848,896]{2,1,0:T(8,128)(2,1)} %get-tuple-element.166) | copy-start | bytes 4558852
  843.0 114.6 %copy-start.62 = (bf16[848,896]{1,0:T(8,128)(2,1)S(1)}, bf16[848,896]{1,0:T(8,128)(2,1)}, u32[]{:S(2)}) copy-start(bf16[848,896]{1,0:T(8,128)(2,1)} %copy-done.61) | copy-start | bytes 4558852
  962.1 132.1 %collective-permute-start.45 = (bf16[4,848,896]{2,1,0:T(8,128)(2,1)}, bf16[4,848,896]{2,1,0:T(8,128)(2,1)}, u32[]{:S(2)}, u32[]{:S(2)}) collective-permute-start(bf16[4,848,896]{2,1,0:T(8,128)(2,1)} %pad_maximum_fusion.1.refs_0_), channel_id=1, source_target_pairs={{0,4},{4,0},{8,12},{12,8},{16,20},{20,16},{24,28},{28,24},{1,5},{5... | collective-permute-start | bytes 18235400 | tf_op jit(solution)/shard_map/ppermute | solution.py:276
  964.8 48.2 %collective-permute-start.35 = (bf16[1,864,1152]{2,1,0:T(8,128)(2,1)S(1)}, bf16[1,864,1152]{2,1,0:T(8,128)(2,1)S(1)}, u32[]{:S(2)}, u32[]{:S(2)}) collective-permute-start(bf16[1,864,1152]{2,1,0:T(8,128)(2,1)S(1)} %slice.337), channel_id=1, source_target_pairs={{0,8},{4,12},{8,16},{12,20},{16,24},{20,28},{24,0},{28,4},{1,9},{5... | collective-permute-start | bytes 5971976 | tf_op jit(solution)/shard_map/ppermute | solution.py:276
  965.0 12.5 %collective-permute-start.12 = (bf16[128,2048]{1,0:T(8,128)(2,1)S(1)}, bf16[128,2048]{1,0:T(8,128)(2,1)S(1)}, u32[]{:S(2)}, u32[]{:S(2)}) collective-permute-start(bf16[128,2048]{1,0:T(8,128)(2,1)S(1)} %select_bitcast_fusion.14), channel_id=1, source_target_pairs={{0,2},{1,3},{2,0},{3,1},{4,6},{5,7},{6,4},{7,5},{8,10},{9,11},{10,... | collective-permute-start | bytes 1572872 | tf_op jit(solution)/shard_map/ppermute | solution.py:299
  968.3 84.9 %collective-permute-start.36 = (bf16[1,864,1152]{2,1,0:T(8,128)(2,1)S(1)}, bf16[1,864,1152]{2,1,0:T(8,128)(2,1)S(1)}, u32[]{:S(2)}, u32[]{:S(2)}) collective-permute-start(bf16[1,864,1152]{2,1,0:T(8,128)(2,1)S(1)} %slice.339), channel_id=1, source_target_pairs={{0,24},{4,28},{8,0},{12,4},{16,8},{20,12},{24,16},{28,20},{1,25},{... | collective-permute-start | bytes 5971976 | tf_op jit(solution)/shard_map/ppermute | solution.py:276
  1013.0 45.9 %copy-start.14 = (bf16[1,864,1152]{2,1,0:T(8,128)(2,1)}, bf16[1,864,1152]{2,1,0:T(8,128)(2,1)S(1)}, u32[]{:S(2)}) copy-start(bf16[1,864,1152]{2,1,0:T(8,128)(2,1)S(1)} %collective-permute-done.35.refs_4_) | copy-start | bytes 5971972
  (124 other events, 1060.8 us)
Sparse Core Ops, SparseCore 0:
  347.0 228.4 reduce-scatter.1
Sparse Core Ops, SparseCore 1:
  350.3 274.8 all-gather.1

commit v3 on v2

--- a/solution.py
+++ b/solution.py
@@ -35,22 +35,24 @@
 def column(block,h):
     return jnp.sum(jnp.where(lanes(block.shape)==h,block,0.0),axis=1,keepdims=True)
 def causal(C): return rows((C,C))>=lanes((C,C))
-def earlier(C): return (rows((C,C))//MB)>(lanes((C,C))//MB)
-def level(C,size):
+def earlier(C): return (rows((C,C))>>4)>(lanes((C,C))>>4)
+def level(C,b):
     i=rows((C,C)); j=lanes((C,C))
-    return (i//(2*size)==j//(2*size))&((i//size)%2==1)&((j//size)%2==0)
-
-def block_inverse(low,C):
-    eye=jnp.where(rows((C,C))==lanes((C,C)),1.0,0.0)
-    size=MB
-    t=eye-jnp.where(level(C,size),low,0.0)
-    size*=2
-    while size<C:
-        part=split(jnp.where(level(C,size),low,0.0))
-        ts=split(t)
-        t=t-nn3(split(nn3(ts,part)),ts)
-        size*=2
-    return t
+    return ((i>>(b+1))==(j>>(b+1)))&((i>>b)>(j>>b))
+
+def block_inverses(lows,C):
+    b=4
+    mask=level(C,b)
+    ys=[jnp.where(mask,-low,0.0) for low in lows]
+    b+=1
+    while (1<<b)<C:
+        mask=level(C,b)
+        parts=[jnp.where(mask,low,0.0) for low in lows]
+        yb=[y.astype(BF) for y in ys]
+        zs=[p+nn(y,p) for y,p in zip(yb,parts)]
+        ys=[y-(z+nn(z,b2)) for y,z,b2 in zip(ys,zs,yb)]
+        b+=1
+    return ys
 
 def map_kernel(C,k_ref,v_ref,r_ref,t_ref,uw_ref,x_ref,y_ref):
     p=pl.program_id(0)
@@ -58,24 +60,25 @@
     last=y_ref.shape[0]-1
     @pl.when(p==0)
     def _(): y_ref[last]=jnp.zeros((80,LN),BF)
+    units=[(odd,c,pl.ds(c*C,C)) for c in range(N//C) for odd in range(2)]
+    mask=earlier(C)
+    eye=jnp.where(rows((C,C))==lanes((C,C)),1.0,0.0)
+    ks=[head_of(k_ref[sl,:],odd) for odd,c,sl in units]
+    kws=[jnp.concatenate([aug(k),head_of(v_ref[sl,:],odd)-k],axis=1) for k,(odd,c,sl) in zip(ks,units)]
+    krs=[(kw[:,:LN]*column(r_ref[sl,:],2*p+odd)).astype(BF) for kw,(odd,c,sl) in zip(kws,units)]
+    lows=[jnp.where(mask,nt(kw[:,:LN],kr),0.0) for kw,kr in zip(kws,krs)]
+    ys=block_inverses(lows,C)
+    total=[None,None]
+    uws=[kw+nn(y,kw) for y,kw in zip(ys,kws)]
+    xcs=[tn(kr,jnp.where(lanes(uw.shape)<LN,-uw,uw)) for kr,uw in zip(krs,uws)]
+    for (odd,c,sl),y,uw,xc in zip(units,ys,uws,xcs):
+        t_ref[odd,c]=(y+eye).astype(BF)
+        uw_ref[odd,sl,:]=uw.astype(BF)
+        x_ref[odd,c]=xc.astype(BF)
+        total[odd]=xc if total[odd] is None else total[odd]+xc+nn(xc[:,:LN],total[odd])
     for odd in range(2):
         h=2*p+odd
-        total=None
-        for c in range(N//C):
-            sl=pl.ds(c*C,C)
-            k=head_of(k_ref[sl,:],odd)
-            w=head_of(v_ref[sl,:],odd)-k
-            ka=aug(k)
-            r=column(r_ref[sl,:],h)
-            kr=ka*r
-            t=block_inverse(jnp.where(earlier(C),nt(ka,kr),0.0),C)
-            t_ref[odd,c]=t.astype(BF)
-            uw=nn(t,jnp.concatenate([ka,w],axis=1))
-            uw_ref[odd,sl,:]=uw.astype(BF)
-            xc=tn(kr,jnp.where(lanes(uw.shape)<LN,-uw,uw))
-            x_ref[odd,c]=xc.astype(BF)
-            total=xc if total is None else total+xc+nn(xc[:,:LN],total)
-        a=total[:,:LN]; o=total[:,LN:]
+        a=total[odd][:,:LN]; o=total[odd][:,LN:]
         y_ref[h]=pair(a,o)[:80].astype(BF)
         col=jnp.sum(jnp.where(lanes(a.shape)==HW,a,0.0),axis=1,keepdims=True)[:80]
         y_ref[last]=jnp.where(lanes((80,LN))==h,col,y_ref[last].astype(F32)).astype(BF)
@@ -83,6 +86,7 @@
 def local_kernel(C,q_ref,k_ref,r_ref,t_ref,uw_ref,qe_ref,zo_ref,pt_ref,vv_ref):
     p=pl.program_id(0)
     N=q_ref.shape[0]
+    mask=causal(C)
     for c in range(N//C):
         sl=pl.ds(c*C,C)
         offs=[]
@@ -91,7 +95,7 @@
             q=head_of(q_ref[sl,:],odd); qa=aug(q)
             ka=aug(head_of(k_ref[sl,:],odd))
             kr=ka*column(r_ref[sl,:],h)
-            pm=jnp.where(causal(C),nt(qa,kr),0.0)
+            pm=jnp.where(mask,nt(qa,kr),0.0)
             t=t_ref[odd,c]
             puw=nn(pm,uw_ref[odd,sl,:])
             qe_ref[odd,sl,:]=(qa-puw[:,:LN]).astype(BF)
@@ -118,26 +122,31 @@
     N=zo_ref.shape[0]
     segs=y_ref.shape[0]
     seg=seg_ref[0]
-    add=[[None]*(N//C) for _ in range(2)]
-    for odd in range(2):
-        h=2*p+odd
-        s=start_of(is_ref,ib_ref,odd)
-        for j in range(segs-1):
-            at=seg_ref[1+j]
-            a,o=unpack(y_ref[at,odd],yb_ref[at,0],h)
-            s=s+jnp.where(j<seg,1.0,0.0)*(nn(a,s)+o)
-        for c in range(N//C):
-            sl=pl.ds(c*C,C)
-            sb=s.astype(BF)
+    nc=N//C
+    ss=[start_of(is_ref,ib_ref,odd) for odd in range(2)]
+    for j in range(segs-1):
+        at=seg_ref[1+j]
+        on=jnp.where(j<seg,1.0,0.0)
+        for odd in range(2):
+            a,o=unpack(y_ref[at,odd],yb_ref[at,0],2*p+odd)
+            ss[odd]=ss[odd]+on*(nn(a,ss[odd])+o)
+    sbs=[[],[]]
+    for c in range(nc):
+        for odd in range(2):
+            sb=ss[odd].astype(BF)
+            sbs[odd].append(sb)
+            x=x_ref[odd,c]
+            ss[odd]=ss[odd]+nn(x[:,:LN],sb)+x[:,LN:].astype(F32)
+    for c in range(nc):
+        sl=pl.ds(c*C,C)
+        add=[]
+        for odd in range(2):
+            sb=sbs[odd][c]
             s_ref[odd,c]=sb
             uw=uw_ref[odd,sl,:]
             e_ref[odd,sl,:]=(nn(uw[:,:LN],sb)-uw[:,LN:].astype(F32)).astype(BF)
-            add[odd][c]=nn(qe_ref[odd,sl,:],sb)
-            x=x_ref[odd,c]
-            s=s+nn(x[:,:LN],sb)+x[:,LN:].astype(F32)
-    for c in range(N//C):
-        sl=pl.ds(c*C,C)
-        z_ref[sl,:]=zo_ref[sl,:]+pair(add[0][c],add[1][c])
+            add.append(nn(qe_ref[odd,sl,:],sb))
+        z_ref[sl,:]=zo_ref[sl,:]+pair(add[0],add[1])
 
 def state_grad_kernel(C,dz_ref,qe_ref,x_ref,d_ref,dseg_ref):
     N=dz_ref.shape[0]
@@ -156,6 +165,7 @@
 def query_grad_kernel(C,q_ref,k_ref,r_ref,dz_ref,e_ref,s_ref,pt_ref,dq_ref,b_ref,l_ref):
     p=pl.program_id(0)
     N=q_ref.shape[0]
+    mask=causal(C)
     for c in range(N//C):
         sl=pl.ds(c*C,C)
         outs=[]
@@ -165,7 +175,7 @@
             qa=aug(head_of(q_ref[sl,:],odd))
             ka=aug(head_of(k_ref[sl,:],odd))
             kr=ka*column(r_ref[sl,:],h)
-            fu=jnp.where(causal(C),-nt(dzb,e_ref[odd,sl,:]),0.0).astype(BF)
+            fu=jnp.where(mask,-nt(dzb,e_ref[odd,sl,:]),0.0).astype(BF)
             outs.append(dz+nt(dzb,s_ref[odd,c])+nn(fu,kr))
             b_ref[odd,sl,:]=tn(fu,qa).astype(BF)
             l_ref[odd,sl,:]=-tn(pt_ref[odd,c],dzb)
@@ -179,42 +189,47 @@
     @pl.when(p==0)
     def _(): dr_ref[...]=jnp.zeros_like(dr_ref)
     pad=jnp.zeros((LN-80,LN),F32)
-    dks=[[None]*(N//C) for _ in range(2)]
-    lams=[[None]*(N//C) for _ in range(2)]
-    for odd in range(2):
-        h=2*p+odd
-        full=jnp.zeros((LN,LN),F32)
-        g=jnp.zeros((LN,LN),F32)
-        for j in reversed(range(segs)):
-            at=seg_ref[1+j]
-            a,_=unpack(y_ref[at,odd],yb_ref[at,0],h)
+    nc=N//C
+    full=[jnp.zeros((LN,LN),F32) for _ in range(2)]
+    gs=[jnp.zeros((LN,LN),F32) for _ in range(2)]
+    for j in reversed(range(segs)):
+        at=seg_ref[1+j]
+        for odd in range(2):
+            a,_=unpack(y_ref[at,odd],yb_ref[at,0],2*p+odd)
             d=jnp.concatenate([head_of(da_ref[at,0].astype(F32),odd),pad],0)
-            full=full+tn(a,full)+d
-            g=jnp.where(j==seg+1,full,g)
-        gi_ref[odd]=full[:72]
-        for c in reversed(range(N//C)):
-            sl=pl.ds(c*C,C)
-            gb=g.astype(BF)
+            full[odd]=full[odd]+tn(a,full[odd])+d
+            gs[odd]=jnp.where(j==seg+1,full[odd],gs[odd])
+    for odd in range(2): gi_ref[odd]=full[odd][:72]
+    gbs=[[None]*nc for _ in range(2)]
+    for c in reversed(range(nc)):
+        for odd in range(2):
+            gb=gs[odd].astype(BF)
+            gbs[odd][c]=gb
+            gs[odd]=gs[odd]+tn(x_ref[odd,c][:,:LN],gb)+d_ref[odd,c]
+    mask=earlier(C)
+    for c in range(nc):
+        sl=pl.ds(c*C,C)
+        dks=[]; lams=[]
+        for odd in range(2):
+            h=2*p+odd
+            gb=gbs[odd][c]
             ka=aug(head_of(k_ref[sl,:],odd))
             r=column(r_ref[sl,:],h)
             kr=ka*r
             e=e_ref[odd,sl,:]
             lam=l_ref[odd,sl,:]-nn(vv_ref[odd,sl,:],gb)
             lb=lam.astype(BF)
-            hu=jnp.where(earlier(C),-nt(lb,e),0.0).astype(BF)
+            hu=jnp.where(mask,-nt(lb,e),0.0).astype(BF)
             b=b_ref[odd,sl,:].astype(F32)+tn(hu,ka)-nt(e,gb)
-            dks[odd][c]=r*b+nt(lb,s_ref[odd,c])+nn(hu,kr)+lam
-            lams[odd][c]=lam
+            dks.append(r*b+nt(lb,s_ref[odd,c])+nn(hu,kr)+lam)
+            lams.append(lam)
             dr=jnp.sum(ka*b,axis=1,keepdims=True)
             dr_ref[sl,:]=jnp.where(lanes((C,dr_ref.shape[1]))==h,dr,dr_ref[sl,:])
-            g=g+tn(x_ref[odd,c][:,:LN],gb)+d_ref[odd,c]
-    for c in range(N//C):
-        sl=pl.ds(c*C,C)
-        dk_ref[sl,:]=pair(dks[0][c],dks[1][c]).astype(BF)
-        dv_ref[sl,:]=-pair(lams[0][c],lams[1][c]).astype(BF)
+        dk_ref[sl,:]=pair(dks[0],dks[1]).astype(BF)
+        dv_ref[sl,:]=-pair(lams[0],lams[1]).astype(BF)
         dq=dq_ref[sl,:].astype(F32); dg=dg_ref[sl,:].astype(F32)
         for odd in range(2):
-            first=pair(head_of(dq,odd),dks[odd][c]); second=pair(-lams[odd][c],head_of(dg,odd))
+            first=pair(head_of(dq,odd),dks[odd]); second=pair(-lams[odd],head_of(dg,odd))
             pk_ref[odd,sl,:]=jnp.concatenate([first,second],axis=1).astype(BF)
 
 def params(): return pltpu.CompilerParams(dimension_semantics=("arbitrary",),vmem_limit_bytes=VL)
@@ -276,20 +291,25 @@
     return lax.ppermute(v, "seq", pairs)
 
 
-def seq_gather(v):
+def seq_gather(v, *later):
     Z, X = grid_of()
     i = lax.axis_index("seq")
     j = jnp.arange(Z * X, dtype=jnp.int32)
     if (Z, X) != (4, 2):
         return lax.all_gather(v, "seq", axis=0, tiled=False), j
-    both = jnp.stack([v, shift(v, 0, 1)])
+    other = shift(v, 0, 1)
+    if later:
+        other, later = together(other, later)
+    both = jnp.stack([v, other])
     left = shift(both, 1, 0)
     right = shift(both, 3, 0)
     far0 = shift(left[:1], 1, 0)
     far1 = shift(right[1:], 3, 0)
     z, x = i // X, i % X
-    order = ((j // X - z) % Z) * X + (j % X - x) % X
-    return jnp.concatenate([both, right, far0, far1, left]), order
+    every = jnp.concatenate([both, right, far0, far1, left])
+    if later:
+        return every, *later
+    return every, ((j // X - z) % Z) * X + (j % X - x) % X
 
 
 def head_shift(v, dy, dc):
@@ -336,6 +356,10 @@
     return lax.dot_general(a, b, (((ca,), (cb,)), ((), ())), preferred_element_type=F32)
 
 
+def together(*values):
+    return lax.optimization_barrier(values)
+
+
 def at(v, i, axis=0):
     return lax.dynamic_index_in_dim(v, i, axis, keepdims=False)
 
@@ -344,98 +368,76 @@
     return (a.astype(F32) + b.astype(F32)).astype(BF)
 
 
-def pair_reduce(v):
-    x = lax.axis_index("seq") % 2
-    return plus(at(v, x, 1), shift(at(v, 1 - x, 1), 0, 1))
-
-
-def ring_start(v):
-    z = lax.axis_index("seq") // 2
-    v = v.reshape((4, -1) + v.shape[1:])
-    if v.shape[1] == 1:
-        h = v.shape[2] // 32 * 16
-        top, low = v[:, 0, :h], v[:, 0, h:]
-    else:
-        top, low = v[:, 0], v[:, 1]
-    a = shift(at(top, (z + 2) % 4), 1, 0)
-    b = shift(at(low, (z + 2) % 4), 3, 0)
-    return top, low, a, b
-
-
-def ring_end(state, parts):
-    top, low, a, b = state
-    z = lax.axis_index("seq") // 2
-    join = jnp.stack if parts == 2 else lambda p: jnp.concatenate(p, axis=0)
-    up = join([plus(at(top, (z + 1) % 4), a), at(low, (z + 1) % 4)])
-    down = join([at(top, (z + 3) % 4), plus(at(low, (z + 3) % 4), b)])
-    got = shift(up, 1, 0).astype(F32) + shift(down, 3, 0).astype(F32)
-    return (join([at(top, z), at(low, z)]).astype(F32) + got).astype(BF)
-
-
-def split_columns(D):
-    return D * 7 // 16 // LN * LN
-
-
-def result_gather(vc, vd):
-    Z, X = grid_of()
+def slices_kernel(at_ref, g0, u0, h0, g1, u1, h1, x_ref, c_ref, send_ref, keep_ref):
+    rows = g0.shape[0]
+    for g, u, h, out in ((g0, u0, h0, send_ref), (g1, u1, h1, keep_ref)):
+        for t, (left, right) in enumerate(((g, x_ref), (u, x_ref), (h, c_ref))):
+            out[pl.ds(t * rows, rows), :] = dot(left[...], right[...]).astype(BF)
+
+
+def mlp_slices(k, rows, d_gate, d_up, hidden, mlp_group, cot_group):
     i = lax.axis_index("seq")
-    z, x = i // X, i % X
-    h = vc.shape[0] // 32 * 16
-    left, right = shift(vc, 1, 0), shift(vc, 3, 0)
-    both = jnp.stack([vd, shift(vd, 0, 1)])
-    far = jnp.concatenate([shift(left[:h], 1, 0), shift(right[h:], 3, 0)], axis=0)
-    mine = jnp.stack([vc, right, far, left])
-    dl, dr = shift(both, 1, 0), shift(both, 3, 0)
-    other = shift(mine, 0, 1)
-    f0, f1 = shift(dl[:1], 1, 0), shift(dr[1:], 3, 0)
-    k = jnp.arange(4, dtype=jnp.int32)
-    zs = (z + k) % 4
-    at_c = jnp.concatenate([zs * 2 + x, zs * 2 + 1 - x])
-    at_d = jnp.stack([zs * 2 + x, zs * 2 + 1 - x], axis=1).reshape(8)
-    return [mine, other], [both, dr, f0, f1, dl], jnp.concatenate([at_c, at_d]).astype(jnp.int32)
-
-
-def pieces_of(refs):
-    return [(ref, k) for ref in refs for k in range(ref.shape[0])]
-
-
-def finish_kernel(nc, nd, plan, at_ref, *refs):
-    i = pl.program_id(0)
-    outs, scratch = refs[nc + nd : -1], refs[-1]
-
-    def write(group, base):
-        for out, (first, rows, turned) in zip(outs, plan):
-            for slot, (ref, k) in enumerate(pieces_of(group)):
-                start = pl.multiple_of(at_ref[base + slot] * rows, 16)
-                scratch[pl.ds(start, rows), :] = ref[k, pl.ds(first, rows), :].astype(F32)
-            if turned:
-                out[...] = scratch[pl.ds(0, out.shape[1]), :].T
-            else:
-                out[...] = scratch[pl.ds(0, out.shape[0]), :]
-
-    split = pl.num_programs(0) * 7 // 16
-
-    @pl.when(i < split)
-    def _():
-        write(refs[:nc], 0)
-
-    @pl.when(i >= split)
-    def _():
-        write(refs[nc : nc + nd], 8)
-
-
-def finish(gathered, plan, widths):
-    group_c, group_d, slots = gathered
-    D = group_c[0].shape[2] + group_d[0].shape[2]
-    rc, rd = group_c[0].shape[1], group_d[0].shape[1]
-    split = group_c[0].shape[2] // LN
-    in_specs = [
-        pl.BlockSpec((g.shape[0], rc, LN), lambda i, o: (0, 0, jnp.minimum(i, split - 1)))
-        for g in group_c
-    ] + [
-        pl.BlockSpec((g.shape[0], rd, LN), lambda i, o: (0, 0, jnp.maximum(i - split, 0)))
-        for g in group_d
-    ]
+    z, x = i // 2, i % 2
+    to = ((z + k) % 4) * 2
+    which = jnp.stack([to + 1 - x, to + x]).astype(jnp.int32)
+    N, D = mlp_group.shape
+    tile = min(D, 512)
+    act = [pl.BlockSpec((rows, N), lambda j, o, n=n: (o[n], 0)) for n in (0, 1)]
+    col = pl.BlockSpec((N, tile), lambda j, o: (0, j))
+    out = pl.BlockSpec((3 * rows, tile), lambda j, o: (0, j))
+    return pl.pallas_call(
+        slices_kernel,
+        grid_spec=pltpu.PrefetchScalarGridSpec(
+            num_scalar_prefetch=1,
+            grid=(D // tile,),
+            in_specs=[act[0]] * 3 + [act[1]] * 3 + [col, col],
+            out_specs=[out, out],
+        ),
+        out_shape=[jax.ShapeDtypeStruct((3 * rows, D), BF)] * 2,
+        compiler_params=params(),
+        name="mlp_slices",
+    )(which, d_gate, d_up, hidden, d_gate, d_up, hidden, mlp_group, cot_group)
+
+
+def gather1(v):
+    return shift(v, 1, 0), shift(v, 0, 1)
+
+
+def gather2(v, left):
+    return shift(v, 3, 0), shift(left, 0, 1)
+
+
+def gather3(v, left, right):
+    h = v.shape[0] // 32 * 16
+    return shift(left[:h], 1, 0), shift(right[h:], 3, 0), shift(right, 0, 1)
+
+
+def gather4(far_a, far_b):
+    far = jnp.concatenate([far_a, far_b], axis=0)
+    return far, shift(far, 0, 1)
+
+
+def slots():
+    i = lax.axis_index("seq")
+    z, x = i // 2, i % 2
+    zs = (z + jnp.arange(4, dtype=jnp.int32)) % 4
+    return jnp.concatenate([zs * 2 + x, zs * 2 + 1 - x]).astype(jnp.int32)
+
+
+def finish_kernel(plan, at_ref, *refs):
+    pieces, outs, scratch = refs[:8], refs[8:-1], refs[-1]
+    for out, (first, rows, turned) in zip(outs, plan):
+        for slot, ref in enumerate(pieces):
+            start = pl.multiple_of(at_ref[slot] * rows, 16)
+            scratch[pl.ds(start, rows), :] = ref[pl.ds(first, rows), :].astype(F32)
+        if turned:
+            out[...] = scratch[pl.ds(0, out.shape[1]), :].T
+        else:
+            out[...] = scratch[pl.ds(0, out.shape[0]), :]
+
+
+def finish(pieces, plan, widths, name):
+    R, D = pieces[0].shape
     out_specs, out_shape = [], []
     for w, (_, _, turned) in zip(widths, plan):
         if turned:
@@ -445,27 +447,23 @@
             out_specs.append(pl.BlockSpec((w, LN), lambda i, o: (0, i)))
             out_shape.append(jax.ShapeDtypeStruct((w, D), F32))
     return pl.pallas_call(
-        functools.partial(finish_kernel, len(group_c), len(group_d), plan),
+        functools.partial(finish_kernel, plan),
         grid_spec=pltpu.PrefetchScalarGridSpec(
             num_scalar_prefetch=1,
             grid=(D // LN,),
-            in_specs=in_specs,
+            in_specs=[pl.BlockSpec((R, LN), lambda i, o: (0, i))] * 8,
             out_specs=out_specs,
             scratch_shapes=[pltpu.VMEM((8 * max(p[1] for p in plan), LN), F32)],
         ),
         out_shape=out_shape,
         compiler_params=params(),
-        name="finish",
-    )(slots, *group_c, *group_d)
+        name=name,
+    )(slots(), *pieces)
 
 
 def halves(v):
     hi = v.astype(BF)
     return jnp.stack([hi, (v - hi.astype(F32)).astype(BF)])
-
-
-def together(*values):
-    return lax.optimization_barrier(values)
 
 
 def body(
@@ -506,8 +504,6 @@
     normed = (unit_in * norm1_gain).astype(BF)
     group_in = head_gather(normed)
     group_cot = head_gather(out_cotangent)
-    if wide:
-        normed_all = lax.all_gather(normed, everywhere, axis=0, tiled=True)
     key_rows = dot(group_in, key_weight)
     value_rows = dot(group_in, value_weight)
     rate_pre = dot(group_in, rate_weight) + rate_bias
@@ -515,6 +511,9 @@
     rate_rows = rate_sig * rate_scale
     inv, uw, step_maps, seg_map = K["map"](key_rows, value_rows, rate_rows)
     all_maps, order = seq_gather(seg_map)
+    if wide:
+        normed_late, all_maps = together(normed, all_maps)
+        normed_all = lax.all_gather(normed_late, everywhere, axis=0, tiled=True)
     place = jnp.concatenate([seg, order])
     query_rows = dot(group_in, query_weight)
     gate_pre = dot(group_in, gate_weight)
@@ -544,21 +543,9 @@
     d_up_mlp = (d_hidden * silu_gate).astype(BF)
     if wide:
         rows = -(-width // (16 * segs)) * 16
-        fit = lambda v: jnp.pad(v, ((0, rows * segs - width), (0, 0))).reshape(segs, rows, tokens)
-        by_shard = lambda v: v.reshape(segs, -1, v.shape[1])
-        both = jnp.concatenate([fit(d_gate_mlp), fit(d_up_mlp)], axis=1).reshape(-1, tokens)
-        last = fit(hidden).reshape(-1, tokens)
-        c = split_columns(model_width)
-        parts = [
-            jnp.concatenate(
-                [by_shard(dot(both, mlp_group[:, s]).astype(BF)), by_shard(dot(last, group_cot[:, s]).astype(BF))],
-                axis=1,
-            )
-            for s in (slice(0, c), slice(c, None))
-        ]
-        d_gate_mlp, parts[0] = together(d_gate_mlp, parts[0])
-        cross = pair_reduce(parts[0].reshape(4, 2, -1, c))
-        near = ring_start(parts[1])
+        slices = lambda k: mlp_slices(k, rows, d_gate_mlp, d_up_mlp, hidden, mlp_group, group_cot)
+        d_gate_mlp, (sent, kept2) = together(d_gate_mlp, slices(2))
+        got2 = shift(sent, 0, 1)
     d_mlp_input = head_scatter(dot(d_gate_mlp, mlp_gate, 0, 1) + dot(d_up_mlp, mlp_up, 0, 1))
     scaled_mid = d_mlp_input * norm2_gain
     norm2_part = jnp.sum(d_mlp_input * unit_mid, axis=0)
@@ -566,6 +553,13 @@
         scaled_mid - unit_mid * jnp.mean(scaled_mid * unit_mid, axis=-1, keepdims=True)
     )
     d_attn = d_middle.astype(BF)
+    if wide:
+        sent, kept1 = slices(1)
+        d_attn, got2, sent, kept1 = together(d_attn, got2, sent, kept1)
+        got1 = shift(sent, 0, 1)
+        far = plus(kept2, got2)
+        h = far.shape[0] // 32 * 16
+        a_far, b_far = shift(far[:h], 1, 0), shift(far[h:], 3, 0)
     d_attn_group = head_gather(d_attn)
     d_gated = dot(d_attn_group, out_weight, 1, 1)
     out_weight_grad = dot(gated_out, d_attn_group, 0, 0).astype(BF)
@@ -578,23 +572,35 @@
     d_z = inv_scale * (
         d_zhat - back_sums[0][:, None] / model_width - z_hat * (back_sums[1][:, None] / model_width)
     )
+    if wide:
+        d_z, a_far, b_far = together(d_z, a_far, b_far)
     step_grads, seg_grad = K["sgrad"](d_z, q_eff, step_maps)
     if wide:
-        seg_grad, cross, near = together(seg_grad, cross, near)
-    all_grads, _ = seq_gather(seg_grad)
-    if wide:
-        all_grads, near, out_late = together(all_grads, near, out_weight_grad)
-        second = ring_end(near, 2)
-        out_slice = lax.psum_scatter(out_late, "seq", scatter_dimension=0, tiled=True)
+        seg_grad, got1, normed_all = together(seg_grad, got1, normed_all)
+        ahead = plus(kept1, got1)
+        up = jnp.concatenate([plus(ahead[:h], a_far), ahead[h:]], axis=0)
+    if wide:
+        all_grads, (sent3, kept3), (sent0, kept0) = seq_gather(seg_grad, slices(3), slices(0))
+    else:
+        all_grads, _ = seq_gather(seg_grad)
+    if wide:
+        out_slice = lax.psum_scatter(out_weight_grad, "seq", scatter_dimension=0, tiled=True)
+        got3, got0 = shift(sent3, 0, 1), shift(sent0, 0, 1)
+        all_grads, up = together(all_grads, up)
+        from_left = shift(up, 1, 0)
     d_query, b_part, lam_part = K["qgrad"](query_rows, key_rows, rate_rows, d_z, errors, states, pt)
     d_key, d_value, d_rate, init_grad, packed = K["kgrad"](
         place, all_maps, all_maps, all_grads, key_rows, rate_rows, errors, states, vv,
         b_part, lam_part, step_maps, step_grads, d_query, d_gate_pre,
     )
     if wide:
-        d_rate, packed, second = together(d_rate, packed, second)
-        second = pair_reduce(second[None])[0]
-        first = ring_end(ring_start(cross), 1)
+        d_rate, packed, got3, from_left, out_slice = together(
+            d_rate, packed, got3, from_left, out_slice
+        )
+        behind = plus(kept3, got3)
+        down = jnp.concatenate([behind[:h], plus(behind[h:], b_far)], axis=0)
+        first = shift(down, 3, 0).astype(F32) + from_left.astype(F32)
+        first = (first + kept0.astype(F32) + got0.astype(F32)).astype(BF)
     d_rate_pre = (d_rate * rate_scale * rate_sig * (1.0 - rate_sig)).astype(BF)
     scale_part = jnp.sum(d_rate * rate_sig, axis=0)
     total = dot(d_query, query_weight, 1, 1)
@@ -612,7 +618,12 @@
     if wide:
         packed = lax.all_to_all(packed, "seq", split_axis=0, concat_axis=0, tiled=True)
         packed = packed.reshape(segs * tokens, packed.shape[2])
-        own = [dot(packed, v, 0, 0).astype(BF) for v in (normed_all[:, :c], normed_all[:, c:])]
+        left, crossed = gather1(first)
+        left, crossed, packed, first = together(left, crossed, packed, first)
+        own = dot(packed, normed_all, 0, 0).astype(BF)
+        right, crossed_left = gather2(first, left)
+        left, right, crossed_left = together(left, right, crossed_left)
+        far_a, far_b, crossed_right = gather3(first, left, right)
         norm_parts = lax.psum((norm1_part, norm2_part), "head")
         ends = [0]
         extra = [d_rate_pre.reshape(-1)]
@@ -620,21 +631,34 @@
             extra.append(halves(v).reshape(-1))
         for v in extra:
             ends.append(ends[-1] + v.shape[0])
-        cd = model_width - c
-        extra = jnp.concatenate(extra + [jnp.zeros((16 * cd - ends[-1],), BF)]).reshape(16, cd)
-        gathered = result_gather(
-            jnp.concatenate([first, own[0], out_slice[:, :c]], axis=0),
-            jnp.concatenate([second, own[1], out_slice[:, c:], extra], axis=0),
+        extra = jnp.concatenate(extra + [jnp.zeros((16 * model_width - ends[-1],), BF)])
+        second = jnp.concatenate([own, out_slice, extra.reshape(16, model_width)], axis=0)
+        far_a, far_b, crossed_right, second = together(far_a, far_b, crossed_right, second)
+        far, crossed_far = gather4(far_a, far_b)
+        left2, crossed2 = gather1(second)
+        far, crossed_far, left2, crossed2, second = together(
+            far, crossed_far, left2, crossed2, second
         )
+        right2, crossed_left2 = gather2(second, left2)
+        pieces = (first, right, far, left, crossed, crossed_right, crossed_far, crossed_left)
+        plan = tuple((t * rows, rows, False) for t in range(3))
+        mlp_sums = finish(pieces, plan, (width,) * 3, "mlp_finish")
+        left2, right2, crossed_left2 = together(left2, right2, crossed_left2)
+        far_a, far_b, crossed_right2 = gather3(second, left2, right2)
+        far_a, far_b, crossed_right2, mlp_sums = together(far_a, far_b, crossed_right2, mlp_sums)
+        gate_sum, up_sum, down_sum = mlp_sums
+        far2, crossed_far2 = gather4(far_a, far_b)
         full = segs * HW
-        first_row = 3 * rows
-        plan = tuple((t * rows, rows, False) for t in range(3))
-        plan += tuple((first_row + t * HW, HW, t < 4) for t in range(5))
-        sums = finish(gathered, plan, (width,) * 3 + (full,) * 5)
-        gate_sum, up_sum, down_sum, query_sum, key_sum, value_sum, pre_sum, out_sum = sums
+        pieces = (
+            second, right2, far2, left2, crossed2, crossed_right2, crossed_far2, crossed_left2
+        )
+        plan = tuple((t * HW, HW, t < 4) for t in range(5))
+        query_sum, key_sum, value_sum, pre_sum, out_sum = finish(
+            pieces, plan, (full,) * 5, "head_finish"
+        )
         gate_sum, up_sum = gate_sum.T, up_sum.T
-        shared = jnp.concatenate([g[:, -16:] for g in gathered[1]], axis=0).reshape(segs, -1)
-        shared = shared[jnp.argsort(gathered[2][segs:])]
+        shared = jnp.stack([v[-16:] for v in pieces]).reshape(segs, -1)
+        shared = shared[jnp.argsort(slots())]
         from_all = [shared[:, s:e] for s, e in zip(ends[:-1], ends[1:])]
         d_rate_all = from_all[0].reshape(segs * tokens, local_heads)
         totals = [jnp.sum(v.astype(F32).reshape(2 * segs, -1), axis=0) for v in from_all[1:]]

time: 1140 us -> 983 us (0.86)
  waiting for transfers between devices: 659 us -> 483 us
  starting transfers between devices: 74.6 us -> 118 us
  matrix products: 100 us -> 77.2 us
    ppermute x30 -> x34, waiting for transfers between devices: 576 us -> 311 us  [shift(): return lax.ppermute(v, 'seq', pairs)]
    all_to_all x1, waiting for transfers between devices: 9.91 us -> 71.5 us  [body(): lax.all_to_all(packed, 'seq', split_axis=0, concat_axis=0, tiled=True)]
    ppermute x30 -> x34, starting transfers between devices: 54.6 us -> 97.6 us  [shift(): return lax.ppermute(v, 'seq', pairs)]
    pallas_call x1 -> x6, Pallas kernels: 30.1 us -> 65 us  [the longest x2 39.3 us: finish(): pl.pallas_call(functools.partial(finish_kernel, plan), grid_spec=pltpu.Pr...]
    dot_general x26 -> x21, matrix products: 100 us -> 77.2 us  [dot(): lax.dot_general(a, b, (((ca,), (cb,)), ((), ())), preferred_element_type=...]
    pallas_call x1, Pallas kernels: 32.1 us -> 11 us  [body(): inv, uw, step_maps, seg_map = K['map'](key_rows, value_rows, rate_rows)]
    ppermute x16, waiting for transfers between devices: 66.8 us -> 84.9 us  [head_shift(): return lax.ppermute(v, 'head', pairs)]
    another operation x11 -> x6, other arithmetic: 17.4 us -> 0.36 us  [the longest x4 0.3 us: mlp_slices(): which = jnp.stack([to + 1 - x, to + x]).astype(jnp.int32)]
  transfers between devices with their start and end apart: 49 -> 53, of which waited for: 32 -> 35; matrix products, arithmetic and copies ran while one was open for 13% -> 15% of each run, Pallas kernels for 5% -> 10%
where the time goes in v3:
time: 983 us; the launch traced here: 973 us
  waiting for transfers between devices  483 us (49%)
  Pallas kernels  131 us (13%)
  starting transfers between devices  118 us (12%)
  matrix products  77.2 us (8%)
  other arithmetic  70.1 us (7%)
  local copies, waits for them, and re-layouts  51.1 us (5%)
  blocking collectives  24.6 us (3%)
  between operations  17.7 us (2%)
    ppermute x34, waiting for transfers between devices, shift(): return lax.ppermute(v, 'seq', pairs)  311 us
    ppermute x34, starting transfers between devices, shift(): return lax.ppermute(v, 'seq', pairs)  97.6 us
    ppermute x16, waiting for transfers between devices, head_shift(): return lax.ppermute(v, 'head', pairs)  84.9 us
    dot_general x21, matrix products, dot(): lax.dot_general(a, b, (((ca,), (cb,)), ((), ())), preferred_element_type=...  77.2 us
    all_to_all x1, waiting for transfers between devices, body(): lax.all_to_all(packed, 'seq', split_axis=0, concat_axis=0, tiled=True)  71.5 us
    pallas_call x2, Pallas kernels, finish(): pl.pallas_call(functools.partial(finish_kernel, plan), grid_spec=pltpu.Pr...  39.3 us
    unnamed x272, local copies, waits for them, and re-layouts  36 us
    pallas_call x4, Pallas kernels, mlp_slices(): pl.pallas_call(slices_kernel, grid_spec=pltpu.PrefetchScalarGridSpec(num_...  25.7 us
  transfers between devices with their start and end apart: 53, of which 35 were waited for; matrix products, arithmetic and copies ran while one was open for 15% of the time, Pallas kernels for 10%

profile of v3, /device:TPU:0, one launch (start us, length us, event | category | flops | bytes accessed | tf_op | source)
XLA Modules:
  0.0 972.7 jit_solution(5918680546974391452)
XLA Ops:
  15.0 10.7 %collective-permute-done = bf16[128,2048]{1,0:T(8,128)(2,1)S(1)} collective-permute-done((bf16[128,2048]{1,0:T(8,128)(2,1)S(1)}, bf16[128,2048]{1,0:T(8,128)(2,1)S(1)}, u32[]{:S(2)}, u32[]{:S(2)}) %collective-permute-start) | collective-permute-done | bytes 524320 | tf_op jit(solution)/shard_map/ppermute | solution.py:319
  38.7 11.0 %segment_maps.1 = (bf16[8,4,128,128]{3,2,1,0:T(8,128)(2,1)S(1)}, bf16[8,512,256]{2,1,0:T(8,128)(2,1)S(1)}, bf16[8,4,128,256]{3,2,1,0:T(8,128)(2,1)}, bf16[9,80,128]{2,1,0:T(8,128)(2,1)S(1)}) custom-call(f32[512,512]{1,0:T(8,128)S(1)} %fusion.50.k_ref, f32[512,512]{1,0:T(8,128)S(1)} %fusion.49.v_ref, f32[512,8]{1,0:T(8,128)S(1)} %get-tuple-element.263.r_ref), custom_call_target="tpu_custom_call" | custom-call | tf_op jit(solution)/shard_map/segment_maps/pallas_call | solution.py:512
  53.8 5.0 collective-permute-done.2
  63.4 8.8 collective-permute-done.4
  73.0 5.9 collective-permute-done.3
  78.9 3.1 collective-permute-start.6
  88.7 3.5 fusion.48.q_ref
  92.2 8.2 local_parts.1
  102.5 9.2 forward_states.1
  114.0 6.5 all-reduce.2
  120.6 4.7 multiply_convert_fusion.3
  132.0 9.9 %collective-permute-done.13 = bf16[128,2048]{1,0:T(8,128)(2,1)} collective-permute-done((bf16[128,2048]{1,0:T(8,128)(2,1)}, bf16[128,2048]{1,0:T(8,128)(2,1)}, u32[]{:S(2)}, u32[]{:S(2)}) %collective-permute-start.13) | collective-permute-done | bytes 524320 | tf_op jit(solution)/shard_map/ppermute | solution.py:319
  143.4 9.5 collective-permute-done.8
  159.0 21.8 %collective-permute-done.9 = bf16[128,2048]{1,0:T(8,128)(2,1)S(1)} collective-permute-done((bf16[128,2048]{1,0:T(8,128)(2,1)S(1)}, bf16[128,2048]{1,0:T(8,128)(2,1)S(1)}, u32[]{:S(2)}, u32[]{:S(2)}) %collective-permute-start.9) | collective-permute-done | bytes 524320 | tf_op jit(solution)/shard_map/ppermute | solution.py:319
  185.5 3.1 convolution_bitcast_fusion.1
  188.7 3.2 convolution_bitcast_fusion.2
  191.9 6.0 multiply_convert_fusion
  197.9 6.7 mlp_slices.4
  204.6 5.4 fusion.54
  210.1 3.8 add_convert_fusion.5
  224.1 6.4 mlp_slices.5
  230.5 3.4 collective-permute-done.16
  237.8 26.0 %collective-permute-done.17 = bf16[528,2048]{1,0:T(8,128)(2,1)} collective-permute-done((bf16[528,2048]{1,0:T(8,128)(2,1)}, bf16[528,2048]{1,0:T(8,128)(2,1)}, u32[]{:S(2)}, u32[]{:S(2)}) %collective-permute-start.17) | collective-permute-done | bytes 2162720 | tf_op jit(solution)/shard_map/ppermute | solution.py:291
  266.1 11.7 %collective-permute-done.18 = bf16[128,2048]{1,0:T(8,128)(2,1)S(1)} collective-permute-done((bf16[128,2048]{1,0:T(8,128)(2,1)S(1)}, bf16[128,2048]{1,0:T(8,128)(2,1)S(1)}, u32[]{:S(2)}, u32[]{:S(2)}) %collective-permute-start.18) | collective-permute-done | bytes 524320 | tf_op jit(solution)/shard_map/ppermute | solution.py:319
  281.9 6.3 mlp_slices.7
  288.2 6.4 mlp_slices.6
  306.4 5.0 multiply_reduce_fusion.1
  311.5 7.2 all-reduce.1
  320.3 28.8 %collective-permute-done.20 = bf16[256,2048]{1,0:T(8,128)(2,1)} collective-permute-done((bf16[256,2048]{1,0:T(8,128)(2,1)}, bf16[256,2048]{1,0:T(8,128)(2,1)}, u32[]{:S(2)}, u32[]{:S(2)}) %collective-permute-start.20) | collective-permute-done | bytes 1048608 | tf_op jit(solution)/shard_map/ppermute | solution.py:291
  349.1 5.6 state_grads.1
  358.7 3.1 add_convert_fusion.2
  370.4 14.4 %collective-permute-done.25 = bf16[2,4,80,128]{3,2,1,0:T(8,128)(2,1)S(1)} collective-permute-done((bf16[2,4,80,128]{3,2,1,0:T(8,128)(2,1)S(1)}, bf16[2,4,80,128]{3,2,1,0:T(8,128)(2,1)S(1)}, u32[]{:S(2)}, u32[]{:S(2)}) %collective-permute-start.25) | collective-permute-done | bytes 163872 | tf_op jit(solution)/shard_map/ppermute | solution.py:291
  384.8 3.9 collective-permute-start.27
  388.7 3.3 collective-permute-done.26
  395.2 9.1 query_grads.1
  406.3 23.1 %key_grads.1 = (bf16[512,512]{1,0:T(8,128)(2,1)S(1)}, bf16[512,512]{1,0:T(8,128)(2,1)S(1)}, f32[512,8]{1,0:T(8,128)S(1)}, f32[8,72,128]{2,1,0:T(8,128)S(1)}, bf16[8,512,256]{2,1,0:T(8,128)(2,1)}) custom-call(s32[9]{0:T(128)S(1)} %pad_add_fusion.seg_ref, bf16[8,9,80,128]{3,2,1,0:T(8,128)(2,1)} %constant_dynamic-update-slice_fusion.y_ref.yb_ref, ...), custom_call_target="tpu_custom_call" | custom-call | tf_op jit(solution)/shard_map/key_grads/pallas_call | solution.py:592
  429.4 15.6 %reduce-scatter.2.cloned.1.call-done = bf16[64,2048]{1,0:T(8,128)(2,1)} async-done(((bf16[512,2048]{1,0:T(8,128)(2,1)}), bf16[64,2048]{1,0:T(8,128)(2,1)}) %reduce-scatter.2.cloned.1.call-update) | async-done | bytes 262160 | tf_op jit(solution)/shard_map/reduce_scatter | solution.py:587
  445.1 6.5 collective-permute-done.29
  451.6 3.1 add_convert_fusion.1
  459.4 3.3 fusion.55
  462.7 4.3 all-to-all-start
  471.4 5.2 collective-permute-done.33
  476.6 31.7 %collective-permute-done.32 = bf16[528,2048]{1,0:T(8,128)(2,1)} collective-permute-done((bf16[528,2048]{1,0:T(8,128)(2,1)}, bf16[528,2048]{1,0:T(8,128)(2,1)}, u32[]{:S(2)}, u32[]{:S(2)}) %collective-permute-start.32) | collective-permute-done | bytes 2162720 | tf_op jit(solution)/shard_map/ppermute | solution.py:291
  508.3 4.7 add_convert_fusion.refs_0_
  515.1 5.5 collective-permute-start.35
  527.9 71.5 %all-to-all-done = bf16[8,512,256]{2,1,0:T(8,128)(2,1)} async-done(((bf16[8,512,256]{2,1,0:T(8,128)(2,1)}), bf16[8,512,256]{2,1,0:T(8,128)(2,1)}, u32[]{:S(2)}, u32[]{:S(2)}) %all-to-all-start) | async-done | bytes 2097184 | tf_op jit(solution)/shard_map/all_to_all | solution.py:619
  605.3 11.3 %collective-permute-done.31 = bf16[128,2048]{1,0:T(8,128)(2,1)S(1)} collective-permute-done((bf16[128,2048]{1,0:T(8,128)(2,1)}, bf16[128,2048]{1,0:T(8,128)(2,1)S(1)}, u32[]{:S(2)}, u32[]{:S(2)}) %collective-permute-start.31) | collective-permute-done | bytes 524320 | tf_op jit(solution)/shard_map/ppermute | solution.py:319
  616.6 3.2 fusion.28
  619.8 10.9 %all-reduce = (f32[2048]{0:T(1024)S(1)}, f32[2048]{0:T(1024)S(1)}) all-reduce(f32[2048]{0:T(1024)S(1)} %get-tuple-element.203, f32[2048]{0:T(1024)S(1)} %copy-done.90), channel_id=1, replica_groups=mesh['seq'=8,'head'=4] {'head'}, use_global_device_ids=true, to_apply=%region_17.18 | all-reduce | flops 4096 | bytes 32768 | tf_op jit(solution)/shard_map/psum | solution.py:627
  630.7 16.2 %collective-permute-done.36.refs_1_ = bf16[528,2048]{1,0:T(8,128)(2,1)} collective-permute-done((bf16[528,2048]{1,0:T(8,128)(2,1)S(1)}, bf16[528,2048]{1,0:T(8,128)(2,1)}, u32[]{:S(2)}, u32[]{:S(2)}) %collective-permute-start.36) | collective-permute-done | bytes 2162720 | tf_op jit(solution)/shard_map/ppermute | solution.py:291
  647.2 22.2 %collective-permute-start.40 = (bf16[528,2048]{1,0:T(8,128)(2,1)}, bf16[528,2048]{1,0:T(8,128)(2,1)}, u32[]{:S(2)}, u32[]{:S(2)}) collective-permute-start(bf16[528,2048]{1,0:T(8,128)(2,1)} %collective-permute-done.36.refs_1_), channel_id=1, source_target_pairs={{0,4},{4,0},{8,12},{12,8},{16,20},{20,16},{24,28},{28,24},{1,5},{5... | collective-permute-start | bytes 6488072 | tf_op jit(solution)/shard_map/ppermute | solution.py:291
  671.8 27.7 %collective-permute-start.39 = (bf16[272,2048]{1,0:T(8,128)(2,1)S(1)}, bf16[272,2048]{1,0:T(8,128)(2,1)S(1)}, u32[]{:S(2)}, u32[]{:S(2)}) collective-permute-start(bf16[272,2048]{1,0:T(8,128)(2,1)S(1)} %slice.261), channel_id=1, source_target_pairs={{0,24},{4,28},{8,0},{12,4},{16,8},{20,12},{24,16},{28,20},{1,25},{... | collective-permute-start | bytes 3342344 | tf_op jit(solution)/shard_map/ppermute | solution.py:291
  701.0 11.0 %convolution_convert_fusion.3 = bf16[256,2048]{1,0:T(8,128)(2,1)S(1)} fusion(bf16[4096,256]{1,0:T(8,128)(2,1)} %bitcast.61, bf16[4096,2048]{1,0:T(8,128)(2,1)} %all-gather.2.cloned.1.call-done), kind=kOutput, calls=%fused_computation.21 | convolution fusion | flops 4295491584 | bytes 19922944 | tf_op jit(solution)/shard_map/dot_general | solution.py:356
  712.2 33.3 %collective-permute-done.38 = bf16[256,2048]{1,0:T(8,128)(2,1)S(1)} collective-permute-done((bf16[256,2048]{1,0:T(8,128)(2,1)S(1)}, bf16[256,2048]{1,0:T(8,128)(2,1)S(1)}, u32[]{:S(2)}, u32[]{:S(2)}) %collective-permute-start.38) | collective-permute-done | bytes 1048608 | tf_op jit(solution)/shard_map/ppermute | solution.py:291
  748.3 3.7 convolution_convert_fusion.2
  758.4 27.1 %collective-permute-done.42.refs_3_ = bf16[336,2048]{1,0:T(8,128)(2,1)} collective-permute-done((bf16[336,2048]{1,0:T(8,128)(2,1)S(1)}, bf16[336,2048]{1,0:T(8,128)(2,1)}, u32[]{:S(2)}, u32[]{:S(2)}) %collective-permute-start.42) | collective-permute-done | bytes 1376288 | tf_op jit(solution)/shard_map/ppermute | solution.py:291
  785.6 38.9 %collective-permute-done.43.refs_4_ = bf16[336,2048]{1,0:T(8,128)(2,1)} collective-permute-done((bf16[336,2048]{1,0:T(8,128)(2,1)S(1)}, bf16[336,2048]{1,0:T(8,128)(2,1)}, u32[]{:S(2)}, u32[]{:S(2)}) %collective-permute-start.43) | collective-permute-done | bytes 1376288 | tf_op jit(solution)/shard_map/ppermute | solution.py:291
  824.4 5.5 collective-permute-start.44
  837.2 21.5 %collective-permute-done.44.refs_1_ = bf16[336,2048]{1,0:T(8,128)(2,1)S(1)} collective-permute-done((bf16[336,2048]{1,0:T(8,128)(2,1)S(1)}, bf16[336,2048]{1,0:T(8,128)(2,1)S(1)}, u32[]{:S(2)}, u32[]{:S(2)}) %collective-permute-start.44) | collective-permute-done | bytes 1376288 | tf_op jit(solution)/shard_map/ppermute | solution.py:291
  861.8 3.6 fusion.27
  871.2 21.1 %mlp_finish.1 = (f32[1376,2048]{1,0:T(8,128)}, f32[1376,2048]{1,0:T(8,128)}, f32[1376,2048]{1,0:T(8,128)}) custom-call(s32[8]{0:T(128)S(1)} %pad_add_fusion.5.at_ref, bf16[528,2048]{1,0:T(8,128)(2,1)S(1)} %add_convert_fusion.refs_0_, bf16[528,2048]{1,0:T(8,128)(2,1)} %collective-permute-done.36.refs_1_, ...), custom_call_target="tpu_custom_call" | custom-call | tf_op jit(solution)/shard_map/mlp_finish/pallas_call | solution.py:449
  899.1 27.1 %collective-permute-done.49.refs_6_ = bf16[336,2048]{1,0:T(8,128)(2,1)S(1)} collective-permute-done((bf16[336,2048]{1,0:T(8,128)(2,1)S(1)}, bf16[336,2048]{1,0:T(8,128)(2,1)S(1)}, u32[]{:S(2)}, u32[]{:S(2)}) %collective-permute-start.49) | collective-permute-done | bytes 1376288 | tf_op jit(solution)/shard_map/ppermute | solution.py:291
  931.2 8.7 fusion.59
  946.9 18.1 %head_finish.1 = (f32[2048,512]{1,0:T(8,128)}, f32[2048,512]{1,0:T(8,128)}, f32[2048,512]{1,0:T(8,128)}, f32[2048,512]{1,0:T(8,128)}, f32[512,2048]{1,0:T(8,128)}) custom-call(s32[8]{0:T(128)S(1)} %pad_add_fusion.5.at_ref, bf16[336,2048]{1,0:T(8,128)(2,1)S(1)} %pad_maximum_fusion.6.refs_0_, bf16[336,2048]{1,0:T(8,128)(2,1)S(1)} %copy-done.24, ...), custom_call_target="tpu_custom_call" | custom-call | tf_op jit(solution)/shard_map/head_finish/pallas_call | solution.py:449
  (485 shorter events, 182.6 us)
Async XLA Ops:
  8.0 117.3 %copy-start = (bf16[512,2048]{1,0:T(8,128)(2,1)S(1)}, bf16[512,2048]{1,0:T(8,128)(2,1)}, u32[]{:S(2)}) copy-start(bf16[512,2048]{1,0:T(8,128)(2,1)} %param.32) | copy-start | bytes 6291460
  8.0 350.7 %all-gather.2.cloned.1.call-start = ((), (), s32[]{:S(2)}) async-start(), calls=%async_computation.2 | async-start | bytes 17301504 | tf_op jit(solution)/shard_map/all_gather | solution.py:516
  10.7 15.0 %collective-permute-start = (bf16[128,2048]{1,0:T(8,128)(2,1)S(1)}, bf16[128,2048]{1,0:T(8,128)(2,1)S(1)}, u32[]{:S(2)}, u32[]{:S(2)}) collective-permute-start(bf16[128,2048]{1,0:T(8,128)(2,1)S(1)} %fusion.23), channel_id=1, source_target_pairs={{0,2},{1,3},{2,0},{3,1},{4,6},{5,7},{6,4},{7,5},{8,10},{9,11},{10,... | collective-permute-start | bytes 1572872 | tf_op jit(solution)/shard_map/ppermute | solution.py:319
  27.5 3.0 collective-permute-start.1
  52.1 6.7 collective-permute-start.2
  58.8 13.4 %collective-permute-start.4 = (bf16[2,9,80,128]{3,2,1,0:T(8,128)(2,1)S(1)}, bf16[2,9,80,128]{3,2,1,0:T(8,128)(2,1)S(1)}, u32[]{:S(2)}, u32[]{:S(2)}) collective-permute-start(bf16[2,9,80,128]{3,2,1,0:T(8,128)(2,1)S(1)} %pad_maximum_fusion.11), channel_id=1, source_target_pairs={{0,8},{4,12},{8,16},{12,20},{16,24},{20,28},{24,0},{28,4},{1,9},{5... | collective-permute-start | bytes 1105928 | tf_op jit(solution)/shard_map/ppermute | solution.py:291
  60.6 18.3 %collective-permute-start.3 = (bf16[2,9,80,128]{3,2,1,0:T(8,128)(2,1)S(1)}, bf16[2,9,80,128]{3,2,1,0:T(8,128)(2,1)S(1)}, u32[]{:S(2)}, u32[]{:S(2)}) collective-permute-start(bf16[2,9,80,128]{3,2,1,0:T(8,128)(2,1)S(1)} %pad_maximum_fusion.11), channel_id=1, source_target_pairs={{0,24},{4,28},{8,0},{12,4},{16,8},{20,12},{24,16},{28,20},{1,25},{... | collective-permute-start | bytes 1105928 | tf_op jit(solution)/shard_map/ppermute | solution.py:291
  72.2 12.6 %collective-permute-start.5 = (bf16[1,9,80,128]{3,2,1,0:T(8,128)(2,1)S(1)}, bf16[1,9,80,128]{3,2,1,0:T(8,128)(2,1)S(1)}, u32[]{:S(2)}, u32[]{:S(2)}) collective-permute-start(bf16[1,9,80,128]{3,2,1,0:T(8,128)(2,1)S(1)} %slice.286), channel_id=1, source_target_pairs={{0,8},{4,12},{8,16},{12,20},{16,24},{20,28},{24,0},{28,4},{1,9},{5... | collective-permute-start | bytes 552968 | tf_op jit(solution)/shard_map/ppermute | solution.py:291
  78.9 8.2 collective-permute-start.6
  88.5 356.5 %reduce-scatter.2.cloned.1.call-start = ((), (), s32[]{:S(2)}) async-start(), calls=%async_computation.3 | async-start | bytes 2359296 | tf_op jit(solution)/shard_map/reduce_scatter | solution.py:587
  126.8 2.7 collective-permute-start.7
  126.8 15.1 %collective-permute-start.13 = (bf16[128,2048]{1,0:T(8,128)(2,1)}, bf16[128,2048]{1,0:T(8,128)(2,1)}, u32[]{:S(2)}, u32[]{:S(2)}) collective-permute-start(bf16[128,2048]{1,0:T(8,128)(2,1)} %param.37), channel_id=1, source_target_pairs={{0,2},{1,3},{2,0},{3,1},{4,6},{5,7},{6,4},{7,5},{8,10},{9,11},{10,... | collective-permute-start | bytes 1572872 | tf_op jit(solution)/shard_map/ppermute | solution.py:319
  131.0 21.9 %collective-permute-start.8 = (bf16[128,2048]{1,0:T(8,128)(2,1)}, bf16[128,2048]{1,0:T(8,128)(2,1)}, u32[]{:S(2)}, u32[]{:S(2)}) collective-permute-start(bf16[128,2048]{1,0:T(8,128)(2,1)} %select_bitcast_fusion.19), channel_id=1, source_target_pairs={{0,2},{1,3},{2,0},{3,1},{4,6},{5,7},{6,4},{7,5},{8,10},{9,11},{10,... | collective-permute-start | bytes 1572872 | tf_op jit(solution)/shard_map/ppermute | solution.py:319
  143.3 14.1 %collective-permute-start.14 = (bf16[2,128,2048]{2,1,0:T(8,128)(2,1)S(1)}, bf16[2,128,2048]{2,1,0:T(8,128)(2,1)S(1)}, u32[]{:S(2)}, u32[]{:S(2)}) collective-permute-start(bf16[2,128,2048]{2,1,0:T(8,128)(2,1)S(1)} %pad_maximum_fusion.9), channel_id=1, source_target_pairs={{0,1},{1,0},{2,3},{3,2},{4,5},{5,4},{6,7},{7,6},{8,9},{9,8},{10,11... | collective-permute-start | bytes 3145736 | tf_op jit(solution)/shard_map/ppermute | solution.py:319
  155.1 25.7 %collective-permute-start.9 = (bf16[128,2048]{1,0:T(8,128)(2,1)S(1)}, bf16[128,2048]{1,0:T(8,128)(2,1)S(1)}, u32[]{:S(2)}, u32[]{:S(2)}) collective-permute-start(bf16[128,2048]{1,0:T(8,128)(2,1)S(1)} %multiply_convert_fusion.2), channel_id=1, source_target_pairs={{0,2},{1,3},{2,0},{3,1},{4,6},{5,7},{6,4},{7,5},{8,10},{9,11},{10,... | collective-permute-start | bytes 1572872 | tf_op jit(solution)/shard_map/ppermute | solution.py:319
  180.9 2.7 collective-permute-start.10
  214.0 2.7 collective-permute-start.15
  214.2 49.6 %collective-permute-start.17 = (bf16[528,2048]{1,0:T(8,128)(2,1)}, bf16[528,2048]{1,0:T(8,128)(2,1)}, u32[]{:S(2)}, u32[]{:S(2)}) collective-permute-start(bf16[528,2048]{1,0:T(8,128)(2,1)} %get-tuple-element.120), channel_id=1, source_target_pairs={{0,4},{4,0},{8,12},{12,8},{16,20},{20,16},{24,28},{28,24},{1,5},{5... | collective-permute-start | bytes 6488072 | tf_op jit(solution)/shard_map/ppermute | solution.py:291
  219.1 14.8 %collective-permute-start.16 = (bf16[128,2048]{1,0:T(8,128)(2,1)}, bf16[128,2048]{1,0:T(8,128)(2,1)}, u32[]{:S(2)}, u32[]{:S(2)}) collective-permute-start(bf16[128,2048]{1,0:T(8,128)(2,1)} %select_bitcast_fusion.9), channel_id=1, source_target_pairs={{0,2},{1,3},{2,0},{3,1},{4,6},{5,7},{6,4},{7,5},{8,10},{9,11},{10,... | collective-permute-start | bytes 1572872 | tf_op jit(solution)/shard_map/ppermute | solution.py:319
  263.8 14.0 %collective-permute-start.18 = (bf16[128,2048]{1,0:T(8,128)(2,1)S(1)}, bf16[128,2048]{1,0:T(8,128)(2,1)S(1)}, u32[]{:S(2)}, u32[]{:S(2)}) collective-permute-start(bf16[128,2048]{1,0:T(8,128)(2,1)S(1)} %fusion.47), channel_id=1, source_target_pairs={{0,2},{1,3},{2,0},{3,1},{4,6},{5,7},{6,4},{7,5},{8,10},{9,11},{10,... | collective-permute-start | bytes 1572872 | tf_op jit(solution)/shard_map/ppermute | solution.py:319
  279.0 23.7 %collective-permute-start.19 = (bf16[2,128,2048]{2,1,0:T(8,128)(2,1)}, bf16[2,128,2048]{2,1,0:T(8,128)(2,1)}, u32[]{:S(2)}, u32[]{:S(2)}) collective-permute-start(bf16[2,128,2048]{2,1,0:T(8,128)(2,1)} %pad_maximum_fusion.10), channel_id=1, source_target_pairs={{0,1},{1,0},{2,3},{3,2},{4,5},{5,4},{6,7},{7,6},{8,9},{9,8},{10,11... | collective-permute-start | bytes 3145736 | tf_op jit(solution)/shard_map/ppermute | solution.py:319
  299.2 49.9 %collective-permute-start.21 = (bf16[272,2048]{1,0:T(8,128)(2,1)}, bf16[272,2048]{1,0:T(8,128)(2,1)}, u32[]{:S(2)}, u32[]{:S(2)}) collective-permute-start(bf16[272,2048]{1,0:T(8,128)(2,1)} %slice.313), channel_id=1, source_target_pairs={{0,24},{4,28},{8,0},{12,4},{16,8},{20,12},{24,16},{28,20},{1,25},{... | collective-permute-start | bytes 3342344 | tf_op jit(solution)/shard_map/ppermute | solution.py:291
  301.0 48.1 %collective-permute-start.20 = (bf16[256,2048]{1,0:T(8,128)(2,1)}, bf16[256,2048]{1,0:T(8,128)(2,1)}, u32[]{:S(2)}, u32[]{:S(2)}) collective-permute-start(bf16[256,2048]{1,0:T(8,128)(2,1)} %slice.312), channel_id=1, source_target_pairs={{0,8},{4,12},{8,16},{12,20},{16,24},{20,28},{24,0},{28,4},{1,9},{5... | collective-permute-start | bytes 3145736 | tf_op jit(solution)/shard_map/ppermute | solution.py:291
  301.2 57.5 %collective-permute-start.22 = (bf16[528,2048]{1,0:T(8,128)(2,1)}, bf16[528,2048]{1,0:T(8,128)(2,1)}, u32[]{:S(2)}, u32[]{:S(2)}) collective-permute-start(bf16[528,2048]{1,0:T(8,128)(2,1)} %get-tuple-element.132), channel_id=1, source_target_pairs={{0,4},{4,0},{8,12},{12,8},{16,20},{20,16},{24,28},{28,24},{1,5},{5... | collective-permute-start | bytes 6488072 | tf_op jit(solution)/shard_map/ppermute | solution.py:291
  361.9 4.7 collective-permute-start.23
  366.6 18.1 %collective-permute-start.24 = (bf16[2,4,80,128]{3,2,1,0:T(8,128)(2,1)S(1)}, bf16[2,4,80,128]{3,2,1,0:T(8,128)(2,1)S(1)}, u32[]{:S(2)}, u32[]{:S(2)}) collective-permute-start(bf16[2,4,80,128]{3,2,1,0:T(8,128)(2,1)S(1)} %pad_maximum_fusion.14), channel_id=1, source_target_pairs={{0,24},{4,28},{8,0},{12,4},{16,8},{20,12},{24,16},{28,20},{1,25},{... | collective-permute-start | bytes 491528 | tf_op jit(solution)/shard_map/ppermute | solution.py:291
  368.3 16.4 %collective-permute-start.25 = (bf16[2,4,80,128]{3,2,1,0:T(8,128)(2,1)S(1)}, bf16[2,4,80,128]{3,2,1,0:T(8,128)(2,1)S(1)}, u32[]{:S(2)}, u32[]{:S(2)}) collective-permute-start(bf16[2,4,80,128]{3,2,1,0:T(8,128)(2,1)S(1)} %pad_maximum_fusion.14), channel_id=1, source_target_pairs={{0,8},{4,12},{8,16},{12,20},{16,24},{20,28},{24,0},{28,4},{1,9},{5... | collective-permute-start | bytes 491528 | tf_op jit(solution)/shard_map/ppermute | solution.py:291
  368.7 76.4 %collective-permute-start.28 = (bf16[528,2048]{1,0:T(8,128)(2,1)}, bf16[528,2048]{1,0:T(8,128)(2,1)}, u32[]{:S(2)}, u32[]{:S(2)}) collective-permute-start(bf16[528,2048]{1,0:T(8,128)(2,1)} %get-tuple-element.152), channel_id=1, source_target_pairs={{0,4},{4,0},{8,12},{12,8},{16,20},{20,16},{24,28},{28,24},{1,5},{5... | collective-permute-start | bytes 6488072 | tf_op jit(solution)/shard_map/ppermute | solution.py:291
  384.8 7.2 collective-permute-start.26
  384.8 9.0 collective-permute-start.27
  393.8 57.8 %collective-permute-start.29 = (bf16[528,2048]{1,0:T(8,128)(2,1)}, bf16[528,2048]{1,0:T(8,128)(2,1)}, u32[]{:S(2)}, u32[]{:S(2)}) collective-permute-start(bf16[528,2048]{1,0:T(8,128)(2,1)} %pad_maximum_fusion), channel_id=1, source_target_pairs={{0,8},{4,12},{8,16},{12,20},{16,24},{20,28},{24,0},{28,4},{1,9},{5... | collective-permute-start | bytes 6488072 | tf_op jit(solution)/shard_map/ppermute | solution.py:291
  405.3 71.3 %collective-permute-start.33 = (bf16[528,2048]{1,0:T(8,128)(2,1)}, bf16[528,2048]{1,0:T(8,128)(2,1)}, u32[]{:S(2)}, u32[]{:S(2)}) collective-permute-start(bf16[528,2048]{1,0:T(8,128)(2,1)} %get-tuple-element.160), channel_id=1, source_target_pairs={{0,4},{4,0},{8,12},{12,8},{16,20},{20,16},{24,28},{28,24},{1,5},{5... | collective-permute-start | bytes 6488072 | tf_op jit(solution)/shard_map/ppermute | solution.py:291
  458.0 50.3 %collective-permute-start.32 = (bf16[528,2048]{1,0:T(8,128)(2,1)}, bf16[528,2048]{1,0:T(8,128)(2,1)}, u32[]{:S(2)}, u32[]{:S(2)}) collective-permute-start(bf16[528,2048]{1,0:T(8,128)(2,1)} %pad_maximum_fusion.1), channel_id=1, source_target_pairs={{0,24},{4,28},{8,0},{12,4},{16,8},{20,12},{24,16},{28,20},{1,25},{... | collective-permute-start | bytes 6488072 | tf_op jit(solution)/shard_map/ppermute | solution.py:291
  462.7 136.7 %all-to-all-start = ((bf16[8,512,256]{2,1,0:T(8,128)(2,1)}), bf16[8,512,256]{2,1,0:T(8,128)(2,1)}, u32[]{:S(2)}, u32[]{:S(2)}) async-start(bf16[8,512,256]{2,1,0:T(8,128)(2,1)} %get-tuple-element.161), calls=%async_computation.1 | async-start | bytes 4194304 | tf_op jit(solution)/shard_map/all_to_all | solution.py:619
  513.1 86.3 %collective-permute-start.34 = (bf16[528,2048]{1,0:T(8,128)(2,1)S(1)}, bf16[528,2048]{1,0:T(8,128)(2,1)}, u32[]{:S(2)}, u32[]{:S(2)}) collective-permute-start(bf16[528,2048]{1,0:T(8,128)(2,1)S(1)} %add_convert_fusion.refs_0_), channel_id=1, source_target_pairs={{0,8},{4,12},{8,16},{12,20},{16,24},{20,28},{24,0},{28,4},{1,9},{5... | collective-permute-start | bytes 6488072 | tf_op jit(solution)/shard_map/ppermute | solution.py:291
  515.1 84.3 %collective-permute-start.35 = (bf16[528,2048]{1,0:T(8,128)(2,1)S(1)}, bf16[528,2048]{1,0:T(8,128)(2,1)}, u32[]{:S(2)}, u32[]{:S(2)}) collective-permute-start(bf16[528,2048]{1,0:T(8,128)(2,1)S(1)} %add_convert_fusion.refs_0_), channel_id=1, source_target_pairs={{0,4},{4,0},{8,12},{12,8},{16,20},{20,16},{24,28},{28,24},{1,5},{5... | collective-permute-start | bytes 6488072 | tf_op jit(solution)/shard_map/ppermute | solution.py:291
  527.9 71.9 %collective-permute-start.30 = (bf16[2,128,2048]{2,1,0:T(8,128)(2,1)}, bf16[2,128,2048]{2,1,0:T(8,128)(2,1)}, u32[]{:S(2)}, u32[]{:S(2)}) collective-permute-start(bf16[2,128,2048]{2,1,0:T(8,128)(2,1)} %select_bitcast_fusion), channel_id=1, source_target_pairs={{0,1},{1,0},{2,3},{3,2},{4,5},{5,4},{6,7},{7,6},{8,9},{9,8},{10,11... | collective-permute-start | bytes 3145736 | tf_op jit(solution)/shard_map/ppermute | solution.py:319
  599.4 47.6 %collective-permute-start.36 = (bf16[528,2048]{1,0:T(8,128)(2,1)S(1)}, bf16[528,2048]{1,0:T(8,128)(2,1)}, u32[]{:S(2)}, u32[]{:S(2)}) collective-permute-start(bf16[528,2048]{1,0:T(8,128)(2,1)S(1)} %add_convert_fusion.refs_0_), channel_id=1, source_target_pairs={{0,24},{4,28},{8,0},{12,4},{16,8},{20,12},{24,16},{28,20},{1,25},{... | collective-permute-start | bytes 6488072 | tf_op jit(solution)/shard_map/ppermute | solution.py:291
  599.4 47.8 %collective-permute-start.37 = (bf16[528,2048]{1,0:T(8,128)(2,1)}, bf16[528,2048]{1,0:T(8,128)(2,1)}, u32[]{:S(2)}, u32[]{:S(2)}) collective-permute-start(bf16[528,2048]{1,0:T(8,128)(2,1)} %collective-permute-done.34.refs_3_), channel_id=1, source_target_pairs={{0,4},{4,0},{8,12},{12,8},{16,20},{20,16},{24,28},{28,24},{1,5},{5... | collective-permute-start | bytes 6488072 | tf_op jit(solution)/shard_map/ppermute | solution.py:291
  604.0 12.6 %collective-permute-start.31 = (bf16[128,2048]{1,0:T(8,128)(2,1)}, bf16[128,2048]{1,0:T(8,128)(2,1)S(1)}, u32[]{:S(2)}, u32[]{:S(2)}) collective-permute-start(bf16[128,2048]{1,0:T(8,128)(2,1)} %select_bitcast_fusion.4), channel_id=1, source_target_pairs={{0,2},{1,3},{2,0},{3,1},{4,6},{5,7},{6,4},{7,5},{8,10},{9,11},{10,... | collective-permute-start | bytes 1572872 | tf_op jit(solution)/shard_map/ppermute | solution.py:319
  647.2 98.3 %collective-permute-start.40 = (bf16[528,2048]{1,0:T(8,128)(2,1)}, bf16[528,2048]{1,0:T(8,128)(2,1)}, u32[]{:S(2)}, u32[]{:S(2)}) collective-permute-start(bf16[528,2048]{1,0:T(8,128)(2,1)} %collective-permute-done.36.refs_1_), channel_id=1, source_target_pairs={{0,4},{4,0},{8,12},{12,8},{16,20},{20,16},{24,28},{28,24},{1,5},{5... | collective-permute-start | bytes 6488072 | tf_op jit(solution)/shard_map/ppermute | solution.py:291
  671.8 73.8 %collective-permute-start.39 = (bf16[272,2048]{1,0:T(8,128)(2,1)S(1)}, bf16[272,2048]{1,0:T(8,128)(2,1)S(1)}, u32[]{:S(2)}, u32[]{:S(2)}) collective-permute-start(bf16[272,2048]{1,0:T(8,128)(2,1)S(1)} %slice.261), channel_id=1, source_target_pairs={{0,24},{4,28},{8,0},{12,4},{16,8},{20,12},{24,16},{28,20},{1,25},{... | collective-permute-start | bytes 3342344 | tf_op jit(solution)/shard_map/ppermute | solution.py:291
  701.0 44.6 %collective-permute-start.38 = (bf16[256,2048]{1,0:T(8,128)(2,1)S(1)}, bf16[256,2048]{1,0:T(8,128)(2,1)S(1)}, u32[]{:S(2)}, u32[]{:S(2)}) collective-permute-start(bf16[256,2048]{1,0:T(8,128)(2,1)S(1)} %slice.260), channel_id=1, source_target_pairs={{0,8},{4,12},{8,16},{12,20},{16,24},{20,28},{24,0},{28,4},{1,9},{5... | collective-permute-start | bytes 3145736 | tf_op jit(solution)/shard_map/ppermute | solution.py:291
  747.7 76.7 %collective-permute-start.41 = (bf16[528,2048]{1,0:T(8,128)(2,1)}, bf16[528,2048]{1,0:T(8,128)(2,1)}, u32[]{:S(2)}, u32[]{:S(2)}) collective-permute-start(bf16[528,2048]{1,0:T(8,128)(2,1)} %constant_dynamic-update-slice_fusion.12.refs_2_), channel_id=1, source_target_pairs={{0,4},{4,0},{8,12},{12,8},{16,20},{20,16},{24,28},{28,24},{1,5},{5... | collective-permute-start | bytes 6488072 | tf_op jit(solution)/shard_map/ppermute | solution.py:291
  752.0 33.5 %collective-permute-start.42 = (bf16[336,2048]{1,0:T(8,128)(2,1)S(1)}, bf16[336,2048]{1,0:T(8,128)(2,1)}, u32[]{:S(2)}, u32[]{:S(2)}) collective-permute-start(bf16[336,2048]{1,0:T(8,128)(2,1)S(1)} %pad_maximum_fusion.6.refs_0_), channel_id=1, source_target_pairs={{0,8},{4,12},{8,16},{12,20},{16,24},{20,28},{24,0},{28,4},{1,9},{5... | collective-permute-start | bytes 4128776 | tf_op jit(solution)/shard_map/ppermute | solution.py:291
  753.6 70.8 %collective-permute-start.43 = (bf16[336,2048]{1,0:T(8,128)(2,1)S(1)}, bf16[336,2048]{1,0:T(8,128)(2,1)}, u32[]{:S(2)}, u32[]{:S(2)}) collective-permute-start(bf16[336,2048]{1,0:T(8,128)(2,1)S(1)} %pad_maximum_fusion.6.refs_0_), channel_id=1, source_target_pairs={{0,4},{4,0},{8,12},{12,8},{16,20},{20,16},{24,28},{28,24},{1,5},{5... | collective-permute-start | bytes 4128776 | tf_op jit(solution)/shard_map/ppermute | solution.py:291
  756.1 74.4 %collective-permute-start.11 = (bf16[2,128,2048]{2,1,0:T(8,128)(2,1)}, bf16[2,128,2048]{2,1,0:T(8,128)(2,1)}, u32[]{:S(2)}, u32[]{:S(2)}) collective-permute-start(bf16[2,128,2048]{2,1,0:T(8,128)(2,1)} %select_bitcast_fusion.2), channel_id=1, source_target_pairs={{0,1},{1,0},{2,3},{3,2},{4,5},{5,4},{6,7},{7,6},{8,9},{9,8},{10,11... | collective-permute-start | bytes 3145736 | tf_op jit(solution)/shard_map/ppermute | solution.py:319
  758.3 77.5 %copy-start.35 = (f32[8,72,128]{2,1,0:T(8,128)S(1)}, f32[8,72,128]{2,1,0:T(8,128)}, u32[]{:S(2)}) copy-start(f32[8,72,128]{2,1,0:T(8,128)} %copy-done.34) | copy-start | bytes 884740
  758.3 78.8 %copy-start.104 = (f32[128]{0:T(128)S(1)}, f32[128]{0:T(128)}, u32[]{:S(2)}) copy-start(f32[128]{0:T(128)} %get-tuple-element.204) | copy-start | bytes 1540
  758.3 103.4 %copy-start.39 = (f32[128,2048]{1,0:T(8,128)S(1)}, f32[128,2048]{1,0:T(8,128)}, u32[]{:S(2)}) copy-start(f32[128,2048]{1,0:T(8,128)} %copy-done.37) | copy-start | bytes 3145732
  758.3 103.4 %copy-start.42 = (bf16[128,2048]{1,0:T(8,128)(2,1)S(1)}, bf16[128,2048]{1,0:T(8,128)(2,1)}, u32[]{:S(2)}) copy-start(bf16[128,2048]{1,0:T(8,128)(2,1)} %param.19) | copy-start | bytes 1572868
  758.4 103.3 %copy-start.51 = (bf16[1,128,2048]{2,1,0:T(8,128)(2,1)S(1)}, bf16[1,128,2048]{2,1,0:T(8,128)(2,1)}, u32[]{:S(2)}) copy-start(bf16[1,128,2048]{2,1,0:T(8,128)(2,1)} %copy-done.50) | copy-start | bytes 1572868
  758.4 103.3 %copy-start.64 = (bf16[128,2048]{1,0:T(8,128)(2,1)S(1)}, bf16[128,2048]{1,0:T(8,128)(2,1)}, u32[]{:S(2)}) copy-start(bf16[128,2048]{1,0:T(8,128)(2,1)} %copy-done.63) | copy-start | bytes 1572868
  758.4 103.3 %copy-start.65 = (bf16[1,128,2048]{2,1,0:T(8,128)(2,1)S(1)}, bf16[1,128,2048]{2,1,0:T(8,128)(2,1)}, u32[]{:S(2)}) copy-start(bf16[1,128,2048]{2,1,0:T(8,128)(2,1)} %get-tuple-element.219) | copy-start | bytes 1572868
  758.4 103.3 %copy-start.88 = (f32[2048]{0:T(1024)S(1)}, f32[2048]{0:T(1024)}, u32[]{:S(2)}) copy-start(f32[2048]{0:T(1024)} %param.20) | copy-start | bytes 24580
  758.4 103.3 %copy-start.97 = (f32[128]{0:T(128)S(1)}, f32[128]{0:T(128)}, u32[]{:S(2)}) copy-start(f32[128]{0:T(128)} %copy-done.95) | copy-start | bytes 1540
  758.4 103.3 %copy-start.99 = (f32[128]{0:T(128)S(1)}, f32[128]{0:T(128)}, u32[]{:S(2)}) copy-start(f32[128]{0:T(128)} %copy-done.98) | copy-start | bytes 1540
  824.4 34.2 %collective-permute-start.44 = (bf16[336,2048]{1,0:T(8,128)(2,1)S(1)}, bf16[336,2048]{1,0:T(8,128)(2,1)S(1)}, u32[]{:S(2)}, u32[]{:S(2)}) collective-permute-start(bf16[336,2048]{1,0:T(8,128)(2,1)S(1)} %pad_maximum_fusion.6.refs_0_), channel_id=1, source_target_pairs={{0,24},{4,28},{8,0},{12,4},{16,8},{20,12},{24,16},{28,20},{1,25},{... | collective-permute-start | bytes 4128776 | tf_op jit(solution)/shard_map/ppermute | solution.py:291
  829.9 31.2 %collective-permute-start.45 = (bf16[336,2048]{1,0:T(8,128)(2,1)}, bf16[336,2048]{1,0:T(8,128)(2,1)S(1)}, u32[]{:S(2)}, u32[]{:S(2)}) collective-permute-start(bf16[336,2048]{1,0:T(8,128)(2,1)} %collective-permute-done.42.refs_3_), channel_id=1, source_target_pairs={{0,4},{4,0},{8,12},{12,8},{16,20},{20,16},{24,28},{28,24},{1,5},{5... | collective-permute-start | bytes 4128776 | tf_op jit(solution)/shard_map/ppermute | solution.py:291
  833.1 28.6 %collective-permute-start.12 = (bf16[128,2048]{1,0:T(8,128)(2,1)S(1)}, bf16[128,2048]{1,0:T(8,128)(2,1)S(1)}, u32[]{:S(2)}, u32[]{:S(2)}) collective-permute-start(bf16[128,2048]{1,0:T(8,128)(2,1)S(1)} %select_bitcast_fusion.14), channel_id=1, source_target_pairs={{0,2},{1,3},{2,0},{3,1},{4,6},{5,7},{6,4},{7,5},{8,10},{9,11},{10,... | collective-permute-start | bytes 1572872 | tf_op jit(solution)/shard_map/ppermute | solution.py:319
  861.1 35.1 %collective-permute-start.48 = (bf16[336,2048]{1,0:T(8,128)(2,1)S(1)}, bf16[336,2048]{1,0:T(8,128)(2,1)S(1)}, u32[]{:S(2)}, u32[]{:S(2)}) collective-permute-start(bf16[336,2048]{1,0:T(8,128)(2,1)S(1)} %collective-permute-done.44.refs_1_), channel_id=1, source_target_pairs={{0,4},{4,0},{8,12},{12,8},{16,20},{20,16},{24,28},{28,24},{1,5},{5... | collective-permute-start | bytes 4128776 | tf_op jit(solution)/shard_map/ppermute | solution.py:291
  865.4 30.8 %collective-permute-start.47 = (bf16[176,2048]{1,0:T(8,128)(2,1)S(1)}, bf16[176,2048]{1,0:T(8,128)(2,1)S(1)}, u32[]{:S(2)}, u32[]{:S(2)}) collective-permute-start(bf16[176,2048]{1,0:T(8,128)(2,1)S(1)} %slice.265), channel_id=1, source_target_pairs={{0,24},{4,28},{8,0},{12,4},{16,8},{20,12},{24,16},{28,20},{1,25},{... | collective-permute-start | bytes 2162696 | tf_op jit(solution)/shard_map/ppermute | solution.py:291
  868.8 27.5 %collective-permute-start.46 = (bf16[160,2048]{1,0:T(8,128)(2,1)S(1)}, bf16[160,2048]{1,0:T(8,128)(2,1)S(1)}, u32[]{:S(2)}, u32[]{:S(2)}) collective-permute-start(bf16[160,2048]{1,0:T(8,128)(2,1)S(1)} %slice.264), channel_id=1, source_target_pairs={{0,8},{4,12},{8,16},{12,20},{16,24},{20,28},{24,0},{28,4},{1,9},{5... | collective-permute-start | bytes 1966088 | tf_op jit(solution)/shard_map/ppermute | solution.py:291
  896.4 29.8 %collective-permute-start.49 = (bf16[336,2048]{1,0:T(8,128)(2,1)S(1)}, bf16[336,2048]{1,0:T(8,128)(2,1)S(1)}, u32[]{:S(2)}, u32[]{:S(2)}) collective-permute-start(bf16[336,2048]{1,0:T(8,128)(2,1)S(1)} %constant_dynamic-update-slice_fusion.14.refs_2_), channel_id=1, source_target_pairs={{0,4},{4,0},{8,12},{12,8},{16,20},{20,16},{24,28},{28,24},{1,5},{5... | collective-permute-start | bytes 4128776 | tf_op jit(solution)/shard_map/ppermute | solution.py:291
  (109 other events, 1516.1 us)
Sparse Core Ops, SparseCore 0:
  88.7 126.0 all-gather.1
Sparse Core Ops, SparseCore 1:
  358.7 86.3 reduce-scatter.1

commit v4 on v3

--- a/solution.py
+++ b/solution.py
@@ -291,25 +291,25 @@
     return lax.ppermute(v, "seq", pairs)
 
 
-def seq_gather(v, *later):
+def seq_gather(v, between, *later):
     Z, X = grid_of()
     i = lax.axis_index("seq")
     j = jnp.arange(Z * X, dtype=jnp.int32)
     if (Z, X) != (4, 2):
-        return lax.all_gather(v, "seq", axis=0, tiled=False), j
+        return (lax.all_gather(v, "seq", axis=0, tiled=False), j), between
     other = shift(v, 0, 1)
     if later:
         other, later = together(other, later)
     both = jnp.stack([v, other])
     left = shift(both, 1, 0)
     right = shift(both, 3, 0)
+    left, right, between = together(left, right, between)
     far0 = shift(left[:1], 1, 0)
     far1 = shift(right[1:], 3, 0)
     z, x = i // X, i % X
     every = jnp.concatenate([both, right, far0, far1, left])
-    if later:
-        return every, *later
-    return every, ((j // X - z) % Z) * X + (j % X - x) % X
+    order = ((j // X - z) % Z) * X + (j % X - x) % X
+    return (every, order, *later), between
 
 
 def head_shift(v, dy, dc):
@@ -319,13 +319,13 @@
     return lax.ppermute(v, "head", pairs)
 
 
-def head_gather(v):
+def head_gather(v, across=None):
     H = lax.axis_size("head")
     if H != 4:
         return lax.all_gather(v, "head", axis=0, tiled=True)
     i = lax.axis_index("head")
     y, c = i // 2, i % 2
-    mine = jnp.stack([v, head_shift(v, 1, 0)])
+    mine = jnp.stack([v, head_shift(v, 1, 0) if across is None else across])
     other = head_shift(mine, 0, 1)
     a = jnp.where(c == 0, mine, other)
     b = jnp.where(c == 0, other, mine)
@@ -334,7 +334,7 @@
     return jnp.concatenate(rows, axis=0)
 
 
-def head_scatter(v):
+def head_scatter(v, hold=None):
     H = lax.axis_size("head")
     v = v.astype(BF)
     if H != 4:
@@ -345,7 +345,10 @@
     got = head_shift(jnp.where(c == 0, v[:, 1], v[:, 0]), 0, 1)
     half = (jnp.where(c == 0, v[:, 0], v[:, 1]).astype(F32) + got.astype(F32)).astype(BF)
     back = head_shift(jnp.where(y == 0, half[1], half[0]), 1, 0)
-    return jnp.where(y == 0, half[0], half[1]).astype(F32) + back.astype(F32)
+    if hold is not None:
+        back, hold = together(back, hold)
+    total = jnp.where(y == 0, half[0], half[1]).astype(F32) + back.astype(F32)
+    return total if hold is None else (total, hold)
 
 
 def gelu_tanh(values):
@@ -397,24 +400,6 @@
         compiler_params=params(),
         name="mlp_slices",
     )(which, d_gate, d_up, hidden, d_gate, d_up, hidden, mlp_group, cot_group)
-
-
-def gather1(v):
-    return shift(v, 1, 0), shift(v, 0, 1)
-
-
-def gather2(v, left):
-    return shift(v, 3, 0), shift(left, 0, 1)
-
-
-def gather3(v, left, right):
-    h = v.shape[0] // 32 * 16
-    return shift(left[:h], 1, 0), shift(right[h:], 3, 0), shift(right, 0, 1)
-
-
-def gather4(far_a, far_b):
-    far = jnp.concatenate([far_a, far_b], axis=0)
-    return far, shift(far, 0, 1)
 
 
 def slots():
@@ -459,6 +444,55 @@
         compiler_params=params(),
         name=name,
     )(slots(), *pieces)
+
+
+def put_heads_kernel(at_ref, own_ref, other_ref, *refs):
+    outs = refs[-5:]
+    for t, out in enumerate(outs):
+        own = own_ref[pl.ds(t * HW, HW), :].astype(F32)
+        other = other_ref[pl.ds(t * HW, HW), :].astype(F32)
+        even = at_ref[1] == 0
+        both = jnp.concatenate([jnp.where(even, own, other), jnp.where(even, other, own)], axis=0)
+        out[...] = both.T if t < 4 else both
+
+
+def put_heads(k, own, other, before):
+    i = lax.axis_index("seq")
+    place = jnp.stack([(i // 2 + k) % 4, i % 2]).astype(jnp.int32)
+    R, D = own.shape
+    width = 8 * HW
+    tile = min(D, 512)
+    piece = pl.BlockSpec((R, tile), lambda j, o: (0, j))
+    turned = pl.BlockSpec((tile, LN), lambda j, o: (j, o[0]))
+    straight = pl.BlockSpec((LN, tile), lambda j, o: (o[0], j))
+    before = [] if before is None else list(before)
+    return pl.pallas_call(
+        put_heads_kernel,
+        grid_spec=pltpu.PrefetchScalarGridSpec(
+            num_scalar_prefetch=1,
+            grid=(D // tile,),
+            in_specs=[piece, piece] + [pl.BlockSpec(memory_space=pl.ANY)] * len(before),
+            out_specs=[turned] * 4 + [straight],
+        ),
+        out_shape=[jax.ShapeDtypeStruct((D, width), F32)] * 4
+        + [jax.ShapeDtypeStruct((width, D), F32)],
+        input_output_aliases={3 + n: n for n in range(len(before))},
+        compiler_params=params(),
+        name="put_heads",
+    )(place, own, other, *before)
+
+
+def rows_of(values, D):
+    values = jnp.concatenate(values)
+    return jnp.concatenate([values, jnp.zeros((16 * D - values.shape[0],), BF)]).reshape(16, D)
+
+
+def in_order(pieces):
+    i = lax.axis_index("seq")
+    z, x = i // 2, i % 2
+    j = jnp.arange(8, dtype=jnp.int32)
+    slot = (j // 2 - z) % 4 + 4 * ((j % 2 - x) % 2)
+    return jnp.stack(pieces)[slot].reshape(8, -1)
 
 
 def halves(v):
@@ -503,21 +537,24 @@
     unit_in = input_f32 * scale_in
     normed = (unit_in * norm1_gain).astype(BF)
     group_in = head_gather(normed)
-    group_cot = head_gather(out_cotangent)
     key_rows = dot(group_in, key_weight)
     value_rows = dot(group_in, value_weight)
     rate_pre = dot(group_in, rate_weight) + rate_bias
     rate_sig = jax.nn.sigmoid(rate_pre)
     rate_rows = rate_sig * rate_scale
     inv, uw, step_maps, seg_map = K["map"](key_rows, value_rows, rate_rows)
-    all_maps, order = seq_gather(seg_map)
+    cot_late, seg_map = together(out_cotangent, seg_map)
+    cot_across = head_shift(cot_late, 1, 0) if heads == 4 else cot_late
+    query_rows = dot(group_in, query_weight)
+    local = K["local"](query_rows, key_rows, rate_rows, inv, uw)
+    (all_maps, order), (local, cot_across) = seq_gather(seg_map, (local, cot_across))
+    group_cot = head_gather(out_cotangent, cot_across)
+    q_eff, z_off, pt, vv = local
+    place = jnp.concatenate([seg, order])
     if wide:
         normed_late, all_maps = together(normed, all_maps)
         normed_all = lax.all_gather(normed_late, everywhere, axis=0, tiled=True)
-    place = jnp.concatenate([seg, order])
-    query_rows = dot(group_in, query_weight)
     gate_pre = dot(group_in, gate_weight)
-    q_eff, z_off, pt, vv = K["local"](query_rows, key_rows, rate_rows, inv, uw)
     z_rows, errors, states = K["forward"](
         place, all_maps, all_maps, init_state, init_bias[:, None, :], step_maps, uw, q_eff, z_off
     )
@@ -546,7 +583,11 @@
         slices = lambda k: mlp_slices(k, rows, d_gate_mlp, d_up_mlp, hidden, mlp_group, group_cot)
         d_gate_mlp, (sent, kept2) = together(d_gate_mlp, slices(2))
         got2 = shift(sent, 0, 1)
-    d_mlp_input = head_scatter(dot(d_gate_mlp, mlp_gate, 0, 1) + dot(d_up_mlp, mlp_up, 0, 1))
+    d_mlp_part = dot(d_gate_mlp, mlp_gate, 0, 1) + dot(d_up_mlp, mlp_up, 0, 1)
+    if wide:
+        d_mlp_input, (got2, (sent1, kept1)) = head_scatter(d_mlp_part, (got2, slices(1)))
+    else:
+        d_mlp_input = head_scatter(d_mlp_part)
     scaled_mid = d_mlp_input * norm2_gain
     norm2_part = jnp.sum(d_mlp_input * unit_mid, axis=0)
     d_middle = out_cotangent.astype(F32) + scale_mid * (
@@ -554,13 +595,19 @@
     )
     d_attn = d_middle.astype(BF)
     if wide:
-        sent, kept1 = slices(1)
-        d_attn, got2, sent, kept1 = together(d_attn, got2, sent, kept1)
-        got1 = shift(sent, 0, 1)
+        got1 = shift(sent1, 0, 1)
         far = plus(kept2, got2)
         h = far.shape[0] // 32 * 16
         a_far, b_far = shift(far[:h], 1, 0), shift(far[h:], 3, 0)
-    d_attn_group = head_gather(d_attn)
+        across = head_shift(d_attn, 1, 0)
+        across, got1, a_far, b_far = together(across, got1, a_far, b_far)
+        d_attn_group = head_gather(d_attn, across)
+        ahead = plus(kept1, got1)
+        up = jnp.concatenate([plus(ahead[:h], a_far), ahead[h:]], axis=0)
+        up, (sent, kept3) = together(up, slices(3))
+        from_left, got3 = shift(up, 1, 0), shift(sent, 0, 1)
+    else:
+        d_attn_group = head_gather(d_attn)
     d_gated = dot(d_attn_group, out_weight, 1, 1)
     out_weight_grad = dot(gated_out, d_attn_group, 0, 0).astype(BF)
     d_post = d_gated * gate_act
@@ -572,34 +619,28 @@
     d_z = inv_scale * (
         d_zhat - back_sums[0][:, None] / model_width - z_hat * (back_sums[1][:, None] / model_width)
     )
+    mlp_out = head_scatter(dot(hidden, mlp_down, 0, 0))
+    d_z, mlp_out = together(d_z, mlp_out)
+    step_grads, seg_grad = K["sgrad"](d_z, q_eff, step_maps)
+    query_parts = K["qgrad"](query_rows, key_rows, rate_rows, d_z, errors, states, pt)
     if wide:
-        d_z, a_far, b_far = together(d_z, a_far, b_far)
-    step_grads, seg_grad = K["sgrad"](d_z, q_eff, step_maps)
-    if wide:
-        seg_grad, got1, normed_all = together(seg_grad, got1, normed_all)
-        ahead = plus(kept1, got1)
-        up = jnp.concatenate([plus(ahead[:h], a_far), ahead[h:]], axis=0)
-    if wide:
-        all_grads, (sent3, kept3), (sent0, kept0) = seq_gather(seg_grad, slices(3), slices(0))
+        (all_grads, _, (sent, kept0)), query_parts = seq_gather(seg_grad, query_parts, slices(0))
+        got0 = shift(sent, 0, 1)
+        all_grads, got3, from_left, normed_all = together(all_grads, got3, from_left, normed_all)
+        behind = plus(kept3, got3)
+        down = jnp.concatenate([behind[:h], plus(behind[h:], b_far)], axis=0)
+        from_right = shift(down, 3, 0)
+        out_slice = lax.psum_scatter(out_weight_grad, "seq", scatter_dimension=0, tiled=True)
     else:
-        all_grads, _ = seq_gather(seg_grad)
-    if wide:
-        out_slice = lax.psum_scatter(out_weight_grad, "seq", scatter_dimension=0, tiled=True)
-        got3, got0 = shift(sent3, 0, 1), shift(sent0, 0, 1)
-        all_grads, up = together(all_grads, up)
-        from_left = shift(up, 1, 0)
-    d_query, b_part, lam_part = K["qgrad"](query_rows, key_rows, rate_rows, d_z, errors, states, pt)
+        (all_grads, _), query_parts = seq_gather(seg_grad, query_parts)
+    d_query, b_part, lam_part = query_parts
     d_key, d_value, d_rate, init_grad, packed = K["kgrad"](
         place, all_maps, all_maps, all_grads, key_rows, rate_rows, errors, states, vv,
         b_part, lam_part, step_maps, step_grads, d_query, d_gate_pre,
     )
     if wide:
-        d_rate, packed, got3, from_left, out_slice = together(
-            d_rate, packed, got3, from_left, out_slice
-        )
-        behind = plus(kept3, got3)
-        down = jnp.concatenate([behind[:h], plus(behind[h:], b_far)], axis=0)
-        first = shift(down, 3, 0).astype(F32) + from_left.astype(F32)
+        packed, out_slice = together(packed, out_slice)
+        first = from_left.astype(F32) + from_right.astype(F32)
         first = (first + kept0.astype(F32) + got0.astype(F32)).astype(BF)
     d_rate_pre = (d_rate * rate_scale * rate_sig * (1.0 - rate_sig)).astype(BF)
     scale_part = jnp.sum(d_rate * rate_sig, axis=0)
@@ -613,61 +654,70 @@
     input_grad = d_middle + scale_in * (
         scaled_in - unit_in * jnp.mean(scaled_in * unit_in, axis=-1, keepdims=True)
     )
-    block_out = (middle + head_scatter(dot(hidden, mlp_down, 0, 0))).astype(BF)
+    block_out = (middle + mlp_out).astype(BF)
 
     if wide:
+        extra = [d_rate_pre.reshape(-1)]
+        for v in (scale_part, post_gain_part, post_bias_part):
+            extra.append(halves(v).reshape(-1))
+        first = jnp.concatenate([first, rows_of(extra, model_width)], axis=0)
+        crossed = shift(first, 0, 1)
         packed = lax.all_to_all(packed, "seq", split_axis=0, concat_axis=0, tiled=True)
+        packed, crossed, first = together(packed, crossed, first)
+        left = shift(first, 1, 0)
         packed = packed.reshape(segs * tokens, packed.shape[2])
-        left, crossed = gather1(first)
-        left, crossed, packed, first = together(left, crossed, packed, first)
         own = dot(packed, normed_all, 0, 0).astype(BF)
-        right, crossed_left = gather2(first, left)
+        norm_parts = lax.psum((norm1_part, norm2_part), "head")
+        norm_rows = rows_of([halves(v).reshape(-1) for v in norm_parts], model_width)
+        second = jnp.concatenate([own, out_slice, norm_rows], axis=0)
+        crossed2 = shift(second, 0, 1)
+        left, crossed2, first, second = together(left, crossed2, first, second)
+        right, crossed_left = shift(first, 3, 0), shift(left, 0, 1)
         left, right, crossed_left = together(left, right, crossed_left)
-        far_a, far_b, crossed_right = gather3(first, left, right)
-        norm_parts = lax.psum((norm1_part, norm2_part), "head")
-        ends = [0]
-        extra = [d_rate_pre.reshape(-1)]
-        for v in (scale_part, post_gain_part, post_bias_part, *norm_parts):
-            extra.append(halves(v).reshape(-1))
-        for v in extra:
-            ends.append(ends[-1] + v.shape[0])
-        extra = jnp.concatenate(extra + [jnp.zeros((16 * model_width - ends[-1],), BF)])
-        second = jnp.concatenate([own, out_slice, extra.reshape(16, model_width)], axis=0)
+        h = first.shape[0] // 32 * 16
+        far_a, far_b = shift(left[:h], 1, 0), shift(right[h:], 3, 0)
+        crossed_right = shift(right, 0, 1)
         far_a, far_b, crossed_right, second = together(far_a, far_b, crossed_right, second)
-        far, crossed_far = gather4(far_a, far_b)
-        left2, crossed2 = gather1(second)
-        far, crossed_far, left2, crossed2, second = together(
-            far, crossed_far, left2, crossed2, second
-        )
-        right2, crossed_left2 = gather2(second, left2)
+        far = jnp.concatenate([far_a, far_b], axis=0)
+        crossed_far, left2 = shift(far, 0, 1), shift(second, 1, 0)
+        head_sums = put_heads(0, second, crossed2, None)
+        crossed_far, left2, second, head_sums = together(crossed_far, left2, second, head_sums)
+        right2, crossed_left2 = shift(second, 3, 0), shift(left2, 0, 1)
         pieces = (first, right, far, left, crossed, crossed_right, crossed_far, crossed_left)
         plan = tuple((t * rows, rows, False) for t in range(3))
         mlp_sums = finish(pieces, plan, (width,) * 3, "mlp_finish")
-        left2, right2, crossed_left2 = together(left2, right2, crossed_left2)
-        far_a, far_b, crossed_right2 = gather3(second, left2, right2)
-        far_a, far_b, crossed_right2, mlp_sums = together(far_a, far_b, crossed_right2, mlp_sums)
+        left2, right2, crossed_left2, mlp_sums = together(left2, right2, crossed_left2, mlp_sums)
+        h = second.shape[0] // 32 * 16
+        far_a, far_b = shift(left2[:h], 1, 0), shift(right2[h:], 3, 0)
+        crossed_right2 = shift(right2, 0, 1)
+        head_sums = put_heads(3, left2, crossed_left2, head_sums)
+        far_a, far_b, crossed_right2, head_sums = together(
+            far_a, far_b, crossed_right2, head_sums
+        )
         gate_sum, up_sum, down_sum = mlp_sums
-        far2, crossed_far2 = gather4(far_a, far_b)
-        full = segs * HW
+        gate_sum, up_sum = gate_sum.T, up_sum.T
+        small_rows = [v[-16:-12] for v in pieces]
+        far_a, far_b, small_rows = together(far_a, far_b, small_rows)
+        from_all = in_order(small_rows)
+        count = tokens * local_heads
+        d_rate_all = from_all[:, :count].reshape(segs * tokens, local_heads)
+        small = [dot(normed_all, d_rate_all, 0, 0), jnp.sum(d_rate_all.astype(F32), axis=0)]
+        for v in (scale_part, post_gain_part, post_bias_part):
+            n = v.shape[0]
+            both = from_all[:, count : count + 2 * n].astype(F32).reshape(2 * segs, n)
+            small.append(jnp.sum(both, axis=0))
+            count += 2 * n
+        far2 = jnp.concatenate([far_a, far_b], axis=0)
+        crossed_far2 = shift(far2, 0, 1)
+        head_sums = put_heads(1, right2, crossed_right2, head_sums)
+        query_sum, key_sum, value_sum, pre_sum, out_sum = put_heads(
+            2, far2, crossed_far2, head_sums
+        )
         pieces = (
             second, right2, far2, left2, crossed2, crossed_right2, crossed_far2, crossed_left2
         )
-        plan = tuple((t * HW, HW, t < 4) for t in range(5))
-        query_sum, key_sum, value_sum, pre_sum, out_sum = finish(
-            pieces, plan, (full,) * 5, "head_finish"
-        )
-        gate_sum, up_sum = gate_sum.T, up_sum.T
-        shared = jnp.stack([v[-16:] for v in pieces]).reshape(segs, -1)
-        shared = shared[jnp.argsort(slots())]
-        from_all = [shared[:, s:e] for s, e in zip(ends[:-1], ends[1:])]
-        d_rate_all = from_all[0].reshape(segs * tokens, local_heads)
-        totals = [jnp.sum(v.astype(F32).reshape(2 * segs, -1), axis=0) for v in from_all[1:]]
-        small = (
-            dot(normed_all, d_rate_all, 0, 0),
-            jnp.sum(d_rate_all.astype(F32), axis=0),
-            *totals[:3],
-        )
-        gain_grads = totals[3:]
+        norms = in_order([v[-16:-12] for v in pieces]).astype(F32)
+        gain_grads = jnp.sum(norms.reshape(segs, 2, 2, model_width), axis=(0, 2))
     else:
         grads = (
             dot(hidden, group_cot),

time: 983 us -> 836 us (0.85)
  waiting for transfers between devices: 483 us -> 346 us
    all_to_all x1, waiting for transfers between devices: 71.5 us -> 9.27 us  [body(): lax.all_to_all(packed, 'seq', split_axis=0, concat_axis=0, tiled=True)]
    ppermute x34, waiting for transfers between devices: 311 us -> 278 us  [shift(): return lax.ppermute(v, 'seq', pairs)]
    ppermute x16, waiting for transfers between devices: 84.9 us -> 59 us  [head_shift(): return lax.ppermute(v, 'head', pairs)]
    pallas_call x2 -> x1, Pallas kernels: 39.3 us -> 20.5 us  [finish(): pl.pallas_call(functools.partial(finish_kernel, plan), grid_spec=pltpu.Pr...]
    pallas_call x1 -> x5, Pallas kernels: 8.23 us -> 23.9 us  [the longest x4 15.7 us: put_heads(): pl.pallas_call(put_heads_kernel, grid_spec=pltpu.PrefetchScalarGridSpec(n...]
    reduce_scatter x1, waiting for transfers between devices: 15.6 us -> 0.02 us  [body(): lax.psum_scatter(out_weight_grad, 'seq', scatter_dimension=0, tiled=True)]
    unnamed x272 -> x285, local copies, waits for them, and re-layouts: 36 us -> 42.8 us
  transfers between devices with their start and end apart: 53 -> 53, of which waited for: 35 -> 33; matrix products, arithmetic and copies ran while one was open for 15% -> 17% of each run, Pallas kernels for 10% -> 14%
where the time goes in v4:
time: 836 us; the launch traced here: 824 us
  waiting for transfers between devices  346 us (41%)
  Pallas kernels  130 us (16%)
  starting transfers between devices  113 us (14%)
  matrix products  74.3 us (9%)
  other arithmetic  62.6 us (7%)
  local copies, waits for them, and re-layouts  56.2 us (7%)
  blocking collectives  24.4 us (3%)
  between operations  17.6 us (2%)
    ppermute x34, waiting for transfers between devices, shift(): return lax.ppermute(v, 'seq', pairs)  278 us
    ppermute x34, starting transfers between devices, shift(): return lax.ppermute(v, 'seq', pairs)  92.9 us
    dot_general x21, matrix products, dot(): lax.dot_general(a, b, (((ca,), (cb,)), ((), ())), preferred_element_type=...  74.3 us
    ppermute x16, waiting for transfers between devices, head_shift(): return lax.ppermute(v, 'head', pairs)  59 us
    unnamed x285, local copies, waits for them, and re-layouts  42.8 us
    pallas_call x4, Pallas kernels, mlp_slices(): pl.pallas_call(slices_kernel, grid_spec=pltpu.PrefetchScalarGridSpec(num_...  26.4 us
    pallas_call x1, Pallas kernels, body(): K['kgrad']  23.1 us
    pallas_call x1, Pallas kernels, finish(): pl.pallas_call(functools.partial(finish_kernel, plan), grid_spec=pltpu.Pr...  20.5 us
  transfers between devices with their start and end apart: 53, of which 33 were waited for; matrix products, arithmetic and copies ran while one was open for 17% of the time, Pallas kernels for 14%

profile of v4, /device:TPU:0, one launch (start us, length us, event | category | flops | bytes accessed | tf_op | source)
XLA Modules:
  0.0 824.3 jit_solution(18350263743361014626)
XLA Ops:
  15.0 10.7 %collective-permute-done = bf16[128,2048]{1,0:T(8,128)(2,1)S(1)} collective-permute-done((bf16[128,2048]{1,0:T(8,128)(2,1)S(1)}, bf16[128,2048]{1,0:T(8,128)(2,1)S(1)}, u32[]{:S(2)}, u32[]{:S(2)}) %collective-permute-start) | collective-permute-done | bytes 524320 | tf_op jit(solution)/shard_map/ppermute | solution.py:319
  38.7 11.1 %segment_maps.1 = (bf16[8,4,128,128]{3,2,1,0:T(8,128)(2,1)S(1)}, bf16[8,512,256]{2,1,0:T(8,128)(2,1)S(1)}, bf16[8,4,128,256]{3,2,1,0:T(8,128)(2,1)}, bf16[9,80,128]{2,1,0:T(8,128)(2,1)S(1)}) custom-call(f32[512,512]{1,0:T(8,128)S(1)} %fusion.55.k_ref, f32[512,512]{1,0:T(8,128)S(1)} %fusion.54.v_ref, f32[512,8]{1,0:T(8,128)S(1)} %get-tuple-element.360.r_ref), custom_call_target="tpu_custom_call" | custom-call | tf_op jit(solution)/shard_map/segment_maps/pallas_call | solution.py:545
  53.0 3.4 collective-permute-done.2
  56.5 3.9 collective-permute-start.4
  61.7 8.2 local_parts.1
  81.9 3.5 collective-permute-done.6
  90.1 9.9 %forward_states.1 = (f32[512,512]{1,0:T(8,128)}, bf16[8,512,128]{2,1,0:T(8,128)(2,1)S(1)}, bf16[8,4,128,128]{3,2,1,0:T(8,128)(2,1)S(1)}) custom-call(s32[9]{0:T(128)S(1)} %pad_add_fusion.seg_ref, bf16[8,9,80,128]{3,2,1,0:T(8,128)(2,1)} %constant_dynamic-update-slice_fusion.y_ref.yb_ref, ...), custom_call_target="tpu_custom_call" | custom-call | tf_op jit(solution)/shard_map/forward_states/pallas_call | solution.py:558
  103.5 6.5 all-reduce.2
  110.0 5.0 multiply_convert_fusion.3
  129.6 11.1 %collective-permute-done.9 = bf16[128,2048]{1,0:T(8,128)(2,1)S(1)} collective-permute-done((bf16[128,2048]{1,0:T(8,128)(2,1)S(1)}, bf16[128,2048]{1,0:T(8,128)(2,1)S(1)}, u32[]{:S(2)}, u32[]{:S(2)}) %collective-permute-start.9) | collective-permute-done | bytes 524320 | tf_op jit(solution)/shard_map/ppermute | solution.py:319
  143.1 15.2 %collective-permute-done.11 = bf16[128,2048]{1,0:T(8,128)(2,1)S(1)} collective-permute-done((bf16[128,2048]{1,0:T(8,128)(2,1)S(1)}, bf16[128,2048]{1,0:T(8,128)(2,1)S(1)}, u32[]{:S(2)}, u32[]{:S(2)}) %collective-permute-start.11) | collective-permute-done | bytes 524320 | tf_op jit(solution)/shard_map/ppermute | solution.py:319
  165.2 3.1 convolution_bitcast_fusion
  168.4 5.6 multiply_convert_fusion
  174.0 6.8 mlp_slices.4
  182.2 5.6 fusion.60
  187.8 3.7 add_convert_fusion.5
  192.9 3.8 convolution_convert_fusion.2
  201.1 6.6 mlp_slices.5
  214.2 10.6 %collective-permute-done.14 = bf16[128,2048]{1,0:T(8,128)(2,1)S(1)} collective-permute-done((bf16[128,2048]{1,0:T(8,128)(2,1)S(1)}, bf16[128,2048]{1,0:T(8,128)(2,1)S(1)}, u32[]{:S(2)}, u32[]{:S(2)}) %collective-permute-start.14) | collective-permute-done | bytes 524320 | tf_op jit(solution)/shard_map/ppermute | solution.py:319
  224.8 5.6 collective-permute-done.15
  242.7 6.7 mlp_slices.7
  249.4 6.3 mlp_slices.6
  258.1 5.7 collective-permute-done.18
  263.8 20.6 %collective-permute-done.19 = bf16[272,2048]{1,0:T(8,128)(2,1)S(1)} collective-permute-done((bf16[272,2048]{1,0:T(8,128)(2,1)S(1)}, bf16[272,2048]{1,0:T(8,128)(2,1)S(1)}, u32[]{:S(2)}, u32[]{:S(2)}) %collective-permute-start.19) | collective-permute-done | bytes 1114144 | tf_op jit(solution)/shard_map/ppermute | solution.py:291
  294.0 5.9 multiply_reduce_fusion.1
  300.0 7.0 all-reduce.1
  308.9 5.8 state_grads.1
  315.7 3.3 fusion.63
  324.2 9.1 %query_grads.1 = (bf16[512,512]{1,0:T(8,128)(2,1)S(1)}, bf16[8,512,128]{2,1,0:T(8,128)(2,1)S(1)}, f32[8,512,128]{2,1,0:T(8,128)}) custom-call(f32[512,512]{1,0:T(8,128)S(1)} %copy-done.17, f32[512,512]{1,0:T(8,128)S(1)} %copy-done.9, f32[512,8]{1,0:T(8,128)S(1)} %copy-done.12, f32[512,512]{1,0:T(8,128)S(1)} %subtract_multiply_fusion.1.dz_ref, ...), custom_call_target="tpu_custom_call" | custom-call | tf_op jit(solution)/shard_map/query_grads/pallas_call | solution.py:625
  335.0 9.6 %collective-permute-done.23 = bf16[4,80,128]{2,1,0:T(8,128)(2,1)} collective-permute-done((bf16[4,80,128]{2,1,0:T(8,128)(2,1)S(1)}, bf16[4,80,128]{2,1,0:T(8,128)(2,1)}, u32[]{:S(2)}, u32[]{:S(2)}) %collective-permute-start.23) | collective-permute-done | bytes 81952 | tf_op jit(solution)/shard_map/ppermute | solution.py:291
  349.3 13.9 %collective-permute-done.25 = bf16[2,4,80,128]{3,2,1,0:T(8,128)(2,1)S(1)} collective-permute-done((bf16[2,4,80,128]{3,2,1,0:T(8,128)(2,1)S(1)}, bf16[2,4,80,128]{3,2,1,0:T(8,128)(2,1)S(1)}, u32[]{:S(2)}, u32[]{:S(2)}) %collective-permute-start.25) | collective-permute-done | bytes 163872 | tf_op jit(solution)/shard_map/ppermute | solution.py:291
  365.6 4.0 collective-permute-start.27
  379.2 3.9 collective-permute-start.32
  383.2 23.1 %key_grads.1 = (bf16[512,512]{1,0:T(8,128)(2,1)S(1)}, bf16[512,512]{1,0:T(8,128)(2,1)S(1)}, f32[512,8]{1,0:T(8,128)S(1)}, f32[8,72,128]{2,1,0:T(8,128)S(1)}, bf16[8,512,256]{2,1,0:T(8,128)(2,1)}) custom-call(s32[9]{0:T(128)S(1)} %pad_add_fusion.seg_ref, bf16[8,9,80,128]{3,2,1,0:T(8,128)(2,1)} %constant_dynamic-update-slice_fusion.y_ref.yb_ref, ...), custom_call_target="tpu_custom_call" | custom-call | tf_op jit(solution)/shard_map/key_grads/pallas_call | solution.py:637
  417.5 4.7 all-to-all-start
  422.8 16.6 %collective-permute-done.32 = bf16[528,2048]{1,0:T(8,128)(2,1)} collective-permute-done((bf16[528,2048]{1,0:T(8,128)(2,1)}, bf16[528,2048]{1,0:T(8,128)(2,1)}, u32[]{:S(2)}, u32[]{:S(2)}) %collective-permute-start.32) | collective-permute-done | bytes 2162720 | tf_op jit(solution)/shard_map/ppermute | solution.py:291
  439.4 4.7 add_convert_fusion
  444.3 3.2 collective-permute-start.34
  449.6 7.2 collective-permute-done.31
  458.1 10.9 %all-reduce = (f32[2048]{0:T(1024)S(1)}, f32[2048]{0:T(1024)S(1)}) all-reduce(f32[2048]{0:T(1024)S(1)} %get-tuple-element.299, f32[2048]{0:T(1024)S(1)} %get-tuple-element.301), channel_id=1, replica_groups=mesh['seq'=8,'head'=4] {'head'}, use_global_device_ids=true, to_apply=%region_19.20 | all-reduce | flops 4096 | bytes 32768 | tf_op jit(solution)/shard_map/psum | solution.py:670
  469.3 9.3 %all-to-all-done = bf16[8,512,256]{2,1,0:T(8,128)(2,1)} async-done(((bf16[8,512,256]{2,1,0:T(8,128)(2,1)}), bf16[8,512,256]{2,1,0:T(8,128)(2,1)}, u32[]{:S(2)}, u32[]{:S(2)}) %all-to-all-start) | async-done | bytes 2097184 | tf_op jit(solution)/shard_map/all_to_all | solution.py:665
  478.6 22.2 %collective-permute-done.34.refs_4_ = bf16[544,2048]{1,0:T(8,128)(2,1)} collective-permute-done((bf16[544,2048]{1,0:T(8,128)(2,1)S(1)}, bf16[544,2048]{1,0:T(8,128)(2,1)}, u32[]{:S(2)}, u32[]{:S(2)}) %collective-permute-start.34) | collective-permute-done | bytes 2228256 | tf_op jit(solution)/shard_map/ppermute | solution.py:291
  501.2 10.9 %convolution_convert_fusion.3 = bf16[256,2048]{1,0:T(8,128)(2,1)S(1)} fusion(bf16[4096,256]{1,0:T(8,128)(2,1)} %bitcast.64, bf16[4096,2048]{1,0:T(8,128)(2,1)} %all-gather.2.cloned.1.call-done), kind=kOutput, calls=%fused_computation.22 | convolution fusion | flops 4295491584 | bytes 19922944 | tf_op jit(solution)/shard_map/dot_general | solution.py:359
  513.3 27.1 %collective-permute-done.36.other_ref = bf16[336,2048]{1,0:T(8,128)(2,1)S(1)} collective-permute-done((bf16[336,2048]{1,0:T(8,128)(2,1)S(1)}, bf16[336,2048]{1,0:T(8,128)(2,1)S(1)}, u32[]{:S(2)}, u32[]{:S(2)}) %collective-permute-start.36) | collective-permute-done | bytes 1376288 | tf_op jit(solution)/shard_map/ppermute | solution.py:291
  540.4 10.1 %collective-permute-done.35.refs_3_ = bf16[544,2048]{1,0:T(8,128)(2,1)S(1)} collective-permute-done((bf16[544,2048]{1,0:T(8,128)(2,1)S(1)}, bf16[544,2048]{1,0:T(8,128)(2,1)S(1)}, u32[]{:S(2)}, u32[]{:S(2)}) %collective-permute-start.35) | collective-permute-done | bytes 2228256 | tf_op jit(solution)/shard_map/ppermute | solution.py:291
  553.4 22.6 %collective-permute-start.37 = (bf16[544,2048]{1,0:T(8,128)(2,1)S(1)}, bf16[544,2048]{1,0:T(8,128)(2,1)S(1)}, u32[]{:S(2)}, u32[]{:S(2)}) collective-permute-start(bf16[544,2048]{1,0:T(8,128)(2,1)S(1)} %pad_maximum_fusion.refs_0_), channel_id=1, source_target_pairs={{0,24},{4,28},{8,0},{12,4},{16,8},{20,12},{24,16},{28,20},{1,25},{... | collective-permute-start | bytes 6684680 | tf_op jit(solution)/shard_map/ppermute | solution.py:291
  576.1 18.8 %collective-permute-done.38.refs_7_ = bf16[544,2048]{1,0:T(8,128)(2,1)S(1)} collective-permute-done((bf16[544,2048]{1,0:T(8,128)(2,1)S(1)}, bf16[544,2048]{1,0:T(8,128)(2,1)S(1)}, u32[]{:S(2)}, u32[]{:S(2)}) %collective-permute-start.38) | collective-permute-done | bytes 2228256 | tf_op jit(solution)/shard_map/ppermute | solution.py:291
  594.9 13.9 %collective-permute-done.37.refs_1_ = bf16[544,2048]{1,0:T(8,128)(2,1)S(1)} collective-permute-done((bf16[544,2048]{1,0:T(8,128)(2,1)S(1)}, bf16[544,2048]{1,0:T(8,128)(2,1)S(1)}, u32[]{:S(2)}, u32[]{:S(2)}) %collective-permute-start.37) | collective-permute-done | bytes 2228256 | tf_op jit(solution)/shard_map/ppermute | solution.py:291
  610.6 15.1 %collective-permute-start.40 = (bf16[272,2048]{1,0:T(8,128)(2,1)S(1)}, bf16[272,2048]{1,0:T(8,128)(2,1)S(1)}, u32[]{:S(2)}, u32[]{:S(2)}) collective-permute-start(bf16[272,2048]{1,0:T(8,128)(2,1)S(1)} %slice.285), channel_id=1, source_target_pairs={{0,24},{4,28},{8,0},{12,4},{16,8},{20,12},{24,16},{28,20},{1,25},{... | collective-permute-start | bytes 3342344 | tf_op jit(solution)/shard_map/ppermute | solution.py:291
  625.7 22.1 %collective-permute-done.40 = bf16[272,2048]{1,0:T(8,128)(2,1)S(1)} collective-permute-done((bf16[272,2048]{1,0:T(8,128)(2,1)S(1)}, bf16[272,2048]{1,0:T(8,128)(2,1)S(1)}, u32[]{:S(2)}, u32[]{:S(2)}) %collective-permute-start.40) | collective-permute-done | bytes 1114144 | tf_op jit(solution)/shard_map/ppermute | solution.py:291
  647.8 20.0 %collective-permute-done.39 = bf16[272,2048]{1,0:T(8,128)(2,1)S(1)} collective-permute-done((bf16[272,2048]{1,0:T(8,128)(2,1)S(1)}, bf16[272,2048]{1,0:T(8,128)(2,1)S(1)}, u32[]{:S(2)}, u32[]{:S(2)}) %collective-permute-start.39) | collective-permute-done | bytes 1114144 | tf_op jit(solution)/shard_map/ppermute | solution.py:291
  670.8 3.6 put_heads.4
  674.4 28.5 %collective-permute-done.43.own_ref = bf16[336,2048]{1,0:T(8,128)(2,1)S(1)} collective-permute-done((bf16[336,2048]{1,0:T(8,128)(2,1)S(1)}, bf16[336,2048]{1,0:T(8,128)(2,1)S(1)}, u32[]{:S(2)}, u32[]{:S(2)}) %collective-permute-start.43) | collective-permute-done | bytes 1376288 | tf_op jit(solution)/shard_map/ppermute | solution.py:291
  702.9 8.8 %collective-permute-done.42.refs_6_ = bf16[544,2048]{1,0:T(8,128)(2,1)} collective-permute-done((bf16[544,2048]{1,0:T(8,128)(2,1)S(1)}, bf16[544,2048]{1,0:T(8,128)(2,1)}, u32[]{:S(2)}, u32[]{:S(2)}) %collective-permute-start.42) | collective-permute-done | bytes 2228256 | tf_op jit(solution)/shard_map/ppermute | solution.py:291
  711.7 4.3 collective-permute-start.44
  719.1 20.5 %mlp_finish.1 = (f32[1376,2048]{1,0:T(8,128)}, f32[1376,2048]{1,0:T(8,128)}, f32[1376,2048]{1,0:T(8,128)}) custom-call(s32[8]{0:T(128)S(1)} %pad_add_fusion.6.at_ref, bf16[544,2048]{1,0:T(8,128)(2,1)S(1)} %pad_maximum_fusion.refs_0_, bf16[544,2048]{1,0:T(8,128)(2,1)S(1)} %collective-permute-done.37.refs_1_, bf16[544,2048]{1,0:T(8,128)(2,1)} %copy-done.64, ...), custom_call_target="tpu_custom_call" | custom-call | tf_op jit(solution)/shard_map/mlp_finish/pallas_call | solution.py:434
  739.7 5.1 collective-permute-done.44.own_ref
  747.1 3.7 fusion.27
  758.0 3.6 put_heads.5
  765.1 7.6 collective-permute-done.47
  772.6 3.5 collective-permute-done.48.other_ref
  793.0 3.6 put_heads.6
  797.6 8.8 %fusion.65 = f32[2048,8]{0,1:T(8,128)} fusion(bf16[4096,2048]{1,0:T(8,128)(2,1)} %all-gather.2.cloned.1.call-done, bf16[4096,8]{1,0:T(8,128)(2,1)S(1)} %copy-done.56), kind=kOutput, calls=%fused_computation.270 | convolution fusion | flops 134217728 | bytes 16908288 | tf_op jit(solution)/shard_map/dot_general | solution.py:359
  811.6 5.0 put_heads.7
  (520 shorter events, 195.9 us)
Async XLA Ops:
  8.0 107.7 %copy-start = (bf16[512,2048]{1,0:T(8,128)(2,1)S(1)}, bf16[512,2048]{1,0:T(8,128)(2,1)}, u32[]{:S(2)}) copy-start(bf16[512,2048]{1,0:T(8,128)(2,1)} %param.32) | copy-start | bytes 6291460
  8.0 364.7 %all-gather.2.cloned.1.call-start = ((), (), s32[]{:S(2)}) async-start(), calls=%async_computation.2 | async-start | bytes 17301504 | tf_op jit(solution)/shard_map/all_gather | solution.py:556
  10.7 15.0 %collective-permute-start = (bf16[128,2048]{1,0:T(8,128)(2,1)S(1)}, bf16[128,2048]{1,0:T(8,128)(2,1)S(1)}, u32[]{:S(2)}, u32[]{:S(2)}) collective-permute-start(bf16[128,2048]{1,0:T(8,128)(2,1)S(1)} %fusion.23), channel_id=1, source_target_pairs={{0,2},{1,3},{2,0},{3,1},{4,6},{5,7},{6,4},{7,5},{8,10},{9,11},{10,... | collective-permute-start | bytes 1572872 | tf_op jit(solution)/shard_map/ppermute | solution.py:319
  27.5 3.0 collective-permute-start.1
  32.1 28.2 %copy-start.88 = (bf16[128,2048]{1,0:T(8,128)(2,1)}, bf16[128,2048]{1,0:T(8,128)(2,1)S(1)}, u32[]{:S(2)}) copy-start(bf16[128,2048]{1,0:T(8,128)(2,1)S(1)} %get-tuple-element.348) | copy-start | bytes 1572868
  32.2 28.2 %copy-start.89 = (bf16[128,2048]{1,0:T(8,128)(2,1)}, bf16[128,2048]{1,0:T(8,128)(2,1)S(1)}, u32[]{:S(2)}) copy-start(bf16[128,2048]{1,0:T(8,128)(2,1)S(1)} %get-tuple-element.349) | copy-start | bytes 1572868
  49.8 6.7 collective-permute-start.2
  51.5 22.1 %collective-permute-start.5 = (bf16[128,2048]{1,0:T(8,128)(2,1)S(1)}, bf16[128,2048]{1,0:T(8,128)(2,1)S(1)}, u32[]{:S(2)}, u32[]{:S(2)}) collective-permute-start(bf16[128,2048]{1,0:T(8,128)(2,1)S(1)} %copy-done.59), channel_id=1, source_target_pairs={{0,2},{1,3},{2,0},{3,1},{4,6},{5,7},{6,4},{7,5},{8,10},{9,11},{10,... | collective-permute-start | bytes 1572872 | tf_op jit(solution)/shard_map/ppermute | solution.py:319
  56.5 17.9 %collective-permute-start.4 = (bf16[2,9,80,128]{3,2,1,0:T(8,128)(2,1)S(1)}, bf16[2,9,80,128]{3,2,1,0:T(8,128)(2,1)S(1)}, u32[]{:S(2)}, u32[]{:S(2)}) collective-permute-start(bf16[2,9,80,128]{3,2,1,0:T(8,128)(2,1)S(1)} %pad_maximum_fusion.12), channel_id=1, source_target_pairs={{0,24},{4,28},{8,0},{12,4},{16,8},{20,12},{24,16},{28,20},{1,25},{... | collective-permute-start | bytes 1105928 | tf_op jit(solution)/shard_map/ppermute | solution.py:291
  60.4 16.1 %collective-permute-start.3 = (bf16[2,9,80,128]{3,2,1,0:T(8,128)(2,1)S(1)}, bf16[2,9,80,128]{3,2,1,0:T(8,128)(2,1)S(1)}, u32[]{:S(2)}, u32[]{:S(2)}) collective-permute-start(bf16[2,9,80,128]{3,2,1,0:T(8,128)(2,1)S(1)} %pad_maximum_fusion.12), channel_id=1, source_target_pairs={{0,8},{4,12},{8,16},{12,20},{16,24},{20,28},{24,0},{28,4},{1,9},{5... | collective-permute-start | bytes 1105928 | tf_op jit(solution)/shard_map/ppermute | solution.py:291
  76.5 9.0 %collective-permute-start.6 = (bf16[1,9,80,128]{3,2,1,0:T(8,128)(2,1)S(1)}, bf16[1,9,80,128]{3,2,1,0:T(8,128)(2,1)S(1)}, u32[]{:S(2)}, u32[]{:S(2)}) collective-permute-start(bf16[1,9,80,128]{3,2,1,0:T(8,128)(2,1)S(1)} %slice.246), channel_id=1, source_target_pairs={{0,8},{4,12},{8,16},{12,20},{16,24},{20,28},{24,0},{28,4},{1,9},{5... | collective-permute-start | bytes 552968 | tf_op jit(solution)/shard_map/ppermute | solution.py:291
  78.9 8.4 %collective-permute-start.7 = (bf16[1,9,80,128]{3,2,1,0:T(8,128)(2,1)S(1)}, bf16[1,9,80,128]{3,2,1,0:T(8,128)(2,1)S(1)}, u32[]{:S(2)}, u32[]{:S(2)}) collective-permute-start(bf16[1,9,80,128]{3,2,1,0:T(8,128)(2,1)S(1)} %slice.247), channel_id=1, source_target_pairs={{0,24},{4,28},{8,0},{12,4},{16,8},{20,12},{24,16},{28,20},{1,25},{... | collective-permute-start | bytes 552968 | tf_op jit(solution)/shard_map/ppermute | solution.py:291
  88.7 328.4 %reduce-scatter.2.cloned.1.call-start = ((), (), s32[]{:S(2)}) async-start(), calls=%async_computation.3 | async-start | bytes 2359296 | tf_op jit(solution)/shard_map/reduce_scatter | solution.py:633
  121.1 3.0 collective-permute-start.8
  122.2 5.9 collective-permute-start.10
  126.6 14.0 %collective-permute-start.9 = (bf16[128,2048]{1,0:T(8,128)(2,1)S(1)}, bf16[128,2048]{1,0:T(8,128)(2,1)S(1)}, u32[]{:S(2)}, u32[]{:S(2)}) collective-permute-start(bf16[128,2048]{1,0:T(8,128)(2,1)S(1)} %select_bitcast_fusion.19), channel_id=1, source_target_pairs={{0,2},{1,3},{2,0},{3,1},{4,6},{5,7},{6,4},{7,5},{8,10},{9,11},{10,... | collective-permute-start | bytes 1572872 | tf_op jit(solution)/shard_map/ppermute | solution.py:319
  141.3 17.1 %collective-permute-start.11 = (bf16[128,2048]{1,0:T(8,128)(2,1)S(1)}, bf16[128,2048]{1,0:T(8,128)(2,1)S(1)}, u32[]{:S(2)}, u32[]{:S(2)}) collective-permute-start(bf16[128,2048]{1,0:T(8,128)(2,1)S(1)} %multiply_convert_fusion.2), channel_id=1, source_target_pairs={{0,2},{1,3},{2,0},{3,1},{4,6},{5,7},{6,4},{7,5},{8,10},{9,11},{10,... | collective-permute-start | bytes 1572872 | tf_op jit(solution)/shard_map/ppermute | solution.py:319
  158.4 4.9 collective-permute-start.12
  180.8 49.7 %collective-permute-start.15 = (bf16[528,2048]{1,0:T(8,128)(2,1)}, bf16[528,2048]{1,0:T(8,128)(2,1)}, u32[]{:S(2)}, u32[]{:S(2)}) collective-permute-start(bf16[528,2048]{1,0:T(8,128)(2,1)} %get-tuple-element.178), channel_id=1, source_target_pairs={{0,4},{4,0},{8,12},{12,8},{16,20},{20,16},{24,28},{28,24},{1,5},{5... | collective-permute-start | bytes 6488072 | tf_op jit(solution)/shard_map/ppermute | solution.py:291
  192.7 15.1 %collective-permute-start.13 = (bf16[2,128,2048]{2,1,0:T(8,128)(2,1)}, bf16[2,128,2048]{2,1,0:T(8,128)(2,1)}, u32[]{:S(2)}, u32[]{:S(2)}) collective-permute-start(bf16[2,128,2048]{2,1,0:T(8,128)(2,1)} %select_bitcast_fusion.2), channel_id=1, source_target_pairs={{0,1},{1,0},{2,3},{3,2},{4,5},{5,4},{6,7},{7,6},{8,9},{9,8},{10,11... | collective-permute-start | bytes 3145736 | tf_op jit(solution)/shard_map/ppermute | solution.py:319
  197.9 14.2 %collective-permute-start.21 = (bf16[2,128,2048]{2,1,0:T(8,128)(2,1)}, bf16[2,128,2048]{2,1,0:T(8,128)(2,1)}, u32[]{:S(2)}, u32[]{:S(2)}) collective-permute-start(bf16[2,128,2048]{2,1,0:T(8,128)(2,1)} %select_bitcast_fusion.1), channel_id=1, source_target_pairs={{0,1},{1,0},{2,3},{3,2},{4,5},{5,4},{6,7},{7,6},{8,9},{9,8},{10,11... | collective-permute-start | bytes 3145736 | tf_op jit(solution)/shard_map/ppermute | solution.py:319
  209.9 15.0 %collective-permute-start.14 = (bf16[128,2048]{1,0:T(8,128)(2,1)S(1)}, bf16[128,2048]{1,0:T(8,128)(2,1)S(1)}, u32[]{:S(2)}, u32[]{:S(2)}) collective-permute-start(bf16[128,2048]{1,0:T(8,128)(2,1)S(1)} %select_bitcast_fusion.10), channel_id=1, source_target_pairs={{0,2},{1,3},{2,0},{3,1},{4,6},{5,7},{6,4},{7,5},{8,10},{9,11},{10,... | collective-permute-start | bytes 1572872 | tf_op jit(solution)/shard_map/ppermute | solution.py:319
  214.0 41.8 %collective-permute-start.22 = (bf16[128,2048]{1,0:T(8,128)(2,1)S(1)}, bf16[128,2048]{1,0:T(8,128)(2,1)}, u32[]{:S(2)}, u32[]{:S(2)}) collective-permute-start(bf16[128,2048]{1,0:T(8,128)(2,1)S(1)} %select_bitcast_fusion.5), channel_id=1, source_target_pairs={{0,2},{1,3},{2,0},{3,1},{4,6},{5,7},{6,4},{7,5},{8,10},{9,11},{10,... | collective-permute-start | bytes 1572872 | tf_op jit(solution)/shard_map/ppermute | solution.py:319
  230.5 54.0 %collective-permute-start.17 = (bf16[528,2048]{1,0:T(8,128)(2,1)}, bf16[528,2048]{1,0:T(8,128)(2,1)}, u32[]{:S(2)}, u32[]{:S(2)}) collective-permute-start(bf16[528,2048]{1,0:T(8,128)(2,1)} %get-tuple-element.182), channel_id=1, source_target_pairs={{0,4},{4,0},{8,12},{12,8},{16,20},{20,16},{24,28},{28,24},{1,5},{5... | collective-permute-start | bytes 6488072 | tf_op jit(solution)/shard_map/ppermute | solution.py:291
  235.6 28.3 %collective-permute-start.18 = (bf16[256,2048]{1,0:T(8,128)(2,1)}, bf16[256,2048]{1,0:T(8,128)(2,1)}, u32[]{:S(2)}, u32[]{:S(2)}) collective-permute-start(bf16[256,2048]{1,0:T(8,128)(2,1)} %slice.336), channel_id=1, source_target_pairs={{0,8},{4,12},{8,16},{12,20},{16,24},{20,28},{24,0},{28,4},{1,9},{5... | collective-permute-start | bytes 3145736 | tf_op jit(solution)/shard_map/ppermute | solution.py:291
  236.4 48.1 %collective-permute-start.19 = (bf16[272,2048]{1,0:T(8,128)(2,1)S(1)}, bf16[272,2048]{1,0:T(8,128)(2,1)S(1)}, u32[]{:S(2)}, u32[]{:S(2)}) collective-permute-start(bf16[272,2048]{1,0:T(8,128)(2,1)S(1)} %slice.337), channel_id=1, source_target_pairs={{0,24},{4,28},{8,0},{12,4},{16,8},{20,12},{24,16},{28,20},{1,25},{... | collective-permute-start | bytes 3342344 | tf_op jit(solution)/shard_map/ppermute | solution.py:291
  240.4 17.7 %collective-permute-start.16 = (bf16[128,2048]{1,0:T(8,128)(2,1)S(1)}, bf16[128,2048]{1,0:T(8,128)(2,1)S(1)}, u32[]{:S(2)}, u32[]{:S(2)}) collective-permute-start(bf16[128,2048]{1,0:T(8,128)(2,1)S(1)} %fusion.52), channel_id=1, source_target_pairs={{0,2},{1,3},{2,0},{3,1},{4,6},{5,7},{6,4},{7,5},{8,10},{9,11},{10,... | collective-permute-start | bytes 1572872 | tf_op jit(solution)/shard_map/ppermute | solution.py:319
  255.7 28.9 %copy-start.69 = (bf16[528,2048]{1,0:T(8,128)(2,1)S(1)}, bf16[528,2048]{1,0:T(8,128)(2,1)}, u32[]{:S(2)}) copy-start(bf16[528,2048]{1,0:T(8,128)(2,1)} %get-tuple-element.201) | copy-start | bytes 6488068
  284.5 7.7 collective-permute-start.20
  290.6 82.2 %collective-permute-start.28 = (bf16[528,2048]{1,0:T(8,128)(2,1)}, bf16[528,2048]{1,0:T(8,128)(2,1)}, u32[]{:S(2)}, u32[]{:S(2)}) collective-permute-start(bf16[528,2048]{1,0:T(8,128)(2,1)} %get-tuple-element.206), channel_id=1, source_target_pairs={{0,4},{4,0},{8,12},{12,8},{16,20},{20,16},{24,28},{28,24},{1,5},{5... | collective-permute-start | bytes 6488072 | tf_op jit(solution)/shard_map/ppermute | solution.py:291
  291.0 81.7 %collective-permute-start.29 = (bf16[528,2048]{1,0:T(8,128)(2,1)}, bf16[528,2048]{1,0:T(8,128)(2,1)}, u32[]{:S(2)}, u32[]{:S(2)}) collective-permute-start(bf16[528,2048]{1,0:T(8,128)(2,1)} %pad_maximum_fusion.1), channel_id=1, source_target_pairs={{0,8},{4,12},{8,16},{12,20},{16,24},{20,28},{24,0},{28,4},{1,9},{5... | collective-permute-start | bytes 6488072 | tf_op jit(solution)/shard_map/ppermute | solution.py:291
  314.7 29.9 %collective-permute-start.23 = (bf16[4,80,128]{2,1,0:T(8,128)(2,1)S(1)}, bf16[4,80,128]{2,1,0:T(8,128)(2,1)}, u32[]{:S(2)}, u32[]{:S(2)}) collective-permute-start(bf16[4,80,128]{2,1,0:T(8,128)(2,1)S(1)} %get-tuple-element.188), channel_id=1, source_target_pairs={{0,4},{4,0},{8,12},{12,8},{16,20},{20,16},{24,28},{28,24},{1,5},{5... | collective-permute-start | bytes 245768 | tf_op jit(solution)/shard_map/ppermute | solution.py:291
  345.6 17.7 %collective-permute-start.25 = (bf16[2,4,80,128]{3,2,1,0:T(8,128)(2,1)S(1)}, bf16[2,4,80,128]{3,2,1,0:T(8,128)(2,1)S(1)}, u32[]{:S(2)}, u32[]{:S(2)}) collective-permute-start(bf16[2,4,80,128]{3,2,1,0:T(8,128)(2,1)S(1)} %pad_maximum_fusion.15), channel_id=1, source_target_pairs={{0,24},{4,28},{8,0},{12,4},{16,8},{20,12},{24,16},{28,20},{1,25},{... | collective-permute-start | bytes 491528 | tf_op jit(solution)/shard_map/ppermute | solution.py:291
  347.9 17.7 %collective-permute-start.24 = (bf16[2,4,80,128]{3,2,1,0:T(8,128)(2,1)S(1)}, bf16[2,4,80,128]{3,2,1,0:T(8,128)(2,1)S(1)}, u32[]{:S(2)}, u32[]{:S(2)}) collective-permute-start(bf16[2,4,80,128]{3,2,1,0:T(8,128)(2,1)S(1)} %pad_maximum_fusion.15), channel_id=1, source_target_pairs={{0,8},{4,12},{8,16},{12,20},{16,24},{20,28},{24,0},{28,4},{1,9},{5... | collective-permute-start | bytes 491528 | tf_op jit(solution)/shard_map/ppermute | solution.py:291
  347.9 74.8 %collective-permute-start.33 = (bf16[528,2048]{1,0:T(8,128)(2,1)}, bf16[528,2048]{1,0:T(8,128)(2,1)}, u32[]{:S(2)}, u32[]{:S(2)}) collective-permute-start(bf16[528,2048]{1,0:T(8,128)(2,1)} %get-tuple-element.224), channel_id=1, source_target_pairs={{0,4},{4,0},{8,12},{12,8},{16,20},{20,16},{24,28},{28,24},{1,5},{5... | collective-permute-start | bytes 6488072 | tf_op jit(solution)/shard_map/ppermute | solution.py:291
  365.6 6.3 collective-permute-start.26
  365.6 6.2 collective-permute-start.27
  379.2 60.2 %collective-permute-start.32 = (bf16[528,2048]{1,0:T(8,128)(2,1)}, bf16[528,2048]{1,0:T(8,128)(2,1)}, u32[]{:S(2)}, u32[]{:S(2)}) collective-permute-start(bf16[528,2048]{1,0:T(8,128)(2,1)} %pad_maximum_fusion.2), channel_id=1, source_target_pairs={{0,24},{4,28},{8,0},{12,4},{16,8},{20,12},{24,16},{28,20},{1,25},{... | collective-permute-start | bytes 6488072 | tf_op jit(solution)/shard_map/ppermute | solution.py:291
  416.9 5.3 collective-permute-start.30
  417.5 61.1 %all-to-all-start = ((bf16[8,512,256]{2,1,0:T(8,128)(2,1)}), bf16[8,512,256]{2,1,0:T(8,128)(2,1)}, u32[]{:S(2)}, u32[]{:S(2)}) async-start(bf16[8,512,256]{2,1,0:T(8,128)(2,1)} %get-tuple-element.218), calls=%async_computation.1 | async-start | bytes 4194304 | tf_op jit(solution)/shard_map/all_to_all | solution.py:665
  444.3 56.5 %collective-permute-start.34 = (bf16[544,2048]{1,0:T(8,128)(2,1)S(1)}, bf16[544,2048]{1,0:T(8,128)(2,1)}, u32[]{:S(2)}, u32[]{:S(2)}) collective-permute-start(bf16[544,2048]{1,0:T(8,128)(2,1)S(1)} %pad_maximum_fusion.refs_0_), channel_id=1, source_target_pairs={{0,4},{4,0},{8,12},{12,8},{16,20},{20,16},{24,28},{28,24},{1,5},{5... | collective-permute-start | bytes 6684680 | tf_op jit(solution)/shard_map/ppermute | solution.py:291
  447.5 9.2 %collective-permute-start.31 = (bf16[128,2048]{1,0:T(8,128)(2,1)S(1)}, bf16[128,2048]{1,0:T(8,128)(2,1)S(1)}, u32[]{:S(2)}, u32[]{:S(2)}) collective-permute-start(bf16[128,2048]{1,0:T(8,128)(2,1)S(1)} %select_bitcast_fusion.4), channel_id=1, source_target_pairs={{0,2},{1,3},{2,0},{3,1},{4,6},{5,7},{6,4},{7,5},{8,10},{9,11},{10,... | collective-permute-start | bytes 1572872 | tf_op jit(solution)/shard_map/ppermute | solution.py:319
  500.8 49.7 %collective-permute-start.35 = (bf16[544,2048]{1,0:T(8,128)(2,1)S(1)}, bf16[544,2048]{1,0:T(8,128)(2,1)S(1)}, u32[]{:S(2)}, u32[]{:S(2)}) collective-permute-start(bf16[544,2048]{1,0:T(8,128)(2,1)S(1)} %pad_maximum_fusion.refs_0_), channel_id=1, source_target_pairs={{0,8},{4,12},{8,16},{12,20},{16,24},{20,28},{24,0},{28,4},{1,9},{5... | collective-permute-start | bytes 6684680 | tf_op jit(solution)/shard_map/ppermute | solution.py:291
  512.3 28.0 %collective-permute-start.36 = (bf16[336,2048]{1,0:T(8,128)(2,1)S(1)}, bf16[336,2048]{1,0:T(8,128)(2,1)S(1)}, u32[]{:S(2)}, u32[]{:S(2)}) collective-permute-start(bf16[336,2048]{1,0:T(8,128)(2,1)S(1)} %pad_maximum_fusion.7.own_ref), channel_id=1, source_target_pairs={{0,4},{4,0},{8,12},{12,8},{16,20},{20,16},{24,28},{28,24},{1,5},{5... | collective-permute-start | bytes 4128776 | tf_op jit(solution)/shard_map/ppermute | solution.py:291
  540.3 130.5 %copy-start.28 = (bf16[336,2048]{1,0:T(8,128)(2,1)}, bf16[336,2048]{1,0:T(8,128)(2,1)S(1)}, u32[]{:S(2)}) copy-start(bf16[336,2048]{1,0:T(8,128)(2,1)S(1)} %collective-permute-done.36.other_ref) | copy-start | bytes 4128772
  550.5 60.1 %copy-start.63 = (bf16[544,2048]{1,0:T(8,128)(2,1)}, bf16[544,2048]{1,0:T(8,128)(2,1)S(1)}, u32[]{:S(2)}) copy-start(bf16[544,2048]{1,0:T(8,128)(2,1)S(1)} %collective-permute-done.35.refs_3_) | copy-start | bytes 6684676
  550.5 44.4 %collective-permute-start.38 = (bf16[544,2048]{1,0:T(8,128)(2,1)S(1)}, bf16[544,2048]{1,0:T(8,128)(2,1)S(1)}, u32[]{:S(2)}, u32[]{:S(2)}) collective-permute-start(bf16[544,2048]{1,0:T(8,128)(2,1)S(1)} %collective-permute-done.35.refs_3_), channel_id=1, source_target_pairs={{0,4},{4,0},{8,12},{12,8},{16,20},{20,16},{24,28},{28,24},{1,5},{5... | collective-permute-start | bytes 6684680 | tf_op jit(solution)/shard_map/ppermute | solution.py:291
  553.4 55.4 %collective-permute-start.37 = (bf16[544,2048]{1,0:T(8,128)(2,1)S(1)}, bf16[544,2048]{1,0:T(8,128)(2,1)S(1)}, u32[]{:S(2)}, u32[]{:S(2)}) collective-permute-start(bf16[544,2048]{1,0:T(8,128)(2,1)S(1)} %pad_maximum_fusion.refs_0_), channel_id=1, source_target_pairs={{0,24},{4,28},{8,0},{12,4},{16,8},{20,12},{24,16},{28,20},{1,25},{... | collective-permute-start | bytes 6684680 | tf_op jit(solution)/shard_map/ppermute | solution.py:291
  594.9 73.1 %copy-start.67 = (bf16[544,2048]{1,0:T(8,128)(2,1)}, bf16[544,2048]{1,0:T(8,128)(2,1)S(1)}, u32[]{:S(2)}) copy-start(bf16[544,2048]{1,0:T(8,128)(2,1)S(1)} %collective-permute-done.38.refs_7_) | copy-start | bytes 6684676
  608.8 58.9 %collective-permute-start.41 = (bf16[544,2048]{1,0:T(8,128)(2,1)S(1)}, bf16[544,2048]{1,0:T(8,128)(2,1)S(1)}, u32[]{:S(2)}, u32[]{:S(2)}) collective-permute-start(bf16[544,2048]{1,0:T(8,128)(2,1)S(1)} %collective-permute-done.37.refs_1_), channel_id=1, source_target_pairs={{0,4},{4,0},{8,12},{12,8},{16,20},{20,16},{24,28},{28,24},{1,5},{5... | collective-permute-start | bytes 6684680 | tf_op jit(solution)/shard_map/ppermute | solution.py:291
  610.6 37.2 %collective-permute-start.40 = (bf16[272,2048]{1,0:T(8,128)(2,1)S(1)}, bf16[272,2048]{1,0:T(8,128)(2,1)S(1)}, u32[]{:S(2)}, u32[]{:S(2)}) collective-permute-start(bf16[272,2048]{1,0:T(8,128)(2,1)S(1)} %slice.285), channel_id=1, source_target_pairs={{0,24},{4,28},{8,0},{12,4},{16,8},{20,12},{24,16},{28,20},{1,25},{... | collective-permute-start | bytes 3342344 | tf_op jit(solution)/shard_map/ppermute | solution.py:291
  625.7 42.1 %collective-permute-start.39 = (bf16[272,2048]{1,0:T(8,128)(2,1)S(1)}, bf16[272,2048]{1,0:T(8,128)(2,1)S(1)}, u32[]{:S(2)}, u32[]{:S(2)}) collective-permute-start(bf16[272,2048]{1,0:T(8,128)(2,1)S(1)} %slice.284), channel_id=1, source_target_pairs={{0,8},{4,12},{8,16},{12,20},{16,24},{20,28},{24,0},{28,4},{1,9},{5... | collective-permute-start | bytes 3342344 | tf_op jit(solution)/shard_map/ppermute | solution.py:291
  667.8 49.9 %copy-start.43 = (f32[8,72,128]{2,1,0:T(8,128)S(1)}, f32[8,72,128]{2,1,0:T(8,128)}, u32[]{:S(2)}) copy-start(f32[8,72,128]{2,1,0:T(8,128)} %copy-done.42) | copy-start | bytes 884740
  669.1 50.0 %copy-start.64 = (bf16[544,2048]{1,0:T(8,128)(2,1)}, bf16[544,2048]{1,0:T(8,128)(2,1)S(1)}, u32[]{:S(2)}) copy-start(bf16[544,2048]{1,0:T(8,128)(2,1)S(1)} %constant_dynamic-update-slice_fusion.12.refs_2_) | copy-start | bytes 6684676
  669.1 42.6 %collective-permute-start.42 = (bf16[544,2048]{1,0:T(8,128)(2,1)S(1)}, bf16[544,2048]{1,0:T(8,128)(2,1)}, u32[]{:S(2)}, u32[]{:S(2)}) collective-permute-start(bf16[544,2048]{1,0:T(8,128)(2,1)S(1)} %constant_dynamic-update-slice_fusion.12.refs_2_), channel_id=1, source_target_pairs={{0,4},{4,0},{8,12},{12,8},{16,20},{20,16},{24,28},{28,24},{1,5},{5... | collective-permute-start | bytes 6684680 | tf_op jit(solution)/shard_map/ppermute | solution.py:291
  670.7 32.2 %collective-permute-start.43 = (bf16[336,2048]{1,0:T(8,128)(2,1)S(1)}, bf16[336,2048]{1,0:T(8,128)(2,1)S(1)}, u32[]{:S(2)}, u32[]{:S(2)}) collective-permute-start(bf16[336,2048]{1,0:T(8,128)(2,1)S(1)} %pad_maximum_fusion.7.own_ref), channel_id=1, source_target_pairs={{0,8},{4,12},{8,16},{12,20},{16,24},{20,28},{24,0},{28,4},{1,9},{5... | collective-permute-start | bytes 4128776 | tf_op jit(solution)/shard_map/ppermute | solution.py:291
  702.9 55.1 %copy-start.24 = (bf16[336,2048]{1,0:T(8,128)(2,1)}, bf16[336,2048]{1,0:T(8,128)(2,1)S(1)}, u32[]{:S(2)}) copy-start(bf16[336,2048]{1,0:T(8,128)(2,1)S(1)} %collective-permute-done.43.own_ref) | copy-start | bytes 4128772
  711.7 33.1 %collective-permute-start.44 = (bf16[336,2048]{1,0:T(8,128)(2,1)S(1)}, bf16[336,2048]{1,0:T(8,128)(2,1)S(1)}, u32[]{:S(2)}, u32[]{:S(2)}) collective-permute-start(bf16[336,2048]{1,0:T(8,128)(2,1)S(1)} %pad_maximum_fusion.7.own_ref), channel_id=1, source_target_pairs={{0,24},{4,28},{8,0},{12,4},{16,8},{20,12},{24,16},{28,20},{1,25},{... | collective-permute-start | bytes 4128776 | tf_op jit(solution)/shard_map/ppermute | solution.py:291
  716.0 28.8 %collective-permute-start.45 = (bf16[336,2048]{1,0:T(8,128)(2,1)S(1)}, bf16[336,2048]{1,0:T(8,128)(2,1)S(1)}, u32[]{:S(2)}, u32[]{:S(2)}) collective-permute-start(bf16[336,2048]{1,0:T(8,128)(2,1)S(1)} %collective-permute-done.43.own_ref), channel_id=1, source_target_pairs={{0,4},{4,0},{8,12},{12,8},{16,20},{20,16},{24,28},{28,24},{1,5},{5... | collective-permute-start | bytes 4128776 | tf_op jit(solution)/shard_map/ppermute | solution.py:291
  717.8 59.6 %copy-start.109 = (s32[1024]{0:T(1024)}, s32[1024]{0:T(1024)S(1)}, u32[]{:S(2)}) copy-start(s32[1024]{0:T(1024)S(1)} %pad_clamp_fusion) | copy-start | bytes 12292
  744.8 31.4 %collective-permute-start.48 = (bf16[336,2048]{1,0:T(8,128)(2,1)S(1)}, bf16[336,2048]{1,0:T(8,128)(2,1)S(1)}, u32[]{:S(2)}, u32[]{:S(2)}) collective-permute-start(bf16[336,2048]{1,0:T(8,128)(2,1)S(1)} %collective-permute-done.44.own_ref), channel_id=1, source_target_pairs={{0,4},{4,0},{8,12},{12,8},{16,20},{20,16},{24,28},{28,24},{1,5},{5... | collective-permute-start | bytes 4128776 | tf_op jit(solution)/shard_map/ppermute | solution.py:291
  752.5 12.6 %collective-permute-start.46 = (bf16[160,2048]{1,0:T(8,128)(2,1)S(1)}, bf16[160,2048]{1,0:T(8,128)(2,1)S(1)}, u32[]{:S(2)}, u32[]{:S(2)}) collective-permute-start(bf16[160,2048]{1,0:T(8,128)(2,1)S(1)} %slice.288), channel_id=1, source_target_pairs={{0,8},{4,12},{8,16},{12,20},{16,24},{20,28},{24,0},{28,4},{1,9},{5... | collective-permute-start | bytes 1966088 | tf_op jit(solution)/shard_map/ppermute | solution.py:291
  754.4 18.3 %collective-permute-start.47 = (bf16[176,2048]{1,0:T(8,128)(2,1)S(1)}, bf16[176,2048]{1,0:T(8,128)(2,1)S(1)}, u32[]{:S(2)}, u32[]{:S(2)}) collective-permute-start(bf16[176,2048]{1,0:T(8,128)(2,1)S(1)} %slice.289), channel_id=1, source_target_pairs={{0,24},{4,28},{8,0},{12,4},{16,8},{20,12},{24,16},{28,20},{1,25},{... | collective-permute-start | bytes 2162696 | tf_op jit(solution)/shard_map/ppermute | solution.py:291
  782.8 23.5 %collective-permute-start.49 = (bf16[336,2048]{1,0:T(8,128)(2,1)S(1)}, bf16[336,2048]{1,0:T(8,128)(2,1)}, u32[]{:S(2)}, u32[]{:S(2)}) collective-permute-start(bf16[336,2048]{1,0:T(8,128)(2,1)S(1)} %constant_dynamic-update-slice_fusion.14.own_ref), channel_id=1, source_target_pairs={{0,4},{4,0},{8,12},{12,8},{16,20},{20,16},{24,28},{28,24},{1,5},{5... | collective-permute-start | bytes 4128776 | tf_op jit(solution)/shard_map/ppermute | solution.py:291
  (119 other events, 1039.3 us)
Sparse Core Ops, SparseCore 0:
  88.9 116.2 all-gather.1
Sparse Core Ops, SparseCore 1:
  322.4 87.2 reduce-scatter.1

commit v5 on v4

--- a/solution.py
+++ b/solution.py
@@ -608,8 +608,9 @@
         from_left, got3 = shift(up, 1, 0), shift(sent, 0, 1)
     else:
         d_attn_group = head_gather(d_attn)
+    out_weight_grad = dot(gated_out, d_attn_group, 0, 0).astype(BF)
+    d_attn_group, out_weight_grad = together(d_attn_group, out_weight_grad)
     d_gated = dot(d_attn_group, out_weight, 1, 1)
-    out_weight_grad = dot(gated_out, d_attn_group, 0, 0).astype(BF)
     d_post = d_gated * gate_act
     d_gate_pre = gelu_back(d_gated * post_out)[0].astype(BF)
     post_gain_part = jnp.sum(d_post * z_hat, axis=0)
@@ -691,13 +692,12 @@
         far_a, far_b = shift(left2[:h], 1, 0), shift(right2[h:], 3, 0)
         crossed_right2 = shift(right2, 0, 1)
         head_sums = put_heads(3, left2, crossed_left2, head_sums)
+        head_sums, small_rows = together(head_sums, [v[-16:-12] for v in pieces])
         far_a, far_b, crossed_right2, head_sums = together(
             far_a, far_b, crossed_right2, head_sums
         )
         gate_sum, up_sum, down_sum = mlp_sums
         gate_sum, up_sum = gate_sum.T, up_sum.T
-        small_rows = [v[-16:-12] for v in pieces]
-        far_a, far_b, small_rows = together(far_a, far_b, small_rows)
         from_all = in_order(small_rows)
         count = tokens * local_heads
         d_rate_all = from_all[:, :count].reshape(segs * tokens, local_heads)

time: 836 us -> 831 us (level)
    unnamed x285 -> x261, local copies, waits for them, and re-layouts: 42.8 us -> 39.4 us
  transfers between devices with their start and end apart: 53 -> 53, of which waited for: 33 -> 33; matrix products, arithmetic and copies ran while one was open for 17% -> 18% of each run, Pallas kernels for 14% -> 14%
where the time goes in v5:
time: 831 us; the launch traced here: 816 us
  waiting for transfers between devices  343 us (41%)
  Pallas kernels  130 us (16%)
  starting transfers between devices  111 us (13%)
  matrix products  73.6 us (9%)
  other arithmetic  62.9 us (8%)
  local copies, waits for them, and re-layouts  53.8 us (6%)
  blocking collectives  24.4 us (3%)
  between operations  17.5 us (2%)
    ppermute x34, waiting for transfers between devices, shift(): return lax.ppermute(v, 'seq', pairs)  274 us
    ppermute x34, starting transfers between devices, shift(): return lax.ppermute(v, 'seq', pairs)  90.9 us
    dot_general x21, matrix products, dot(): lax.dot_general(a, b, (((ca,), (cb,)), ((), ())), preferred_element_type=...  73.6 us
    ppermute x16, waiting for transfers between devices, head_shift(): return lax.ppermute(v, 'head', pairs)  59.9 us
    unnamed x261, local copies, waits for them, and re-layouts  39.4 us
    pallas_call x4, Pallas kernels, mlp_slices(): pl.pallas_call(slices_kernel, grid_spec=pltpu.PrefetchScalarGridSpec(num_...  26.4 us
    pallas_call x1, Pallas kernels, body(): K['kgrad']  23.1 us
    pallas_call x1, Pallas kernels, finish(): pl.pallas_call(functools.partial(finish_kernel, plan), grid_spec=pltpu.Pr...  20.5 us
  transfers between devices with their start and end apart: 53, of which 33 were waited for; matrix products, arithmetic and copies ran while one was open for 18% of the time, Pallas kernels for 14%

profile of v5, /device:TPU:0, one launch (start us, length us, event | category | flops | bytes accessed | tf_op | source)
XLA Modules:
  0.0 815.8 jit_solution(9600856774995465967)
XLA Ops:
  15.0 10.7 %collective-permute-done = bf16[128,2048]{1,0:T(8,128)(2,1)S(1)} collective-permute-done((bf16[128,2048]{1,0:T(8,128)(2,1)S(1)}, bf16[128,2048]{1,0:T(8,128)(2,1)S(1)}, u32[]{:S(2)}, u32[]{:S(2)}) %collective-permute-start) | collective-permute-done | bytes 524320 | tf_op jit(solution)/shard_map/ppermute | solution.py:319
  38.7 11.1 %segment_maps.1 = (bf16[8,4,128,128]{3,2,1,0:T(8,128)(2,1)S(1)}, bf16[8,512,256]{2,1,0:T(8,128)(2,1)S(1)}, bf16[8,4,128,256]{3,2,1,0:T(8,128)(2,1)}, bf16[9,80,128]{2,1,0:T(8,128)(2,1)S(1)}) custom-call(f32[512,512]{1,0:T(8,128)S(1)} %fusion.52.k_ref, f32[512,512]{1,0:T(8,128)S(1)} %fusion.51.v_ref, f32[512,8]{1,0:T(8,128)S(1)} %get-tuple-element.370.r_ref), custom_call_target="tpu_custom_call" | custom-call | tf_op jit(solution)/shard_map/segment_maps/pallas_call | solution.py:545
  53.0 3.4 collective-permute-done.2
  56.5 3.9 collective-permute-start.4
  61.7 8.2 %local_parts.1 = (bf16[8,512,128]{2,1,0:T(8,128)(2,1)S(1)}, f32[512,512]{1,0:T(8,128)S(1)}, bf16[8,4,128,128]{3,2,1,0:T(8,128)(2,1)S(1)}, bf16[8,512,128]{2,1,0:T(8,128)(2,1)S(1)}) custom-call(f32[512,512]{1,0:T(8,128)S(1)} %fusion.50.q_ref, f32[512,512]{1,0:T(8,128)} %copy-done.8, f32[512,8]{1,0:T(8,128)S(1)} %get-tuple-element.370.r_ref, ...), custom_call_target="tpu_custom_call" | custom-call | tf_op jit(solution)/shard_map/local_parts/pallas_call | solution.py:549
  81.9 3.6 collective-permute-done.6
  90.1 9.9 %forward_states.1 = (f32[512,512]{1,0:T(8,128)}, bf16[8,512,128]{2,1,0:T(8,128)(2,1)S(1)}, bf16[8,4,128,128]{3,2,1,0:T(8,128)(2,1)S(1)}) custom-call(s32[9]{0:T(128)S(1)} %pad_add_fusion.seg_ref, bf16[8,9,80,128]{3,2,1,0:T(8,128)(2,1)} %constant_dynamic-update-slice_fusion.y_ref.yb_ref, ...), custom_call_target="tpu_custom_call" | custom-call | tf_op jit(solution)/shard_map/forward_states/pallas_call | solution.py:558
  103.5 6.5 all-reduce.2
  110.0 5.0 multiply_convert_fusion.3
  129.6 11.0 %collective-permute-done.9 = bf16[128,2048]{1,0:T(8,128)(2,1)S(1)} collective-permute-done((bf16[128,2048]{1,0:T(8,128)(2,1)S(1)}, bf16[128,2048]{1,0:T(8,128)(2,1)S(1)}, u32[]{:S(2)}, u32[]{:S(2)}) %collective-permute-start.9) | collective-permute-done | bytes 524320 | tf_op jit(solution)/shard_map/ppermute | solution.py:319
  143.1 15.2 %collective-permute-done.11 = bf16[128,2048]{1,0:T(8,128)(2,1)S(1)} collective-permute-done((bf16[128,2048]{1,0:T(8,128)(2,1)S(1)}, bf16[128,2048]{1,0:T(8,128)(2,1)S(1)}, u32[]{:S(2)}, u32[]{:S(2)}) %collective-permute-start.11) | collective-permute-done | bytes 524320 | tf_op jit(solution)/shard_map/ppermute | solution.py:319
  160.1 3.1 convolution_bitcast_fusion.2
  165.2 3.1 convolution_bitcast_fusion
  168.3 5.6 multiply_convert_fusion
  173.9 6.7 mlp_slices.4
  182.1 5.6 fusion.57
  187.7 3.7 add_convert_fusion.5
  192.8 3.8 convolution_convert_fusion.2
  201.1 6.6 mlp_slices.5
  214.1 10.7 %collective-permute-done.14 = bf16[128,2048]{1,0:T(8,128)(2,1)S(1)} collective-permute-done((bf16[128,2048]{1,0:T(8,128)(2,1)S(1)}, bf16[128,2048]{1,0:T(8,128)(2,1)S(1)}, u32[]{:S(2)}, u32[]{:S(2)}) %collective-permute-start.14) | collective-permute-done | bytes 524320 | tf_op jit(solution)/shard_map/ppermute | solution.py:319
  224.8 5.6 collective-permute-done.15
  242.7 6.7 mlp_slices.7
  249.4 6.3 mlp_slices.6
  258.1 5.7 collective-permute-done.18
  263.8 20.6 %collective-permute-done.19 = bf16[272,2048]{1,0:T(8,128)(2,1)S(1)} collective-permute-done((bf16[272,2048]{1,0:T(8,128)(2,1)S(1)}, bf16[272,2048]{1,0:T(8,128)(2,1)S(1)}, u32[]{:S(2)}, u32[]{:S(2)}) %collective-permute-start.19) | collective-permute-done | bytes 1114144 | tf_op jit(solution)/shard_map/ppermute | solution.py:291
  296.7 5.2 multiply_reduce_fusion.1
  302.0 7.0 all-reduce.1
  310.6 5.8 state_grads.1
  317.4 3.3 fusion.60
  323.2 9.1 %query_grads.1 = (bf16[512,512]{1,0:T(8,128)(2,1)S(1)}, bf16[8,512,128]{2,1,0:T(8,128)(2,1)S(1)}, f32[8,512,128]{2,1,0:T(8,128)}) custom-call(f32[512,512]{1,0:T(8,128)S(1)} %copy-done.17, f32[512,512]{1,0:T(8,128)S(1)} %copy-done.9, f32[512,8]{1,0:T(8,128)S(1)} %copy-done.12, f32[512,512]{1,0:T(8,128)S(1)} %subtract_multiply_fusion.1.dz_ref, ...), custom_call_target="tpu_custom_call" | custom-call | tf_op jit(solution)/shard_map/query_grads/pallas_call | solution.py:626
  334.0 10.5 %collective-permute-done.23 = bf16[4,80,128]{2,1,0:T(8,128)(2,1)} collective-permute-done((bf16[4,80,128]{2,1,0:T(8,128)(2,1)S(1)}, bf16[4,80,128]{2,1,0:T(8,128)(2,1)}, u32[]{:S(2)}, u32[]{:S(2)}) %collective-permute-start.23) | collective-permute-done | bytes 81952 | tf_op jit(solution)/shard_map/ppermute | solution.py:291
  349.3 13.6 %collective-permute-done.25 = bf16[2,4,80,128]{3,2,1,0:T(8,128)(2,1)S(1)} collective-permute-done((bf16[2,4,80,128]{3,2,1,0:T(8,128)(2,1)S(1)}, bf16[2,4,80,128]{3,2,1,0:T(8,128)(2,1)S(1)}, u32[]{:S(2)}, u32[]{:S(2)}) %collective-permute-start.25) | collective-permute-done | bytes 163872 | tf_op jit(solution)/shard_map/ppermute | solution.py:291
  366.0 4.0 collective-permute-start.27
  373.2 3.1 add_convert_fusion.1
  379.6 3.9 collective-permute-start.32
  383.6 23.1 %key_grads.1 = (bf16[512,512]{1,0:T(8,128)(2,1)S(1)}, bf16[512,512]{1,0:T(8,128)(2,1)S(1)}, f32[512,8]{1,0:T(8,128)S(1)}, f32[8,72,128]{2,1,0:T(8,128)S(1)}, bf16[8,512,256]{2,1,0:T(8,128)(2,1)}) custom-call(s32[9]{0:T(128)S(1)} %pad_add_fusion.seg_ref, bf16[8,9,80,128]{3,2,1,0:T(8,128)(2,1)} %constant_dynamic-update-slice_fusion.y_ref.yb_ref, ...), custom_call_target="tpu_custom_call" | custom-call | tf_op jit(solution)/shard_map/key_grads/pallas_call | solution.py:638
  417.8 4.7 all-to-all-start
  423.1 16.7 %collective-permute-done.32 = bf16[528,2048]{1,0:T(8,128)(2,1)} collective-permute-done((bf16[528,2048]{1,0:T(8,128)(2,1)}, bf16[528,2048]{1,0:T(8,128)(2,1)}, u32[]{:S(2)}, u32[]{:S(2)}) %collective-permute-start.32) | collective-permute-done | bytes 2162720 | tf_op jit(solution)/shard_map/ppermute | solution.py:291
  439.8 4.7 add_convert_fusion
  449.0 8.0 collective-permute-done.31
  458.4 10.9 %all-reduce = (f32[2048]{0:T(1024)S(1)}, f32[2048]{0:T(1024)S(1)}) all-reduce(f32[2048]{0:T(1024)S(1)} %get-tuple-element.309, f32[2048]{0:T(1024)S(1)} %get-tuple-element.311), channel_id=1, replica_groups=mesh['seq'=8,'head'=4] {'head'}, use_global_device_ids=true, to_apply=%region_19.20 | all-reduce | flops 4096 | bytes 32768 | tf_op jit(solution)/shard_map/psum | solution.py:671
  469.5 9.7 %all-to-all-done = bf16[8,512,256]{2,1,0:T(8,128)(2,1)} async-done(((bf16[8,512,256]{2,1,0:T(8,128)(2,1)}), bf16[8,512,256]{2,1,0:T(8,128)(2,1)}, u32[]{:S(2)}, u32[]{:S(2)}) %all-to-all-start) | async-done | bytes 2097184 | tf_op jit(solution)/shard_map/all_to_all | solution.py:666
  479.3 22.3 %collective-permute-done.34.refs_4_ = bf16[544,2048]{1,0:T(8,128)(2,1)} collective-permute-done((bf16[544,2048]{1,0:T(8,128)(2,1)S(1)}, bf16[544,2048]{1,0:T(8,128)(2,1)}, u32[]{:S(2)}, u32[]{:S(2)}) %collective-permute-start.34) | collective-permute-done | bytes 2228256 | tf_op jit(solution)/shard_map/ppermute | solution.py:291
  502.0 10.9 %convolution_convert_fusion.3 = bf16[256,2048]{1,0:T(8,128)(2,1)S(1)} fusion(bf16[4096,256]{1,0:T(8,128)(2,1)} %bitcast.64, bf16[4096,2048]{1,0:T(8,128)(2,1)} %all-gather.2.cloned.1.call-done), kind=kOutput, calls=%fused_computation.22 | convolution fusion | flops 4295491584 | bytes 19922944 | tf_op jit(solution)/shard_map/dot_general | solution.py:359
  513.7 26.9 %collective-permute-done.36.other_ref = bf16[336,2048]{1,0:T(8,128)(2,1)S(1)} collective-permute-done((bf16[336,2048]{1,0:T(8,128)(2,1)S(1)}, bf16[336,2048]{1,0:T(8,128)(2,1)S(1)}, u32[]{:S(2)}, u32[]{:S(2)}) %collective-permute-start.36) | collective-permute-done | bytes 1376288 | tf_op jit(solution)/shard_map/ppermute | solution.py:291
  540.6 9.9 %collective-permute-done.35.refs_3_ = bf16[544,2048]{1,0:T(8,128)(2,1)S(1)} collective-permute-done((bf16[544,2048]{1,0:T(8,128)(2,1)S(1)}, bf16[544,2048]{1,0:T(8,128)(2,1)S(1)}, u32[]{:S(2)}, u32[]{:S(2)}) %collective-permute-start.35) | collective-permute-done | bytes 2228256 | tf_op jit(solution)/shard_map/ppermute | solution.py:291
  553.2 23.4 %collective-permute-start.37 = (bf16[544,2048]{1,0:T(8,128)(2,1)S(1)}, bf16[544,2048]{1,0:T(8,128)(2,1)S(1)}, u32[]{:S(2)}, u32[]{:S(2)}) collective-permute-start(bf16[544,2048]{1,0:T(8,128)(2,1)S(1)} %pad_maximum_fusion.refs_0_), channel_id=1, source_target_pairs={{0,24},{4,28},{8,0},{12,4},{16,8},{20,12},{24,16},{28,20},{1,25},{... | collective-permute-start | bytes 6684680 | tf_op jit(solution)/shard_map/ppermute | solution.py:291
  576.6 23.2 %collective-permute-done.38.refs_7_ = bf16[544,2048]{1,0:T(8,128)(2,1)S(1)} collective-permute-done((bf16[544,2048]{1,0:T(8,128)(2,1)S(1)}, bf16[544,2048]{1,0:T(8,128)(2,1)S(1)}, u32[]{:S(2)}, u32[]{:S(2)}) %collective-permute-start.38) | collective-permute-done | bytes 2228256 | tf_op jit(solution)/shard_map/ppermute | solution.py:291
  599.8 15.2 %collective-permute-done.37.refs_1_ = bf16[544,2048]{1,0:T(8,128)(2,1)S(1)} collective-permute-done((bf16[544,2048]{1,0:T(8,128)(2,1)S(1)}, bf16[544,2048]{1,0:T(8,128)(2,1)S(1)}, u32[]{:S(2)}, u32[]{:S(2)}) %collective-permute-start.37) | collective-permute-done | bytes 2228256 | tf_op jit(solution)/shard_map/ppermute | solution.py:291
  616.1 9.8 %collective-permute-start.40 = (bf16[272,2048]{1,0:T(8,128)(2,1)S(1)}, bf16[272,2048]{1,0:T(8,128)(2,1)S(1)}, u32[]{:S(2)}, u32[]{:S(2)}) collective-permute-start(bf16[272,2048]{1,0:T(8,128)(2,1)S(1)} %slice.285), channel_id=1, source_target_pairs={{0,24},{4,28},{8,0},{12,4},{16,8},{20,12},{24,16},{28,20},{1,25},{... | collective-permute-start | bytes 3342344 | tf_op jit(solution)/shard_map/ppermute | solution.py:291
  625.9 22.0 %collective-permute-done.40 = bf16[272,2048]{1,0:T(8,128)(2,1)S(1)} collective-permute-done((bf16[272,2048]{1,0:T(8,128)(2,1)S(1)}, bf16[272,2048]{1,0:T(8,128)(2,1)S(1)}, u32[]{:S(2)}, u32[]{:S(2)}) %collective-permute-start.40) | collective-permute-done | bytes 1114144 | tf_op jit(solution)/shard_map/ppermute | solution.py:291
  647.9 20.3 %collective-permute-done.39 = bf16[272,2048]{1,0:T(8,128)(2,1)S(1)} collective-permute-done((bf16[272,2048]{1,0:T(8,128)(2,1)S(1)}, bf16[272,2048]{1,0:T(8,128)(2,1)S(1)}, u32[]{:S(2)}, u32[]{:S(2)}) %collective-permute-start.39) | collective-permute-done | bytes 1114144 | tf_op jit(solution)/shard_map/ppermute | solution.py:291
  671.2 3.1 collective-permute-start.43
  674.6 3.6 put_heads.4
  678.1 28.1 %collective-permute-done.43.own_ref = bf16[336,2048]{1,0:T(8,128)(2,1)S(1)} collective-permute-done((bf16[336,2048]{1,0:T(8,128)(2,1)S(1)}, bf16[336,2048]{1,0:T(8,128)(2,1)S(1)}, u32[]{:S(2)}, u32[]{:S(2)}) %collective-permute-start.43) | collective-permute-done | bytes 1376288 | tf_op jit(solution)/shard_map/ppermute | solution.py:291
  706.2 5.8 collective-permute-done.42.refs_6_
  712.0 7.6 collective-permute-start.44
  722.0 3.5 fusion.27
  727.1 20.5 %mlp_finish.1 = (f32[1376,2048]{1,0:T(8,128)}, f32[1376,2048]{1,0:T(8,128)}, f32[1376,2048]{1,0:T(8,128)}) custom-call(s32[8]{0:T(128)S(1)} %pad_add_fusion.6.at_ref, bf16[544,2048]{1,0:T(8,128)(2,1)S(1)} %pad_maximum_fusion.refs_0_, bf16[544,2048]{1,0:T(8,128)(2,1)S(1)} %collective-permute-done.37.refs_1_, bf16[544,2048]{1,0:T(8,128)(2,1)} %copy-done.61, ...), custom_call_target="tpu_custom_call" | custom-call | tf_op jit(solution)/shard_map/mlp_finish/pallas_call | solution.py:434
  753.3 3.6 put_heads.5
  763.1 8.7 %fusion.62 = f32[2048,8]{0,1:T(8,128)} fusion(bf16[4096,2048]{1,0:T(8,128)(2,1)} %all-gather.2.cloned.1.call-done, bf16[4096,8]{1,0:T(8,128)(2,1)S(1)} %reshape.435), kind=kOutput, calls=%fused_computation.267 | convolution fusion | flops 134217728 | bytes 16908288 | tf_op jit(solution)/shard_map/dot_general | solution.py:359
  784.1 4.9 put_heads.6
  790.6 9.3 %collective-permute-done.49.other_ref = bf16[336,2048]{1,0:T(8,128)(2,1)S(1)} collective-permute-done((bf16[336,2048]{1,0:T(8,128)(2,1)S(1)}, bf16[336,2048]{1,0:T(8,128)(2,1)S(1)}, u32[]{:S(2)}, u32[]{:S(2)}) %collective-permute-start.49) | collective-permute-done | bytes 1376288 | tf_op jit(solution)/shard_map/ppermute | solution.py:291
  804.5 3.6 put_heads.7
  (497 shorter events, 186.7 us)
Async XLA Ops:
  8.0 107.7 %copy-start = (bf16[512,2048]{1,0:T(8,128)(2,1)S(1)}, bf16[512,2048]{1,0:T(8,128)(2,1)}, u32[]{:S(2)}) copy-start(bf16[512,2048]{1,0:T(8,128)(2,1)} %param.32) | copy-start | bytes 6291460
  8.0 365.1 %all-gather.2.cloned.1.call-start = ((), (), s32[]{:S(2)}) async-start(), calls=%async_computation.2 | async-start | bytes 17301504 | tf_op jit(solution)/shard_map/all_gather | solution.py:556
  10.7 15.0 %collective-permute-start = (bf16[128,2048]{1,0:T(8,128)(2,1)S(1)}, bf16[128,2048]{1,0:T(8,128)(2,1)S(1)}, u32[]{:S(2)}, u32[]{:S(2)}) collective-permute-start(bf16[128,2048]{1,0:T(8,128)(2,1)S(1)} %fusion.23), channel_id=1, source_target_pairs={{0,2},{1,3},{2,0},{3,1},{4,6},{5,7},{6,4},{7,5},{8,10},{9,11},{10,... | collective-permute-start | bytes 1572872 | tf_op jit(solution)/shard_map/ppermute | solution.py:319
  27.5 3.0 collective-permute-start.1
  49.8 6.7 collective-permute-start.2
  51.5 22.1 %collective-permute-start.5 = (bf16[128,2048]{1,0:T(8,128)(2,1)S(1)}, bf16[128,2048]{1,0:T(8,128)(2,1)S(1)}, u32[]{:S(2)}, u32[]{:S(2)}) collective-permute-start(bf16[128,2048]{1,0:T(8,128)(2,1)S(1)} %copy-done.56), channel_id=1, source_target_pairs={{0,2},{1,3},{2,0},{3,1},{4,6},{5,7},{6,4},{7,5},{8,10},{9,11},{10,... | collective-permute-start | bytes 1572872 | tf_op jit(solution)/shard_map/ppermute | solution.py:319
  56.5 17.9 %collective-permute-start.4 = (bf16[2,9,80,128]{3,2,1,0:T(8,128)(2,1)S(1)}, bf16[2,9,80,128]{3,2,1,0:T(8,128)(2,1)S(1)}, u32[]{:S(2)}, u32[]{:S(2)}) collective-permute-start(bf16[2,9,80,128]{3,2,1,0:T(8,128)(2,1)S(1)} %pad_maximum_fusion.12), channel_id=1, source_target_pairs={{0,24},{4,28},{8,0},{12,4},{16,8},{20,12},{24,16},{28,20},{1,25},{... | collective-permute-start | bytes 1105928 | tf_op jit(solution)/shard_map/ppermute | solution.py:291
  60.4 16.1 %collective-permute-start.3 = (bf16[2,9,80,128]{3,2,1,0:T(8,128)(2,1)S(1)}, bf16[2,9,80,128]{3,2,1,0:T(8,128)(2,1)S(1)}, u32[]{:S(2)}, u32[]{:S(2)}) collective-permute-start(bf16[2,9,80,128]{3,2,1,0:T(8,128)(2,1)S(1)} %pad_maximum_fusion.12), channel_id=1, source_target_pairs={{0,8},{4,12},{8,16},{12,20},{16,24},{20,28},{24,0},{28,4},{1,9},{5... | collective-permute-start | bytes 1105928 | tf_op jit(solution)/shard_map/ppermute | solution.py:291
  76.5 9.0 %collective-permute-start.6 = (bf16[1,9,80,128]{3,2,1,0:T(8,128)(2,1)S(1)}, bf16[1,9,80,128]{3,2,1,0:T(8,128)(2,1)S(1)}, u32[]{:S(2)}, u32[]{:S(2)}) collective-permute-start(bf16[1,9,80,128]{3,2,1,0:T(8,128)(2,1)S(1)} %slice.246), channel_id=1, source_target_pairs={{0,8},{4,12},{8,16},{12,20},{16,24},{20,28},{24,0},{28,4},{1,9},{5... | collective-permute-start | bytes 552968 | tf_op jit(solution)/shard_map/ppermute | solution.py:291
  78.9 8.4 %collective-permute-start.7 = (bf16[1,9,80,128]{3,2,1,0:T(8,128)(2,1)S(1)}, bf16[1,9,80,128]{3,2,1,0:T(8,128)(2,1)S(1)}, u32[]{:S(2)}, u32[]{:S(2)}) collective-permute-start(bf16[1,9,80,128]{3,2,1,0:T(8,128)(2,1)S(1)} %slice.247), channel_id=1, source_target_pairs={{0,24},{4,28},{8,0},{12,4},{16,8},{20,12},{24,16},{28,20},{1,25},{... | collective-permute-start | bytes 552968 | tf_op jit(solution)/shard_map/ppermute | solution.py:291
  88.7 328.7 %reduce-scatter.2.cloned.1.call-start = ((), (), s32[]{:S(2)}) async-start(), calls=%async_computation.3 | async-start | bytes 2359296 | tf_op jit(solution)/shard_map/reduce_scatter | solution.py:634
  121.1 3.0 collective-permute-start.8
  122.2 6.0 collective-permute-start.10
  126.6 14.0 %collective-permute-start.9 = (bf16[128,2048]{1,0:T(8,128)(2,1)S(1)}, bf16[128,2048]{1,0:T(8,128)(2,1)S(1)}, u32[]{:S(2)}, u32[]{:S(2)}) collective-permute-start(bf16[128,2048]{1,0:T(8,128)(2,1)S(1)} %select_bitcast_fusion.19), channel_id=1, source_target_pairs={{0,2},{1,3},{2,0},{3,1},{4,6},{5,7},{6,4},{7,5},{8,10},{9,11},{10,... | collective-permute-start | bytes 1572872 | tf_op jit(solution)/shard_map/ppermute | solution.py:319
  141.3 17.1 %collective-permute-start.11 = (bf16[128,2048]{1,0:T(8,128)(2,1)S(1)}, bf16[128,2048]{1,0:T(8,128)(2,1)S(1)}, u32[]{:S(2)}, u32[]{:S(2)}) collective-permute-start(bf16[128,2048]{1,0:T(8,128)(2,1)S(1)} %multiply_convert_fusion.2), channel_id=1, source_target_pairs={{0,2},{1,3},{2,0},{3,1},{4,6},{5,7},{6,4},{7,5},{8,10},{9,11},{10,... | collective-permute-start | bytes 1572872 | tf_op jit(solution)/shard_map/ppermute | solution.py:319
  158.4 4.8 collective-permute-start.12
  180.7 49.8 %collective-permute-start.15 = (bf16[528,2048]{1,0:T(8,128)(2,1)}, bf16[528,2048]{1,0:T(8,128)(2,1)}, u32[]{:S(2)}, u32[]{:S(2)}) collective-permute-start(bf16[528,2048]{1,0:T(8,128)(2,1)} %get-tuple-element.183), channel_id=1, source_target_pairs={{0,4},{4,0},{8,12},{12,8},{16,20},{20,16},{24,28},{28,24},{1,5},{5... | collective-permute-start | bytes 6488072 | tf_op jit(solution)/shard_map/ppermute | solution.py:291
  192.6 15.1 %collective-permute-start.13 = (bf16[2,128,2048]{2,1,0:T(8,128)(2,1)}, bf16[2,128,2048]{2,1,0:T(8,128)(2,1)}, u32[]{:S(2)}, u32[]{:S(2)}) collective-permute-start(bf16[2,128,2048]{2,1,0:T(8,128)(2,1)} %select_bitcast_fusion.2), channel_id=1, source_target_pairs={{0,1},{1,0},{2,3},{3,2},{4,5},{5,4},{6,7},{7,6},{8,9},{9,8},{10,11... | collective-permute-start | bytes 3145736 | tf_op jit(solution)/shard_map/ppermute | solution.py:319
  197.9 14.2 %collective-permute-start.21 = (bf16[2,128,2048]{2,1,0:T(8,128)(2,1)}, bf16[2,128,2048]{2,1,0:T(8,128)(2,1)}, u32[]{:S(2)}, u32[]{:S(2)}) collective-permute-start(bf16[2,128,2048]{2,1,0:T(8,128)(2,1)} %select_bitcast_fusion.1), channel_id=1, source_target_pairs={{0,1},{1,0},{2,3},{3,2},{4,5},{5,4},{6,7},{7,6},{8,9},{9,8},{10,11... | collective-permute-start | bytes 3145736 | tf_op jit(solution)/shard_map/ppermute | solution.py:319
  209.8 15.0 %collective-permute-start.14 = (bf16[128,2048]{1,0:T(8,128)(2,1)S(1)}, bf16[128,2048]{1,0:T(8,128)(2,1)S(1)}, u32[]{:S(2)}, u32[]{:S(2)}) collective-permute-start(bf16[128,2048]{1,0:T(8,128)(2,1)S(1)} %select_bitcast_fusion.10), channel_id=1, source_target_pairs={{0,2},{1,3},{2,0},{3,1},{4,6},{5,7},{6,4},{7,5},{8,10},{9,11},{10,... | collective-permute-start | bytes 1572872 | tf_op jit(solution)/shard_map/ppermute | solution.py:319
  213.9 41.8 %collective-permute-start.22 = (bf16[128,2048]{1,0:T(8,128)(2,1)S(1)}, bf16[128,2048]{1,0:T(8,128)(2,1)}, u32[]{:S(2)}, u32[]{:S(2)}) collective-permute-start(bf16[128,2048]{1,0:T(8,128)(2,1)S(1)} %select_bitcast_fusion.5), channel_id=1, source_target_pairs={{0,2},{1,3},{2,0},{3,1},{4,6},{5,7},{6,4},{7,5},{8,10},{9,11},{10,... | collective-permute-start | bytes 1572872 | tf_op jit(solution)/shard_map/ppermute | solution.py:319
  230.5 53.9 %collective-permute-start.17 = (bf16[528,2048]{1,0:T(8,128)(2,1)}, bf16[528,2048]{1,0:T(8,128)(2,1)}, u32[]{:S(2)}, u32[]{:S(2)}) collective-permute-start(bf16[528,2048]{1,0:T(8,128)(2,1)} %get-tuple-element.187), channel_id=1, source_target_pairs={{0,4},{4,0},{8,12},{12,8},{16,20},{20,16},{24,28},{28,24},{1,5},{5... | collective-permute-start | bytes 6488072 | tf_op jit(solution)/shard_map/ppermute | solution.py:291
  235.5 28.3 %collective-permute-start.18 = (bf16[256,2048]{1,0:T(8,128)(2,1)}, bf16[256,2048]{1,0:T(8,128)(2,1)}, u32[]{:S(2)}, u32[]{:S(2)}) collective-permute-start(bf16[256,2048]{1,0:T(8,128)(2,1)} %slice.336), channel_id=1, source_target_pairs={{0,8},{4,12},{8,16},{12,20},{16,24},{20,28},{24,0},{28,4},{1,9},{5... | collective-permute-start | bytes 3145736 | tf_op jit(solution)/shard_map/ppermute | solution.py:291
  236.3 48.1 %collective-permute-start.19 = (bf16[272,2048]{1,0:T(8,128)(2,1)S(1)}, bf16[272,2048]{1,0:T(8,128)(2,1)S(1)}, u32[]{:S(2)}, u32[]{:S(2)}) collective-permute-start(bf16[272,2048]{1,0:T(8,128)(2,1)S(1)} %slice.337), channel_id=1, source_target_pairs={{0,24},{4,28},{8,0},{12,4},{16,8},{20,12},{24,16},{28,20},{1,25},{... | collective-permute-start | bytes 3342344 | tf_op jit(solution)/shard_map/ppermute | solution.py:291
  240.3 17.7 %collective-permute-start.16 = (bf16[128,2048]{1,0:T(8,128)(2,1)S(1)}, bf16[128,2048]{1,0:T(8,128)(2,1)S(1)}, u32[]{:S(2)}, u32[]{:S(2)}) collective-permute-start(bf16[128,2048]{1,0:T(8,128)(2,1)S(1)} %fusion.49), channel_id=1, source_target_pairs={{0,2},{1,3},{2,0},{3,1},{4,6},{5,7},{6,4},{7,5},{8,10},{9,11},{10,... | collective-permute-start | bytes 1572872 | tf_op jit(solution)/shard_map/ppermute | solution.py:319
  284.5 7.8 collective-permute-start.20
  290.5 82.7 %collective-permute-start.28 = (bf16[528,2048]{1,0:T(8,128)(2,1)}, bf16[528,2048]{1,0:T(8,128)(2,1)}, u32[]{:S(2)}, u32[]{:S(2)}) collective-permute-start(bf16[528,2048]{1,0:T(8,128)(2,1)} %get-tuple-element.212), channel_id=1, source_target_pairs={{0,4},{4,0},{8,12},{12,8},{16,20},{20,16},{24,28},{28,24},{1,5},{5... | collective-permute-start | bytes 6488072 | tf_op jit(solution)/shard_map/ppermute | solution.py:291
  291.0 82.2 %collective-permute-start.29 = (bf16[528,2048]{1,0:T(8,128)(2,1)}, bf16[528,2048]{1,0:T(8,128)(2,1)}, u32[]{:S(2)}, u32[]{:S(2)}) collective-permute-start(bf16[528,2048]{1,0:T(8,128)(2,1)} %pad_maximum_fusion.1), channel_id=1, source_target_pairs={{0,8},{4,12},{8,16},{12,20},{16,24},{20,28},{24,0},{28,4},{1,9},{5... | collective-permute-start | bytes 6488072 | tf_op jit(solution)/shard_map/ppermute | solution.py:291
  316.4 28.2 %collective-permute-start.23 = (bf16[4,80,128]{2,1,0:T(8,128)(2,1)S(1)}, bf16[4,80,128]{2,1,0:T(8,128)(2,1)}, u32[]{:S(2)}, u32[]{:S(2)}) collective-permute-start(bf16[4,80,128]{2,1,0:T(8,128)(2,1)S(1)} %get-tuple-element.194), channel_id=1, source_target_pairs={{0,4},{4,0},{8,12},{12,8},{16,20},{20,16},{24,28},{28,24},{1,5},{5... | collective-permute-start | bytes 245768 | tf_op jit(solution)/shard_map/ppermute | solution.py:291
  345.5 17.4 %collective-permute-start.25 = (bf16[2,4,80,128]{3,2,1,0:T(8,128)(2,1)S(1)}, bf16[2,4,80,128]{3,2,1,0:T(8,128)(2,1)S(1)}, u32[]{:S(2)}, u32[]{:S(2)}) collective-permute-start(bf16[2,4,80,128]{3,2,1,0:T(8,128)(2,1)S(1)} %pad_maximum_fusion.13), channel_id=1, source_target_pairs={{0,24},{4,28},{8,0},{12,4},{16,8},{20,12},{24,16},{28,20},{1,25},{... | collective-permute-start | bytes 491528 | tf_op jit(solution)/shard_map/ppermute | solution.py:291
  347.8 18.1 %collective-permute-start.24 = (bf16[2,4,80,128]{3,2,1,0:T(8,128)(2,1)S(1)}, bf16[2,4,80,128]{3,2,1,0:T(8,128)(2,1)S(1)}, u32[]{:S(2)}, u32[]{:S(2)}) collective-permute-start(bf16[2,4,80,128]{3,2,1,0:T(8,128)(2,1)S(1)} %pad_maximum_fusion.13), channel_id=1, source_target_pairs={{0,8},{4,12},{8,16},{12,20},{16,24},{20,28},{24,0},{28,4},{1,9},{5... | collective-permute-start | bytes 491528 | tf_op jit(solution)/shard_map/ppermute | solution.py:291
  347.8 75.3 %collective-permute-start.33 = (bf16[528,2048]{1,0:T(8,128)(2,1)}, bf16[528,2048]{1,0:T(8,128)(2,1)}, u32[]{:S(2)}, u32[]{:S(2)}) collective-permute-start(bf16[528,2048]{1,0:T(8,128)(2,1)} %get-tuple-element.231), channel_id=1, source_target_pairs={{0,4},{4,0},{8,12},{12,8},{16,20},{20,16},{24,28},{28,24},{1,5},{5... | collective-permute-start | bytes 6488072 | tf_op jit(solution)/shard_map/ppermute | solution.py:291
  365.9 6.3 collective-permute-start.26
  366.0 6.2 collective-permute-start.27
  379.6 60.1 %collective-permute-start.32 = (bf16[528,2048]{1,0:T(8,128)(2,1)}, bf16[528,2048]{1,0:T(8,128)(2,1)}, u32[]{:S(2)}, u32[]{:S(2)}) collective-permute-start(bf16[528,2048]{1,0:T(8,128)(2,1)} %pad_maximum_fusion.2), channel_id=1, source_target_pairs={{0,24},{4,28},{8,0},{12,4},{16,8},{20,12},{24,16},{28,20},{1,25},{... | collective-permute-start | bytes 6488072 | tf_op jit(solution)/shard_map/ppermute | solution.py:291
  417.2 5.3 collective-permute-start.30
  417.8 61.5 %all-to-all-start = ((bf16[8,512,256]{2,1,0:T(8,128)(2,1)}), bf16[8,512,256]{2,1,0:T(8,128)(2,1)}, u32[]{:S(2)}, u32[]{:S(2)}) async-start(bf16[8,512,256]{2,1,0:T(8,128)(2,1)} %get-tuple-element.225), calls=%async_computation.1 | async-start | bytes 4194304 | tf_op jit(solution)/shard_map/all_to_all | solution.py:666
  444.7 56.9 %collective-permute-start.34 = (bf16[544,2048]{1,0:T(8,128)(2,1)S(1)}, bf16[544,2048]{1,0:T(8,128)(2,1)}, u32[]{:S(2)}, u32[]{:S(2)}) collective-permute-start(bf16[544,2048]{1,0:T(8,128)(2,1)S(1)} %pad_maximum_fusion.refs_0_), channel_id=1, source_target_pairs={{0,4},{4,0},{8,12},{12,8},{16,20},{20,16},{24,28},{28,24},{1,5},{5... | collective-permute-start | bytes 6684680 | tf_op jit(solution)/shard_map/ppermute | solution.py:291
  447.8 9.2 %collective-permute-start.31 = (bf16[128,2048]{1,0:T(8,128)(2,1)S(1)}, bf16[128,2048]{1,0:T(8,128)(2,1)S(1)}, u32[]{:S(2)}, u32[]{:S(2)}) collective-permute-start(bf16[128,2048]{1,0:T(8,128)(2,1)S(1)} %select_bitcast_fusion.4), channel_id=1, source_target_pairs={{0,2},{1,3},{2,0},{3,1},{4,6},{5,7},{6,4},{7,5},{8,10},{9,11},{10,... | collective-permute-start | bytes 1572872 | tf_op jit(solution)/shard_map/ppermute | solution.py:319
  501.6 49.0 %collective-permute-start.35 = (bf16[544,2048]{1,0:T(8,128)(2,1)S(1)}, bf16[544,2048]{1,0:T(8,128)(2,1)S(1)}, u32[]{:S(2)}, u32[]{:S(2)}) collective-permute-start(bf16[544,2048]{1,0:T(8,128)(2,1)S(1)} %pad_maximum_fusion.refs_0_), channel_id=1, source_target_pairs={{0,8},{4,12},{8,16},{12,20},{16,24},{20,28},{24,0},{28,4},{1,9},{5... | collective-permute-start | bytes 6684680 | tf_op jit(solution)/shard_map/ppermute | solution.py:291
  513.1 27.5 %collective-permute-start.36 = (bf16[336,2048]{1,0:T(8,128)(2,1)S(1)}, bf16[336,2048]{1,0:T(8,128)(2,1)S(1)}, u32[]{:S(2)}, u32[]{:S(2)}) collective-permute-start(bf16[336,2048]{1,0:T(8,128)(2,1)S(1)} %pad_maximum_fusion.7.own_ref), channel_id=1, source_target_pairs={{0,4},{4,0},{8,12},{12,8},{16,20},{20,16},{24,28},{28,24},{1,5},{5... | collective-permute-start | bytes 4128776 | tf_op jit(solution)/shard_map/ppermute | solution.py:291
  540.6 134.0 %copy-start.26 = (bf16[336,2048]{1,0:T(8,128)(2,1)}, bf16[336,2048]{1,0:T(8,128)(2,1)S(1)}, u32[]{:S(2)}) copy-start(bf16[336,2048]{1,0:T(8,128)(2,1)S(1)} %collective-permute-done.36.other_ref) | copy-start | bytes 4128772
  550.5 175.8 %copy-start.60 = (bf16[544,2048]{1,0:T(8,128)(2,1)}, bf16[544,2048]{1,0:T(8,128)(2,1)S(1)}, u32[]{:S(2)}) copy-start(bf16[544,2048]{1,0:T(8,128)(2,1)S(1)} %collective-permute-done.35.refs_3_) | copy-start | bytes 6684676
  550.5 49.2 %collective-permute-start.38 = (bf16[544,2048]{1,0:T(8,128)(2,1)S(1)}, bf16[544,2048]{1,0:T(8,128)(2,1)S(1)}, u32[]{:S(2)}, u32[]{:S(2)}) collective-permute-start(bf16[544,2048]{1,0:T(8,128)(2,1)S(1)} %collective-permute-done.35.refs_3_), channel_id=1, source_target_pairs={{0,4},{4,0},{8,12},{12,8},{16,20},{20,16},{24,28},{28,24},{1,5},{5... | collective-permute-start | bytes 6684680 | tf_op jit(solution)/shard_map/ppermute | solution.py:291
  553.2 61.7 %collective-permute-start.37 = (bf16[544,2048]{1,0:T(8,128)(2,1)S(1)}, bf16[544,2048]{1,0:T(8,128)(2,1)S(1)}, u32[]{:S(2)}, u32[]{:S(2)}) collective-permute-start(bf16[544,2048]{1,0:T(8,128)(2,1)S(1)} %pad_maximum_fusion.refs_0_), channel_id=1, source_target_pairs={{0,24},{4,28},{8,0},{12,4},{16,8},{20,12},{24,16},{28,20},{1,25},{... | collective-permute-start | bytes 6684680 | tf_op jit(solution)/shard_map/ppermute | solution.py:291
  599.8 68.4 %copy-start.65 = (bf16[544,2048]{1,0:T(8,128)(2,1)}, bf16[544,2048]{1,0:T(8,128)(2,1)S(1)}, u32[]{:S(2)}) copy-start(bf16[544,2048]{1,0:T(8,128)(2,1)S(1)} %collective-permute-done.38.refs_7_) | copy-start | bytes 6684676
  614.9 53.2 %collective-permute-start.41 = (bf16[544,2048]{1,0:T(8,128)(2,1)S(1)}, bf16[544,2048]{1,0:T(8,128)(2,1)S(1)}, u32[]{:S(2)}, u32[]{:S(2)}) collective-permute-start(bf16[544,2048]{1,0:T(8,128)(2,1)S(1)} %collective-permute-done.37.refs_1_), channel_id=1, source_target_pairs={{0,4},{4,0},{8,12},{12,8},{16,20},{20,16},{24,28},{28,24},{1,5},{5... | collective-permute-start | bytes 6684680 | tf_op jit(solution)/shard_map/ppermute | solution.py:291
  616.1 31.8 %collective-permute-start.40 = (bf16[272,2048]{1,0:T(8,128)(2,1)S(1)}, bf16[272,2048]{1,0:T(8,128)(2,1)S(1)}, u32[]{:S(2)}, u32[]{:S(2)}) collective-permute-start(bf16[272,2048]{1,0:T(8,128)(2,1)S(1)} %slice.285), channel_id=1, source_target_pairs={{0,24},{4,28},{8,0},{12,4},{16,8},{20,12},{24,16},{28,20},{1,25},{... | collective-permute-start | bytes 3342344 | tf_op jit(solution)/shard_map/ppermute | solution.py:291
  625.9 42.2 %collective-permute-start.39 = (bf16[272,2048]{1,0:T(8,128)(2,1)S(1)}, bf16[272,2048]{1,0:T(8,128)(2,1)S(1)}, u32[]{:S(2)}, u32[]{:S(2)}) collective-permute-start(bf16[272,2048]{1,0:T(8,128)(2,1)S(1)} %slice.284), channel_id=1, source_target_pairs={{0,8},{4,12},{8,16},{12,20},{16,24},{20,28},{24,0},{28,4},{1,9},{5... | collective-permute-start | bytes 3342344 | tf_op jit(solution)/shard_map/ppermute | solution.py:291
  669.5 51.1 %copy-start.41 = (f32[8,72,128]{2,1,0:T(8,128)S(1)}, f32[8,72,128]{2,1,0:T(8,128)}, u32[]{:S(2)}) copy-start(f32[8,72,128]{2,1,0:T(8,128)} %copy-done.40) | copy-start | bytes 884740
  669.6 55.9 %copy-start.61 = (bf16[544,2048]{1,0:T(8,128)(2,1)}, bf16[544,2048]{1,0:T(8,128)(2,1)S(1)}, u32[]{:S(2)}) copy-start(bf16[544,2048]{1,0:T(8,128)(2,1)S(1)} %constant_dynamic-update-slice_fusion.12.refs_2_) | copy-start | bytes 6684676
  669.6 52.4 %copy-start.45 = (f32[128,2048]{1,0:T(8,128)S(1)}, f32[128,2048]{1,0:T(8,128)}, u32[]{:S(2)}) copy-start(f32[128,2048]{1,0:T(8,128)} %copy-done.43) | copy-start | bytes 3145732
  669.6 52.4 %copy-start.49 = (bf16[128,2048]{1,0:T(8,128)(2,1)S(1)}, bf16[128,2048]{1,0:T(8,128)(2,1)}, u32[]{:S(2)}) copy-start(bf16[128,2048]{1,0:T(8,128)(2,1)} %param.19) | copy-start | bytes 1572868
  669.6 52.4 %copy-start.59 = (bf16[128,2048]{1,0:T(8,128)(2,1)S(1)}, bf16[128,2048]{1,0:T(8,128)(2,1)}, u32[]{:S(2)}) copy-start(bf16[128,2048]{1,0:T(8,128)(2,1)} %param.37) | copy-start | bytes 1572868
  669.6 52.3 %copy-start.63 = (bf16[128,2048]{1,0:T(8,128)(2,1)S(1)}, bf16[128,2048]{1,0:T(8,128)(2,1)}, u32[]{:S(2)}) copy-start(bf16[128,2048]{1,0:T(8,128)(2,1)} %copy-done.62) | copy-start | bytes 1572868
  669.6 42.4 %collective-permute-start.42 = (bf16[544,2048]{1,0:T(8,128)(2,1)S(1)}, bf16[544,2048]{1,0:T(8,128)(2,1)}, u32[]{:S(2)}, u32[]{:S(2)}) collective-permute-start(bf16[544,2048]{1,0:T(8,128)(2,1)S(1)} %constant_dynamic-update-slice_fusion.12.refs_2_), channel_id=1, source_target_pairs={{0,4},{4,0},{8,12},{12,8},{16,20},{20,16},{24,28},{28,24},{1,5},{5... | collective-permute-start | bytes 6684680 | tf_op jit(solution)/shard_map/ppermute | solution.py:291
  671.2 35.1 %collective-permute-start.43 = (bf16[336,2048]{1,0:T(8,128)(2,1)S(1)}, bf16[336,2048]{1,0:T(8,128)(2,1)S(1)}, u32[]{:S(2)}, u32[]{:S(2)}) collective-permute-start(bf16[336,2048]{1,0:T(8,128)(2,1)S(1)} %pad_maximum_fusion.7.own_ref), channel_id=1, source_target_pairs={{0,8},{4,12},{8,16},{12,20},{16,24},{20,28},{24,0},{28,4},{1,9},{5... | collective-permute-start | bytes 4128776 | tf_op jit(solution)/shard_map/ppermute | solution.py:291
  706.2 47.0 %copy-start.22 = (bf16[336,2048]{1,0:T(8,128)(2,1)}, bf16[336,2048]{1,0:T(8,128)(2,1)S(1)}, u32[]{:S(2)}) copy-start(bf16[336,2048]{1,0:T(8,128)(2,1)S(1)} %collective-permute-done.43.own_ref) | copy-start | bytes 4128772
  712.0 36.8 %collective-permute-start.44 = (bf16[336,2048]{1,0:T(8,128)(2,1)S(1)}, bf16[336,2048]{1,0:T(8,128)(2,1)}, u32[]{:S(2)}, u32[]{:S(2)}) collective-permute-start(bf16[336,2048]{1,0:T(8,128)(2,1)S(1)} %pad_maximum_fusion.7.own_ref), channel_id=1, source_target_pairs={{0,24},{4,28},{8,0},{12,4},{16,8},{20,12},{24,16},{28,20},{1,25},{... | collective-permute-start | bytes 4128776 | tf_op jit(solution)/shard_map/ppermute | solution.py:291
  719.6 29.2 %collective-permute-start.45 = (bf16[336,2048]{1,0:T(8,128)(2,1)S(1)}, bf16[336,2048]{1,0:T(8,128)(2,1)S(1)}, u32[]{:S(2)}, u32[]{:S(2)}) collective-permute-start(bf16[336,2048]{1,0:T(8,128)(2,1)S(1)} %collective-permute-done.43.own_ref), channel_id=1, source_target_pairs={{0,4},{4,0},{8,12},{12,8},{16,20},{20,16},{24,28},{28,24},{1,5},{5... | collective-permute-start | bytes 4128776 | tf_op jit(solution)/shard_map/ppermute | solution.py:291
  751.4 27.9 %collective-permute-start.48 = (bf16[336,2048]{1,0:T(8,128)(2,1)}, bf16[336,2048]{1,0:T(8,128)(2,1)S(1)}, u32[]{:S(2)}, u32[]{:S(2)}) collective-permute-start(bf16[336,2048]{1,0:T(8,128)(2,1)} %collective-permute-done.44.own_ref), channel_id=1, source_target_pairs={{0,4},{4,0},{8,12},{12,8},{16,20},{20,16},{24,28},{28,24},{1,5},{5... | collective-permute-start | bytes 4128776 | tf_op jit(solution)/shard_map/ppermute | solution.py:291
  757.8 18.3 %collective-permute-start.46 = (bf16[160,2048]{1,0:T(8,128)(2,1)}, bf16[160,2048]{1,0:T(8,128)(2,1)}, u32[]{:S(2)}, u32[]{:S(2)}) collective-permute-start(bf16[160,2048]{1,0:T(8,128)(2,1)} %slice.288), channel_id=1, source_target_pairs={{0,8},{4,12},{8,16},{12,20},{16,24},{20,28},{24,0},{28,4},{1,9},{5... | collective-permute-start | bytes 1966088 | tf_op jit(solution)/shard_map/ppermute | solution.py:291
  759.9 18.3 %collective-permute-start.47 = (bf16[176,2048]{1,0:T(8,128)(2,1)}, bf16[176,2048]{1,0:T(8,128)(2,1)S(1)}, u32[]{:S(2)}, u32[]{:S(2)}) collective-permute-start(bf16[176,2048]{1,0:T(8,128)(2,1)} %slice.289), channel_id=1, source_target_pairs={{0,24},{4,28},{8,0},{12,4},{16,8},{20,12},{24,16},{28,20},{1,25},{... | collective-permute-start | bytes 2162696 | tf_op jit(solution)/shard_map/ppermute | solution.py:291
  781.5 18.4 %collective-permute-start.49 = (bf16[336,2048]{1,0:T(8,128)(2,1)S(1)}, bf16[336,2048]{1,0:T(8,128)(2,1)S(1)}, u32[]{:S(2)}, u32[]{:S(2)}) collective-permute-start(bf16[336,2048]{1,0:T(8,128)(2,1)S(1)} %constant_dynamic-update-slice_fusion.14.own_ref), channel_id=1, source_target_pairs={{0,4},{4,0},{8,12},{12,8},{16,20},{20,16},{24,28},{28,24},{1,5},{5... | collective-permute-start | bytes 4128776 | tf_op jit(solution)/shard_map/ppermute | solution.py:291
  (107 other events, 892.6 us)
Sparse Core Ops, SparseCore 0:
  88.9 116.3 all-gather.1
Sparse Core Ops, SparseCore 1:
  321.4 86.9 reduce-scatter.1
